TPU v7x, 32 devices: a whole 2x2x4 slice. The times are simulated.
32 devices in a mesh: seq: 4 (over z), kv: 8 (over y, x, core).
Axes of the slice: x: 2, y: 2, z: 4, core: 2. Of those that a mesh axis runs over, the one named last changes fastest.
Arguments:
- tokens: bfloat16 [4, 1536, 2048], P('seq', 'kv'), may hold values from -6 to 6
- doc_ids: int32 [4, 1536], P('seq', 'kv'), may hold values from 0 to 3, as said below
- w_query: bfloat16 [2048, 2048], P(('seq', 'kv')), may hold values from -0.25 to 0.25
- w_key: bfloat16 [2048, 2048], P(('seq', 'kv')), may hold values from -0.125 to 0.125
- w_value: bfloat16 [2048, 2048], P(('seq', 'kv')), may hold values from -0.125 to 0.125
- w_out: bfloat16 [2048, 2048], P(('seq', 'kv')), may hold values from -0.5 to 0.5
- gain_attn: bfloat16 [2048], P(('seq', 'kv')), may hold values from 0.5 to 1.5
- gain_ffn: bfloat16 [2048], P(('seq', 'kv')), may hold values from 0.5 to 1.5
- w_gate: bfloat16 [2048, 8192], P('seq', 'kv'), may hold values from -0.125 to 0.125
- w_up: bfloat16 [2048, 8192], P('seq', 'kv'), may hold values from -0.125 to 0.125
- w_down: bfloat16 [8192, 2048], P('kv', 'seq'), may hold values from -0.0625 to 0.0625
- cotangent: bfloat16 [4, 1536, 2048], P('seq', 'kv'), may hold values from -6 to 6
Outputs:
- result: bfloat16 [4, 1536, 2048], P('seq', 'kv')
- grad_tokens: float32 [4, 1536, 2048], P('seq', 'kv')
- grad_query: float32 [2048, 2048], P(('seq', 'kv'))
- grad_key: float32 [2048, 2048], P(('seq', 'kv'))
- grad_value: float32 [2048, 2048], P(('seq', 'kv'))
- grad_out: float32 [2048, 2048], P(('seq', 'kv'))
- grad_gain_attn: float32 [2048], P(('seq', 'kv'))
- grad_gain_ffn: float32 [2048], P(('seq', 'kv'))
- grad_gate: float32 [2048, 8192], P('seq', 'kv')
- grad_up: float32 [2048, 8192], P('seq', 'kv')
- grad_down: float32 [8192, 2048], P('kv', 'seq')
- mass_stats: float32 [1], replicated
Inputs may be any that keep to these rules, and one draw needn't show every extreme that they name: `doc_ids`: ordered by position pos, the ids of a sequence never fall; each id covers 1 to 768 consecutive positions, and some document has exactly that many.
All inputs are finite; a program needn't handle non-finite values.
Results may differ from a plain program's by a relative error of at most 0.018.
Values may be sent and summed in bfloat16 or wider, within the bound.
No kernel may reach another device: no remote copies, remote signals or barrier semaphores. Data moves between devices by JAX's collectives and lax.ppermute only.
A program may use at most 256 MiB of HBM per device.

v0:
```python
import math

import jax
import jax.numpy as jnp
from jax import lax
from jax.sharding import PartitionSpec as P

HEAD_DIM = 128


EPSILON = 1e-05


def dot_plain(left, right):
    return jnp.dot(left, right, preferred_element_type=jnp.float32)


def dot_left(left, right):
    return lax.dot_general(
        left, right, (((0,), (0,)), ((), ())), preferred_element_type=jnp.float32
    )


def dot_right(left, right):
    return lax.dot_general(
        left, right, (((1,), (1,)), ((), ())), preferred_element_type=jnp.float32
    )


def rms_norm(values, gain):
    return values * lax.rsqrt(jnp.mean(values * values, axis=-1, keepdims=True) + EPSILON) * gain


def rms_back(values, gain, grad):
    inverse = lax.rsqrt(jnp.mean(values * values, axis=-1, keepdims=True) + EPSILON)
    scaled = grad * gain
    moment = jnp.mean(values * scaled, axis=-1, keepdims=True)
    return (
        inverse * scaled - values * (inverse * inverse * inverse) * moment,
        jnp.sum(grad * values * inverse, axis=0),
    )


def stored_positions(rows_index, local, group):
    half = local // 2
    device = rows_index // local
    within = rows_index % local
    return jnp.where(
        within < half, device * half + within, (2 * group - 1 - device) * half + within - half
    )


def rope_tables(positions, head):
    half = head // 2
    freqs = jnp.exp(jnp.arange(half, dtype=jnp.float32) * (-2.0 * math.log(10000.0) / head))
    angles = positions.astype(jnp.float32)[:, None] * freqs[None, :]
    return (jnp.cos(angles)[:, None, :], jnp.sin(angles)[:, None, :])


def rotate(values, cosine, sine):
    half = values.shape[-1] // 2
    first = values[..., :half]
    second = values[..., half:]
    return jnp.concatenate(
        [first * cosine - second * sine, second * cosine + first * sine], axis=-1
    )


def spread(values):
    return lax.all_gather(values, "kv", axis=0, tiled=True)


def collect(values):
    return lax.psum_scatter(values, "kv", scatter_dimension=0, tiled=True)


def per_device(
    tokens,
    doc_ids,
    w_query,
    w_key,
    w_value,
    w_out,
    gain_attn,
    gain_ffn,
    w_gate,
    w_up,
    w_down,
    cotangent,
):
    gathered = (
        lax.all_gather(w_query, ("seq", "kv"), axis=0, tiled=True),
        lax.all_gather(w_key, ("seq", "kv"), axis=0, tiled=True),
        lax.all_gather(w_value, ("seq", "kv"), axis=0, tiled=True),
        lax.all_gather(w_out, ("seq", "kv"), axis=0, tiled=True),
        lax.all_gather(gain_attn, ("seq", "kv"), axis=0, tiled=True),
        lax.all_gather(gain_ffn, ("seq", "kv"), axis=0, tiled=True),
    )
    full_query, full_key, full_value, full_out = (
        gathered[0],
        gathered[1],
        gathered[2],
        gathered[3],
    )
    first_gain = gathered[4].astype(jnp.float32)
    second_gain = gathered[5].astype(jnp.float32)
    seqs, local, width = tokens.shape
    heads = width // HEAD_DIM
    group = lax.axis_size("kv")
    length = local * group
    rows = seqs * local
    block = min(512, length)
    count = length // block
    scale = 1.0 / math.sqrt(HEAD_DIM)
    offset = math.log(length)
    flat = tokens.reshape(rows, width).astype(jnp.float32)
    normed = rms_norm(flat, first_gain).astype(jnp.bfloat16)
    key_pos = stored_positions(
        lax.axis_index("kv") * local + jnp.arange(local, dtype=jnp.int32), local, group
    )
    cosine, sine = rope_tables(key_pos, HEAD_DIM)
    shape = (seqs, local, heads, HEAD_DIM)
    queries = rotate(dot_plain(normed, full_query).reshape(shape), cosine, sine).astype(
        jnp.bfloat16
    )
    keys = rotate(dot_plain(normed, full_key).reshape(shape), cosine, sine).astype(jnp.bfloat16)
    values = dot_plain(normed, full_value).astype(jnp.bfloat16).reshape(shape)
    full_pos = stored_positions(jnp.arange(length, dtype=jnp.int32), local, group)
    query_pos = full_pos.reshape(count, block)

    def attention_weights(q_heads, id_block, pos_block, key_block, key_docs, key_positions):
        scores = (
            jnp.einsum("qhd,khd->hqk", q_heads, key_block, preferred_element_type=jnp.float32)
            * scale
            - offset
        )
        allowed = (id_block.astype(jnp.float32)[:, None] == key_docs[None, :]) & (
            pos_block[:, None] >= key_positions[None, :]
        )
        return jnp.where(allowed[None], jax.nn.sigmoid(scores), 0.0)

    def forward_blocks(q_seq, id_seq, k_heads, v_heads, key_docs, key_positions, nheads):

        def forward_one_block(parts):
            q_block, id_block, pos_block = parts
            weights_now = attention_weights(
                q_block.reshape(block, nheads, HEAD_DIM),
                id_block,
                pos_block,
                k_heads,
                key_docs,
                key_positions,
            )
            out = jnp.einsum(
                "hqk,khd->qhd",
                weights_now.astype(jnp.bfloat16),
                v_heads,
                preferred_element_type=jnp.float32,
            )
            return (out.reshape(block, nheads * HEAD_DIM), jnp.sum(weights_now, axis=2).T)

        outs, mass_part = lax.map(
            forward_one_block,
            (
                q_seq.reshape(count, block, nheads * HEAD_DIM),
                id_seq.reshape(count, block),
                query_pos,
            ),
        )
        return (outs.reshape(length, nheads * HEAD_DIM), mass_part.reshape(length, nheads))

    def backward_blocks(q_seq, id_seq, g_seq, k_heads, v_heads, key_docs, key_positions, nheads):

        def backward_one_block(carry, parts):
            key_total, value_total = carry
            q_block, id_block, pos_block, g_block = parts
            q_heads = q_block.reshape(block, nheads, HEAD_DIM)
            g_heads = g_block.reshape(block, nheads, HEAD_DIM)
            weights_now = attention_weights(
                q_heads, id_block, pos_block, k_heads, key_docs, key_positions
            )
            value_total = value_total + jnp.einsum(
                "hqk,qhd->khd",
                weights_now.astype(jnp.bfloat16),
                g_heads,
                preferred_element_type=jnp.float32,
            )
            grad_weights = jnp.einsum(
                "qhd,khd->hqk", g_heads, v_heads, preferred_element_type=jnp.float32
            )
            grad_scores = (grad_weights * weights_now * (1.0 - weights_now)).astype(jnp.bfloat16)
            grad_q = (
                jnp.einsum("hqk,khd->qhd", grad_scores, k_heads, preferred_element_type=jnp.float32)
                * scale
            )
            key_total = (
                key_total
                + jnp.einsum(
                    "hqk,qhd->khd", grad_scores, q_heads, preferred_element_type=jnp.float32
                )
                * scale
            )
            return ((key_total, value_total), grad_q.reshape(block, nheads * HEAD_DIM))

        zeros = jnp.zeros((k_heads.shape[0], nheads, HEAD_DIM), jnp.float32)
        (key_total, value_total), grad_q = lax.scan(
            backward_one_block,
            (zeros, zeros),
            (
                q_seq.reshape(count, block, nheads * HEAD_DIM),
                id_seq.reshape(count, block),
                query_pos,
                g_seq.reshape(count, block, nheads * HEAD_DIM),
            ),
        )
        return (grad_q.reshape(length, nheads * HEAD_DIM), key_total, value_total)

    all_queries, all_ids = (
        lax.all_gather(queries.reshape(seqs, local, width), "kv", axis=1, tiled=True),
        lax.all_gather(doc_ids.astype(jnp.bfloat16), "kv", axis=1, tiled=True),
    )
    key_ids = doc_ids.astype(jnp.float32)

    def key_forward(pieces):
        q_seq, id_seq, k_seq, v_seq, kid_seq = pieces
        out, mass_part = forward_blocks(q_seq, id_seq, k_seq, v_seq, kid_seq, key_pos, heads)
        return (out, jnp.sum(mass_part, axis=1))

    partial_out, partial_mass = lax.map(key_forward, (all_queries, all_ids, keys, values, key_ids))
    mixed, mass = (
        lax.psum_scatter(partial_out, "kv", scatter_dimension=1, tiled=True),
        lax.psum_scatter(partial_mass, "kv", scatter_dimension=1, tiled=True),
    )
    peak = lax.pmax(jnp.max(mass), ("seq", "kv"))
    summary = peak.reshape(1)
    mixed16 = mixed.reshape(rows, width).astype(jnp.bfloat16)
    hidden = flat + dot_plain(mixed16, full_out)
    second16 = rms_norm(hidden, second_gain).astype(jnp.bfloat16)
    part_gate, part_up, part_down = (
        lax.all_gather(w_gate, "seq", axis=0, tiled=True),
        lax.all_gather(w_up, "seq", axis=0, tiled=True),
        lax.all_gather(w_down, "seq", axis=1, tiled=True),
    )
    wide = spread(second16)
    gate = dot_plain(wide, part_gate)
    up = dot_plain(wide, part_up)
    gate_sigmoid = jax.nn.sigmoid(gate)
    swish = gate * gate_sigmoid
    inner = (swish * up).astype(jnp.bfloat16)
    result = hidden + collect(dot_plain(inner, part_down))
    grad_result16 = cotangent.reshape(rows, width)
    grad_wide = spread(grad_result16)
    grad_inner = dot_right(grad_wide, part_down)
    grad_gate = (grad_inner * up * (gate_sigmoid * (1.0 + gate * (1.0 - gate_sigmoid)))).astype(
        jnp.bfloat16
    )
    grad_up = (grad_inner * swish).astype(jnp.bfloat16)
    grad_second = collect(dot_right(grad_gate, part_gate) + dot_right(grad_up, part_up))
    grads_gate, grads_up, grads_down = (
        lax.psum_scatter(
            dot_left(wide, grad_gate).astype(jnp.bfloat16), "seq", scatter_dimension=0, tiled=True
        ).astype(jnp.float32),
        lax.psum_scatter(
            dot_left(wide, grad_up).astype(jnp.bfloat16), "seq", scatter_dimension=0, tiled=True
        ).astype(jnp.float32),
        lax.psum_scatter(
            dot_left(grad_wide, inner).astype(jnp.bfloat16), "seq", scatter_dimension=0, tiled=True
        ).astype(jnp.float32),
    )
    grads_down = grads_down.T
    grad_norm2, grad_gain2 = rms_back(hidden, second_gain, grad_second)
    grad_hidden = grad_result16.astype(jnp.float32) + grad_norm2
    grad_hidden16 = grad_hidden.astype(jnp.bfloat16)
    grad_w_out = dot_left(mixed16, grad_hidden16)
    grad_mixed = dot_right(grad_hidden16, full_out).astype(jnp.bfloat16)
    all_grads = lax.all_gather(grad_mixed.reshape(seqs, local, width), "kv", axis=1, tiled=True)

    def key_backward(pieces):
        q_seq, id_seq, g_seq, k_seq, v_seq, kid_seq = pieces
        return backward_blocks(q_seq, id_seq, g_seq, k_seq, v_seq, kid_seq, key_pos, heads)

    part_q, grad_keys, grad_values = lax.map(
        key_backward, (all_queries, all_ids, all_grads, keys, values, key_ids)
    )
    grad_queries = lax.psum_scatter(
        part_q.astype(jnp.bfloat16), "kv", scatter_dimension=1, tiled=True
    ).astype(jnp.float32)
    grad_q_lin = (
        rotate(grad_queries.reshape(shape), cosine, -sine).reshape(rows, width).astype(jnp.bfloat16)
    )
    grad_k_lin = rotate(grad_keys, cosine, -sine).reshape(rows, width).astype(jnp.bfloat16)
    grad_v_lin = grad_values.reshape(rows, width).astype(jnp.bfloat16)
    grad_w_query = dot_left(normed, grad_q_lin)
    grad_w_key = dot_left(normed, grad_k_lin)
    grad_w_value = dot_left(normed, grad_v_lin)
    grad_normed = (
        dot_right(grad_q_lin, full_query)
        + dot_right(grad_k_lin, full_key)
        + dot_right(grad_v_lin, full_value)
    )
    grad_norm1, grad_gain1 = rms_back(flat, first_gain, grad_normed)
    grad_input = (grad_hidden + grad_norm1).reshape(seqs, local, width)
    shards = (
        lax.psum_scatter(grad_w_query, ("seq", "kv"), scatter_dimension=0, tiled=True),
        lax.psum_scatter(grad_w_key, ("seq", "kv"), scatter_dimension=0, tiled=True),
        lax.psum_scatter(grad_w_value, ("seq", "kv"), scatter_dimension=0, tiled=True),
        lax.psum_scatter(grad_w_out, ("seq", "kv"), scatter_dimension=0, tiled=True),
        lax.psum_scatter(grad_gain1, ("seq", "kv"), scatter_dimension=0, tiled=True),
        lax.psum_scatter(grad_gain2, ("seq", "kv"), scatter_dimension=0, tiled=True),
    )
    return (
        result.reshape(seqs, local, width).astype(jnp.bfloat16),
        grad_input,
        shards[0],
        shards[1],
        shards[2],
        shards[3],
        shards[4],
        shards[5],
        grads_gate,
        grads_up,
        grads_down,
        summary,
    )


def solution(mesh):
    in_specs = (
        P("seq", "kv", None),
        P("seq", "kv"),
        P(("seq", "kv"), None),
        P(("seq", "kv"), None),
        P(("seq", "kv"), None),
        P(("seq", "kv"), None),
        P(("seq", "kv")),
        P(("seq", "kv")),
        P("seq", "kv"),
        P("seq", "kv"),
        P("kv", "seq"),
        P("seq", "kv", None),
    )
    out_specs = (
        P("seq", "kv", None),
        P("seq", "kv", None),
        P(("seq", "kv"), None),
        P(("seq", "kv"), None),
        P(("seq", "kv"), None),
        P(("seq", "kv"), None),
        P(("seq", "kv")),
        P(("seq", "kv")),
        P("seq", "kv"),
        P("seq", "kv"),
        P("kv", "seq"),
        P(),
    )
    return jax.shard_map(
        per_device, mesh=mesh, in_specs=in_specs, out_specs=out_specs, check_vma=False
    )
```

profile of v0, /device:TPU:0, one launch (start us, length us, event | category | flops | bytes accessed | tf_op | source)
XLA Modules:
  0.0 2292.7 jit_solution(7770938660843287544)
XLA Ops:
  11.2 43.3 %all-reduce.6 = (bf16[2048]{0:T(1024)(128)(2,1)S(1)}, bf16[2048]{0:T(1024)(128)(2,1)S(1)}) all-reduce(bf16[2048]{0:T(1024)(128)(2,1)S(1)} %dynamic-update-slice.1, bf16[2048]{0:T(1024)(128)(2,1)S(1)} %dynamic-update-slice.2), channel_id=1, replica_groups=mesh['seq'=4,'kv'=8] {'seq','kv'}, use_global_device_ids=true, to_apply=%add.1 | all-reduce | flops 4096 | bytes 16384
  57.5 33.2 %all-gather.18.cloned.1.call-done = bf16[2048,2048]{1,0:T(8,128)(2,1)} async-done(((bf16[64,2048]{1,0:T(8,128)(2,1)}), bf16[2048,2048]{1,0:T(8,128)(2,1)}) %all-gather.18.cloned.1.call-update) | async-done | bytes 8388624 | tf_op jit(solution)/shard_map/all_gather | solution.py:93
  90.7 12.3 copy.55
  103.1 66.2 %all-gather.14.cloned.1.call-done = bf16[2048,2048]{1,0:T(8,128)(2,1)} async-done(((bf16[64,2048]{1,0:T(8,128)(2,1)}), bf16[2048,2048]{1,0:T(8,128)(2,1)}) %all-gather.14.cloned.1.call-update) | async-done | bytes 8388624 | tf_op jit(solution)/shard_map/all_gather | solution.py:92
  169.3 12.4 copy.53
  181.7 5.5 convolution_bitcast_fusion
  195.1 14.2 all-reduce
  209.3 38.7 %all-gather.20.cloned.1.call-done = bf16[2048,2048]{1,0:T(8,128)(2,1)} async-done(((bf16[64,2048]{1,0:T(8,128)(2,1)}), bf16[2048,2048]{1,0:T(8,128)(2,1)}) %all-gather.20.cloned.1.call-update) | async-done | bytes 8388624 | tf_op jit(solution)/shard_map/all_gather | solution.py:94
  248.0 5.2 fusion.34
  255.7 38.7 %all-gather.16.cloned.1.call-done = bf16[1,1536,2048]{2,1,0:T(8,128)(2,1)} async-done(((bf16[1,192,2048]{2,1,0:T(8,128)(2,1)}), bf16[1,1536,2048]{2,1,0:T(8,128)(2,1)}) %all-gather.16.cloned.1.call-update) | async-done | bytes 6291472 | tf_op jit(solution)/shard_map/all_gather | solution.py:219
  294.4 8.6 copy.56
  303.0 60.7 %while.54 = (s32[]{:T(128)}, f32[3,512,2048]{2,1,0:T(8,128)}, f32[3,512,16]{1,2,0:T(8,128)}, bf16[3,512]{1,0:T(4,128)(2,1)S(1)}, f32[192]{0:T(256)S(1)}, /*index...) while((s32[]{:T(128)}, f32[3,512,2048]{2,1,0:T(8,128)}, ...), condition=%wide.region_3.4_spmd.clone.clone, body=%wide.region_1.3_spmd.clone.sunk.clone | while | flops 818180544 | bytes 35435908 | solution.py:162
  312.4 5.5 copy.137
  317.9 4.7 constant_dynamic-update-slice_fusion.6
  332.5 5.5 copy.137
  338.0 4.7 constant_dynamic-update-slice_fusion.6
  352.8 5.5 copy.137
  358.3 4.8 constant_dynamic-update-slice_fusion.6
  364.5 9.7 all-gather.22.cloned.1.call-done
  374.2 94.3 %reduce-scatter.15.cloned.1.call-done = f32[1,192,2048]{2,1,0:T(8,128)} async-done(((f32[1,1536,2048]{2,1,0:T(8,128)}), f32[1,192,2048]{2,1,0:T(8,128)}) %reduce-scatter.15.cloned.1.call-update) | async-done | bytes 1572880 | tf_op jit(solution)/shard_map/reduce_scatter | solution.py:231
  468.5 5.8 multiply_reduce_fusion.2
  477.9 72.9 %all-gather.26.cloned.1.call-done = bf16[2048,1024]{1,0:T(8,128)(2,1)} async-done(((bf16[512,1024]{1,0:T(8,128)(2,1)}), bf16[2048,1024]{1,0:T(8,128)(2,1)}) %all-gather.26.cloned.1.call-update) | async-done | bytes 4194320 | tf_op jit(solution)/shard_map/all_gather | solution.py:240
  550.8 46.4 %all-gather.24.cloned.1.call-done = bf16[1536,2048]{1,0:T(8,128)(2,1)} async-done(((bf16[192,2048]{1,0:T(8,128)(2,1)}), bf16[1536,2048]{1,0:T(8,128)(2,1)}) %all-gather.24.cloned.1.call-update) | async-done | bytes 6291472 | tf_op jit(solution)/shard_map/all_gather | solution.py:70
  597.2 11.7 fusion.83
  608.9 70.7 %all-gather.28.cloned.1.call-done = bf16[2048,1024]{1,0:T(8,128)(2,1)} async-done(((bf16[512,1024]{1,0:T(8,128)(2,1)}), bf16[2048,1024]{1,0:T(8,128)(2,1)}) %all-gather.28.cloned.1.call-update) | async-done | bytes 4194320 | tf_op jit(solution)/shard_map/all_gather | solution.py:241
  679.5 11.7 fusion.84
  691.2 69.0 %all-gather.30.cloned.1.call-done = bf16[1024,2048]{1,0:T(8,128)(2,1)} async-done(((bf16[1024,512]{1,0:T(8,128)(2,1)}), bf16[1024,2048]{1,0:T(8,128)(2,1)}) %all-gather.30.cloned.1.call-update) | async-done | bytes 4194320 | tf_op jit(solution)/shard_map/all_gather | solution.py:242
  760.2 45.8 %all-gather.32.cloned.1.call-done = bf16[1,1536,2048]{2,1,0:T(8,128)(2,1)} async-done(((bf16[1,192,2048]{2,1,0:T(8,128)(2,1)}), bf16[1,1536,2048]{2,1,0:T(8,128)(2,1)}) %all-gather.32.cloned.1.call-update) | async-done | bytes 6291472 | tf_op jit(solution)/shard_map/all_gather | solution.py:70
  806.0 18.0 multiply_convert_fusion.1
  824.1 12.0 fusion.86
  836.1 12.6 convolution_add_fusion
  848.8 13.6 fusion.85
  862.4 78.7 %reduce-scatter.19.cloned.1.call-done = f32[192,2048]{1,0:T(8,128)} async-done(((f32[1536,2048]{1,0:T(8,128)}), f32[192,2048]{1,0:T(8,128)}) %reduce-scatter.19.cloned.1.call-update) | async-done | bytes 1572880 | tf_op jit(solution)/shard_map/reduce_scatter | solution.py:74
  943.6 93.4 %reduce-scatter.17.cloned.1.call-done = f32[192,2048]{1,0:T(8,128)} async-done(((f32[1536,2048]{1,0:T(8,128)}), f32[192,2048]{1,0:T(8,128)}) %reduce-scatter.17.cloned.1.call-update) | async-done | bytes 1572880 | tf_op jit(solution)/shard_map/reduce_scatter | solution.py:74
  1041.4 7.2 convolution_convert_fusion.2
  1052.4 41.8 %all-gather.34.cloned.1.call-done = bf16[1536,2048]{1,0:T(8,128)(2,1)} async-done(((bf16[192,2048]{1,0:T(8,128)(2,1)}), bf16[1536,2048]{1,0:T(8,128)(2,1)}) %all-gather.34.cloned.1.call-update) | async-done | bytes 6291472 | tf_op jit(solution)/shard_map/all_gather | solution.py:276
  1094.2 102.0 %while.55 = (s32[]{:T(128)}, f32[192,16,128]{2,0,1:T(8,128)}, f32[192,16,128]{2,0,1:T(8,128)}, bf16[3,512,2048]{2,1,0:T(8,128)(2,1)}, bf16[3,512,2048]{1,2,0:T(8...) while((s32[]{:T(128)}, f32[192,16,128]{2,0,1:T(8,128)}, ...), condition=%wide.region_10.11_spmd.clone.clone, body=%wide.region_9.10_spmd.clone.sunk.clone | while | flops 2034930176 | bytes 97990168 | solution.py:206
  1096.1 6.6 divide_select_fusion.4
  1107.0 4.6 multiply_convert_fusion.7
  1129.8 6.6 divide_select_fusion.4
  1140.7 4.6 multiply_convert_fusion.7
  1164.0 6.6 divide_select_fusion.4
  1174.8 4.6 multiply_convert_fusion.7
  1179.5 4.3 bitcast_add_fusion.6
  1198.4 11.3 convolution_convert_fusion.1
  1211.8 11.2 convolution_convert_fusion
  1224.9 11.2 convert_bitcast_fusion
  1238.1 8.5 fusion.49
  1248.2 8.2 fusion.46
  1265.9 8.3 fusion.42
  1276.0 8.2 fusion.39
  1284.2 12.4 reduce-scatter.37.cloned.1.call-done
  1298.2 43.0 %pmax.7 = f32[1]{0:T(128)} all-reduce(f32[1]{0:T(128)} %bitcast.25), channel_id=1, replica_groups=mesh['seq'=4,'kv'=8] {'seq','kv'}, use_global_device_ids=true, to_apply=%region_27.28 | all-reduce | flops 1 | bytes 8 | tf_op jit(solution)/shard_map/pmax | solution.py:234
  1341.1 35.5 %reduce-scatter.31.cloned.1.call-done = bf16[512,1024]{1,0:T(8,128)(2,1)} async-done(((bf16[2048,1024]{1,0:T(8,128)(2,1)}), bf16[512,1024]{1,0:T(8,128)(2,1)}) %reduce-scatter.31.cloned.1.call-update) | async-done | bytes 1048592 | tf_op jit(solution)/shard_map/reduce_scatter | solution.py:260
  1379.4 76.7 %reduce-scatter.33.cloned.1.call-done = bf16[512,1024]{1,0:T(8,128)(2,1)} async-done(((bf16[2048,1024]{1,0:T(8,128)(2,1)}), bf16[512,1024]{1,0:T(8,128)(2,1)}) %reduce-scatter.33.cloned.1.call-update) | async-done | bytes 1048592 | tf_op jit(solution)/shard_map/reduce_scatter | solution.py:263
  1458.9 76.8 %reduce-scatter.35.cloned.1.call-done = bf16[512,1024]{0,1:T(8,128)(2,1)} async-done(((bf16[2048,1024]{0,1:T(8,128)(2,1)}), bf16[512,1024]{0,1:T(8,128)(2,1)}) %reduce-scatter.35.cloned.1.call-update) | async-done | bytes 1048592 | tf_op jit(solution)/shard_map/reduce_scatter | solution.py:266
  1538.7 6.4 fusion.44
  1545.1 6.5 convolution_add_fusion.2
  1551.6 4.4 fusion.31
  1556.0 44.3 %all-reduce.5 = (f32[2048]{0:T(1024)S(1)}, f32[2048]{0:T(1024)S(1)}) all-reduce(f32[2048]{0:T(1024)S(1)} %get-tuple-element.493, f32[2048]{0:T(1024)S(1)} %copy-done.23), channel_id=12, replica_groups=mesh['seq'=4,'kv'=8] {'seq','kv'}, use_global_device_ids=true, to_apply=%region_18.19.clone | all-reduce | flops 4096 | bytes 32768
  1605.0 118.3 %reduce-scatter.29.cloned.1.call-done = f32[64,2048]{1,0:T(8,128)} async-done(((f32[2048,2048]{1,0:T(8,128)}), f32[64,2048]{1,0:T(8,128)}) %reduce-scatter.29.cloned.1.call-update) | async-done | bytes 524304 | tf_op jit(solution)/shard_map/reduce_scatter | solution.py:307
  1723.3 187.5 %reduce-scatter.27.cloned.1.call-done = f32[64,2048]{1,0:T(8,128)} async-done(((f32[2048,2048]{1,0:T(8,128)}), f32[64,2048]{1,0:T(8,128)}) %reduce-scatter.27.cloned.1.call-update) | async-done | bytes 524304 | tf_op jit(solution)/shard_map/reduce_scatter | solution.py:306
  1910.9 187.5 %reduce-scatter.23.cloned.1.call-done = f32[64,2048]{1,0:T(8,128)} async-done(((f32[2048,2048]{1,0:T(8,128)}), f32[64,2048]{1,0:T(8,128)}) %reduce-scatter.23.cloned.1.call-update) | async-done | bytes 524304 | tf_op jit(solution)/shard_map/reduce_scatter | solution.py:304
  2098.4 187.5 %reduce-scatter.25.cloned.1.call-done = f32[64,2048]{1,0:T(8,128)} async-done(((f32[2048,2048]{1,0:T(8,128)}), f32[64,2048]{1,0:T(8,128)}) %reduce-scatter.25.cloned.1.call-update) | async-done | bytes 524304 | tf_op jit(solution)/shard_map/reduce_scatter | solution.py:305
  (243 shorter events, 161.1 us)
Async XLA Ops:
  7.2 83.6 %all-gather.18.cloned.1.call-start = ((), (), s32[]{:S(2)}) async-start(), calls=%async_computation.14 | async-start | bytes 8650752 | tf_op jit(solution)/shard_map/all_gather | solution.py:93
  7.9 161.4 %all-gather.14.cloned.1.call-start = ((), (), s32[]{:S(2)}) async-start(), calls=%async_computation.12 | async-start | bytes 8650752 | tf_op jit(solution)/shard_map/all_gather | solution.py:92
  8.7 239.4 %all-gather.20.cloned.1.call-start = ((), (), s32[]{:S(2)}) async-start(), calls=%async_computation.15 | async-start | bytes 8650752 | tf_op jit(solution)/shard_map/all_gather | solution.py:94
  9.4 285.0 %all-gather.16.cloned.1.call-start = ((), (), s32[]{:S(2)}) async-start(), calls=%async_computation.13 | async-start | bytes 7077888 | tf_op jit(solution)/shard_map/all_gather | solution.py:219
  54.4 193.6 %copy-start.17 = (f32[2048]{0:T(1024)}, f32[2048]{0:T(1024)S(1)}, u32[]{:S(2)}) copy-start(f32[2048]{0:T(1024)S(1)} %convert_element_type.223) | copy-start | bytes 24580
  56.4 191.6 %copy-start.21 = (f32[192]{0:T(256)}, f32[192]{0:T(256)S(1)}, u32[]{:S(2)}) copy-start(f32[192]{0:T(256)S(1)} %get-tuple-element.568) | copy-start | bytes 2308
  57.5 133.0 %copy-start.15 = (f32[192,64]{1,0:T(8,128)}, f32[192,64]{1,0:T(8,128)S(1)}, u32[]{:S(2)}) copy-start(f32[192,64]{1,0:T(8,128)S(1)} %get-tuple-element.566) | copy-start | bytes 147460
  169.3 12.4 copy-start.6
  181.7 5.9 copy-start.10
  191.6 2.0 copy-start.28
  191.6 2.6 copy-start.25
  192.9 181.3 %all-gather.22.cloned.1.call-start = ((), (), s32[]{:S(2)}) async-start(), calls=%async_computation.17 | async-start | bytes 8650752 | tf_op jit(solution)/shard_map/all_gather | solution.py:95
  193.5 275.0 %reduce-scatter.15.cloned.1.call-start = ((), (), s32[]{:S(2)}) async-start(), calls=%async_computation.16 | async-start | bytes 14155776 | tf_op jit(solution)/shard_map/reduce_scatter | solution.py:231
  363.7 187.1 %all-gather.26.cloned.1.call-start = ((), (), s32[]{:S(2)}) async-start(), calls=%async_computation.19 | async-start | bytes 5242880 | tf_op jit(solution)/shard_map/all_gather | solution.py:240
  364.4 232.7 %all-gather.24.cloned.1.call-start = ((), (), s32[]{:S(2)}) async-start(), calls=%async_computation.18 | async-start | bytes 7077888 | tf_op jit(solution)/shard_map/all_gather | solution.py:70
  475.4 204.1 %all-gather.28.cloned.1.call-start = ((), (), s32[]{:S(2)}) async-start(), calls=%async_computation.20 | async-start | bytes 5242880 | tf_op jit(solution)/shard_map/all_gather | solution.py:241
  476.2 284.1 %all-gather.30.cloned.1.call-start = ((), (), s32[]{:S(2)}) async-start(), calls=%async_computation.21 | async-start | bytes 5242880 | tf_op jit(solution)/shard_map/all_gather | solution.py:242
  476.7 329.3 %all-gather.32.cloned.1.call-start = ((), (), s32[]{:S(2)}) async-start(), calls=%async_computation.32 | async-start | bytes 7077888 | tf_op jit(solution)/shard_map/all_gather | solution.py:70
  477.5 463.7 %reduce-scatter.19.cloned.1.call-start = ((), (), s32[]{:S(2)}) async-start(), calls=%async_computation.23 | async-start | bytes 14155776 | tf_op jit(solution)/shard_map/reduce_scatter | solution.py:74
  806.0 18.0 copy-start.26
  824.1 12.0 copy-start.27
  824.1 12.0 copy-start.30
  848.8 188.3 %reduce-scatter.17.cloned.1.call-start = ((), (), s32[]{:S(2)}) async-start(), calls=%async_computation.22 | async-start | bytes 14155776 | tf_op jit(solution)/shard_map/reduce_scatter | solution.py:74
  862.4 174.6 %copy-start.13 = (bf16[1,192,2048]{2,1,0:T(8,128)(2,1)S(1)}, bf16[1,192,2048]{2,1,0:T(8,128)(2,1)}, u32[]{:S(2)}) copy-start(bf16[1,192,2048]{2,1,0:T(8,128)(2,1)} %param.27) | copy-start | bytes 2359300
  862.4 231.8 %all-gather.34.cloned.1.call-start = ((), (), s32[]{:S(2)}) async-start(), calls=%async_computation.33 | async-start | bytes 7077888 | tf_op jit(solution)/shard_map/all_gather | solution.py:276
  1040.3 1.1 copy-start.8
  1048.6 209.4 %reduce-scatter.21.cloned.1.call-start = ((), (), s32[]{:S(2)}) async-start(), calls=%async_computation.24 | async-start | bytes 7077888 | tf_op jit(solution)/shard_map/reduce_scatter | solution.py:285
  1095.9 6.8 copy-start.1
  1111.6 3.9 copy-start
  1111.6 3.9 copy-start.3
  1119.6 3.9 copy-start.4
  1129.6 6.8 copy-start.1
  1145.3 4.3 copy-start
  1145.3 4.3 copy-start.3
  1153.7 3.9 copy-start.4
  1163.7 6.8 copy-start.1
  1179.4 4.3 copy-start
  1179.5 4.3 copy-start.3
  1187.8 3.9 copy-start.4
  1196.2 100.5 %reduce-scatter.37.cloned.1.call-start = ((), (), s32[]{:S(2)}) async-start(), calls=%async_computation.34 | async-start | bytes 884736
  1198.3 178.3 %reduce-scatter.31.cloned.1.call-start = ((), (), s32[]{:S(2)}) async-start(), calls=%async_computation.29 | async-start | bytes 5242880 | tf_op jit(solution)/shard_map/reduce_scatter | solution.py:260
  1209.7 2.1 copy-start.31
  1209.7 246.4 %reduce-scatter.33.cloned.1.call-start = ((), (), s32[]{:S(2)}) async-start(), calls=%async_computation.30 | async-start | bytes 5242880 | tf_op jit(solution)/shard_map/reduce_scatter | solution.py:263
  1223.0 1.9 copy-start.29
  1223.0 312.7 %reduce-scatter.35.cloned.1.call-start = ((), (), s32[]{:S(2)}) async-start(), calls=%async_computation.31 | async-start | bytes 5242880 | tf_op jit(solution)/shard_map/reduce_scatter | solution.py:266
  1236.1 1.5 copy-start.9
  1236.1 2.0 copy-start.14
  1236.1 487.3 %reduce-scatter.29.cloned.1.call-start = ((), (), s32[]{:S(2)}) async-start(), calls=%async_computation.28 | async-start | bytes 17301504 | tf_op jit(solution)/shard_map/reduce_scatter | solution.py:307
  1246.5 1.4 copy-start.5
  1246.5 1.6 copy-start.7
  1246.6 1.6 copy-start.18
  1246.6 1.6 copy-start.22
  1246.6 664.3 %reduce-scatter.27.cloned.1.call-start = ((), (), s32[]{:S(2)}) async-start(), calls=%async_computation.27 | async-start | bytes 17301504 | tf_op jit(solution)/shard_map/reduce_scatter | solution.py:306
  1256.4 842.0 %reduce-scatter.23.cloned.1.call-start = ((), (), s32[]{:S(2)}) async-start(), calls=%async_computation.25 | async-start | bytes 17301504 | tf_op jit(solution)/shard_map/reduce_scatter | solution.py:304
  1259.7 1.4 copy-start.2
  1259.7 1.4 copy-start.16
  1259.7 1.4 copy-start.19
  1265.0 0.9 copy-start.11
  1274.3 1011.6 %reduce-scatter.25.cloned.1.call-start = ((), (), s32[]{:S(2)}) async-start(), calls=%async_computation.26 | async-start | bytes 17301504 | tf_op jit(solution)/shard_map/reduce_scatter | solution.py:305
  1535.8 2.9 copy-start.12
  1538.7 12.9 slice-start
  1545.1 6.5 slice-start.1
  1551.6 4.4 copy-start.23
  1551.6 49.9 %copy-start.24 = (f32[192]{0:T(256)S(1)}, f32[192]{0:T(256)}, u32[]{:S(2)}) copy-start(f32[192]{0:T(256)} %get-tuple-element.567) | copy-start | bytes 2308
  (1 other events, 0.9 us)
Sparse Core Ops, SparseCore 0:
  10.8 79.8 all-gather.17
  93.6 75.6 all-gather.13
  172.2 75.8 all-gather.19
  250.4 44.0 all-gather.15
  297.1 77.0 all-gather.21
  377.5 90.9 reduce-scatter.14
  470.1 80.7 all-gather.25
  553.3 43.8 all-gather.23
  598.8 80.7 all-gather.27
  681.0 79.2 all-gather.29
  762.1 43.8 all-gather.31
  848.9 92.2 reduce-scatter.18
  944.7 92.2 reduce-scatter.16
  1048.8 45.3 all-gather.33
  1196.3 61.7 reduce-scatter.20
  1261.7 34.9 reduce-scatter.36
  1298.8 77.8 reduce-scatter.30
  1378.8 77.2 reduce-scatter.32
  1458.4 77.2 reduce-scatter.34
  1538.5 184.8 reduce-scatter.28
  1726.2 184.6 reduce-scatter.26
  1913.7 184.5 reduce-scatter.22
  2101.3 184.6 reduce-scatter.24
where the time goes:
time: 2300 us; the launch traced here: 2290 us
  waiting for transfers between devices  1690 us (73%)
  matrix products  283 us (12%)
  blocking collectives  145 us (6%)
  local copies, waits for them, and re-layouts  122 us (5%)
  other arithmetic  36.4 us (2%)
    reduce_scatter x1, waiting for transfers between devices, per_device(): lax.psum_scatter(grad_w_value, ('seq', 'kv'), scatter_dimension=0, tiled=...  188 us
    reduce_scatter x1, waiting for transfers between devices, per_device(): lax.psum_scatter(grad_w_key, ('seq', 'kv'), scatter_dimension=0, tiled=True)  188 us
    reduce_scatter x1, waiting for transfers between devices, per_device(): lax.psum_scatter(grad_w_query, ('seq', 'kv'), scatter_dimension=0, tiled=...  188 us
    reduce_scatter x2, waiting for transfers between devices, collect(): return lax.psum_scatter(values, 'kv', scatter_dimension=0, tiled=True)  172 us
    reduce_scatter x1, waiting for transfers between devices, per_device(): lax.psum_scatter(grad_w_out, ('seq', 'kv'), scatter_dimension=0, tiled=True)  118 us
    unnamed x3, blocking collectives  102 us
    reduce_scatter x1, waiting for transfers between devices, per_device(): lax.psum_scatter(partial_out, 'kv', scatter_dimension=1, tiled=True)  94.3 us
    all_gather x2, waiting for transfers between devices, spread(): return lax.all_gather(values, 'kv', axis=0, tiled=True)  92.2 us
  transfers between devices with their start and end apart: 23, of which 23 were waited for; matrix products, arithmetic and copies ran while one was open for 12% of the time, Pallas kernels for 0%

commit v1 on v0

v1 whole, which is shorter than its diff:
```python
import functools
import math

import jax
import jax.numpy as jnp
from jax import lax
from jax.experimental import pallas as pl
from jax.experimental.pallas import tpu as pltpu
from jax.sharding import PartitionSpec as P

HEAD_DIM = 128
EPSILON = 1e-05
BLOCK = 256
LOG2E = math.log2(math.e)
BF16 = jnp.bfloat16
F32 = jnp.float32


def dot_plain(left, right):
    return jnp.dot(left, right, preferred_element_type=F32)


def dot_left(left, right):
    return lax.dot_general(left, right, (((0,), (0,)), ((), ())), preferred_element_type=F32)


def dot_right(left, right):
    return lax.dot_general(left, right, (((1,), (1,)), ((), ())), preferred_element_type=F32)


def rms_norm(values, gain):
    return values * lax.rsqrt(jnp.mean(values * values, axis=-1, keepdims=True) + EPSILON) * gain


def rms_back(values, gain, grad):
    inverse = lax.rsqrt(jnp.mean(values * values, axis=-1, keepdims=True) + EPSILON)
    scaled = grad * gain
    moment = jnp.mean(values * scaled, axis=-1, keepdims=True)
    return inverse * scaled - values * (inverse * inverse * inverse) * moment


ORDER = (0, 2, 4, 6, 1, 3, 5, 7)


def swap(values, mask):
    size = lax.axis_size("kv")
    return lax.ppermute(values, "kv", [(i, i ^ mask) for i in range(size)])


def owners():
    size = lax.axis_size("kv")
    if size == 8:
        return lax.axis_index("kv").astype(jnp.int32) ^ jnp.array(ORDER, jnp.int32)
    return jnp.arange(size, dtype=jnp.int32)


def gather_chunks(values):
    size = lax.axis_size("kv")
    if size != 8:
        return [lax.all_gather(values, "kv", axis=0, tiled=True)]
    half = values.shape[0] // 2
    near_x = swap(values, 2)
    near_y = swap(values, 4)
    core = swap(values, 1)
    far_top = swap(near_x[:half], 4)
    far_low = swap(near_y[half:], 2)
    core_x = swap(near_x, 1)
    core_y = swap(near_y, 1)
    core_top = swap(far_top, 1)
    core_low = swap(far_low, 1)
    return [values, near_x, near_y, far_top, far_low, core, core_x, core_y, core_top, core_low]


def gather_rows(values):
    return jnp.concatenate(gather_chunks(values), axis=0)


def add16(left, right):
    return (left.astype(F32) + right.astype(F32)).astype(BF16)


def scatter_rows(make):
    size = lax.axis_size("kv")
    if size != 8:
        full = make(0, size)
        return lax.psum_scatter(full, "kv", scatter_dimension=0, tiled=True).astype(F32)
    odd = make(4, 8)
    theirs = swap(odd, 1)
    even = make(0, 4)
    local = even.shape[0] // 4
    half = local // 2

    def both(chunk, low):
        rows = slice(chunk * local + low * half, chunk * local + (low + 1) * half)
        return add16(even[rows], theirs[rows])

    send_x = jnp.concatenate([both(1, 0), both(3, 0)], axis=0)
    send_y = jnp.concatenate([both(2, 1), both(3, 1)], axis=0)
    from_x = swap(send_x, 2)
    from_y = swap(send_y, 4)
    last_y = swap(add16(both(2, 0), from_x[half:]), 4)
    last_x = swap(add16(both(1, 1), from_y[half:]), 2)
    top = both(0, 0).astype(F32) + from_x[:half].astype(F32) + last_y.astype(F32)
    low = both(0, 1).astype(F32) + from_y[:half].astype(F32) + last_x.astype(F32)
    return jnp.concatenate([top, low], axis=0)


def spread_small(values, axis):
    size = lax.axis_size(axis)
    return lax.all_to_all(jnp.broadcast_to(values[None], (size,) + values.shape), axis, 0, 0)


def turn(values, cosine, sine):
    return values * cosine + pltpu.roll(values, HEAD_DIM // 2, 1) * sine


def forward_kernel(
    heads, parts, length, scale, offset,
    source, first, qk_hbm, v_hbm, cos_ref, sin_ref, doc_col, doc_row,
    q_ref, k_ref, v_ref, mass_ref, mixed_hbm,
    qk_s, mixed_s, sems,
):
    wide = heads * HEAD_DIM
    rows = length // parts

    def load(b):
        start = pl.multiple_of(source[b] * rows, rows)
        here = pl.ds(b * rows, rows)
        return (
            pltpu.make_async_copy(qk_hbm.at[pl.ds(start, rows), :], qk_s.at[here, :], sems.at[0, b]),
            pltpu.make_async_copy(v_hbm.at[pl.ds(start, rows), :], v_ref.at[here, :], sems.at[1, b]),
        )

    def store(b):
        start = pl.multiple_of(source[b] * rows, rows)
        return pltpu.make_async_copy(
            mixed_s.at[pl.ds(b * rows, rows), :], mixed_hbm.at[pl.ds(start, rows), :], sems.at[2, b]
        )

    for b in range(parts):
        for copy in load(b):
            copy.start()
    for b in range(parts):
        for copy in load(b):
            copy.wait()

    def rope(b, carry):
        here = pl.ds(pl.multiple_of(b * BLOCK, BLOCK), BLOCK)
        cosine = cos_ref[here, :]
        sine = sin_ref[here, :]
        for h in range(heads):
            lanes = slice(h * HEAD_DIM, (h + 1) * HEAD_DIM)
            more = slice(wide + h * HEAD_DIM, wide + (h + 1) * HEAD_DIM)
            q_ref[here, lanes] = turn(qk_s[here, lanes], cosine, sine).astype(BF16)
            k_ref[here, lanes] = turn(qk_s[here, more], cosine, sine).astype(BF16)
        return carry

    lax.fori_loop(0, length // BLOCK, rope, 0)

    def query_block(i, carry):
        here = pl.ds(pl.multiple_of(i * BLOCK, BLOCK), BLOCK)
        docs = doc_col[here, :]
        row = lax.broadcasted_iota(jnp.int32, (BLOCK, BLOCK), 0)
        col = lax.broadcasted_iota(jnp.int32, (BLOCK, BLOCK), 1)

        def key_block(j, carry):
            accs, mass = carry
            there = pl.ds(pl.multiple_of(j * BLOCK, BLOCK), BLOCK)
            allowed = (docs == doc_row[:, there]) & (row + (i - j) * BLOCK >= col)
            out = []
            for h in range(heads):
                lanes = slice(h * HEAD_DIM, (h + 1) * HEAD_DIM)
                score = dot_right(q_ref[here, lanes], k_ref[there, lanes])
                prob = 1.0 / (1.0 + jnp.exp2(score * (-scale * LOG2E) + offset * LOG2E))
                prob = jnp.where(allowed, prob, 0.0)
                for part in range(BLOCK // 128):
                    mass = mass + prob[:, part * 128 : (part + 1) * 128]
                out.append(accs[h] + dot_plain(prob.astype(BF16), v_ref[there, lanes]))
            return (tuple(out), mass)

        zero = jnp.zeros((BLOCK, HEAD_DIM), F32)
        accs, mass = lax.fori_loop(first[i], i + 1, key_block, ((zero,) * heads, zero))
        for h in range(heads):
            mixed_s[here, h * HEAD_DIM : (h + 1) * HEAD_DIM] = accs[h].astype(BF16)
        mass_ref[here, :] = jnp.sum(mass, axis=1, keepdims=True)
        return carry

    lax.fori_loop(0, length // BLOCK, query_block, 0)
    for b in range(parts):
        store(b).start()
    for b in range(parts):
        store(b).wait()


def attend_forward(source, first, qk, v, cosine, sine, doc_col, doc_row):
    length, wide = v.shape
    heads = wide // HEAD_DIM
    parts = source.shape[0]
    vmem = pl.BlockSpec(memory_space=pltpu.VMEM)
    smem = pl.BlockSpec(memory_space=pltpu.SMEM)
    hbm = pl.BlockSpec(memory_space=pl.ANY)
    same = jax.ShapeDtypeStruct((length, wide), BF16)
    return pl.pallas_call(
        functools.partial(
            forward_kernel, heads, parts, length, 1.0 / math.sqrt(HEAD_DIM), math.log(length)
        ),
        name="attend_forward",
        out_shape=(same, same, same, jax.ShapeDtypeStruct((length, 1), F32), same),
        in_specs=[smem, smem, hbm, hbm, vmem, vmem, vmem, vmem],
        out_specs=(vmem, vmem, vmem, vmem, hbm),
        scratch_shapes=[
            pltpu.VMEM((length, 2 * wide), F32),
            pltpu.VMEM((length, wide), BF16),
            pltpu.SemaphoreType.DMA((3, parts)),
        ],
        cost_estimate=pl.CostEstimate(
            flops=2 * length * length * wide,
            transcendentals=length * length * heads,
            bytes_accessed=length * wide * 18,
        ),
    )(source, first, qk, v, cosine, sine, doc_col, doc_row)


def backward_kernel(
    heads, parts, length, scale, offset,
    source, last, q_ref, k_ref, v_ref, g_hbm, cos_ref, sin_ref, doc_col, doc_row,
    out_hbm,
    g_s, dq_s, out_s, sems,
):
    wide = heads * HEAD_DIM
    rows = length // parts

    def load(b):
        start = pl.multiple_of(source[b] * rows, rows)
        return pltpu.make_async_copy(
            g_hbm.at[pl.ds(start, rows), :], g_s.at[pl.ds(b * rows, rows), :], sems.at[0, b]
        )

    def store(b):
        start = pl.multiple_of(source[b] * rows, rows)
        return pltpu.make_async_copy(
            out_s.at[pl.ds(b * rows, rows), :], out_hbm.at[pl.ds(start, rows), :], sems.at[1, b]
        )

    for b in range(parts):
        load(b).start()
    dq_s[...] = jnp.zeros_like(dq_s)
    for b in range(parts):
        load(b).wait()

    def key_block(j, carry):
        there = pl.ds(pl.multiple_of(j * BLOCK, BLOCK), BLOCK)
        docs = doc_col[there, :]
        row = lax.broadcasted_iota(jnp.int32, (BLOCK, BLOCK), 0)
        col = lax.broadcasted_iota(jnp.int32, (BLOCK, BLOCK), 1)

        def query_block(i, carry):
            dks, dvs = carry
            here = pl.ds(pl.multiple_of(i * BLOCK, BLOCK), BLOCK)
            allowed = (docs == doc_row[:, here]) & (col + (i - j) * BLOCK >= row)
            new_k, new_v = [], []
            for h in range(heads):
                lanes = slice(h * HEAD_DIM, (h + 1) * HEAD_DIM)
                query = q_ref[here, lanes]
                grad = g_s[here, lanes]
                score = dot_right(k_ref[there, lanes], query)
                prob = 1.0 / (1.0 + jnp.exp2(score * (-scale * LOG2E) + offset * LOG2E))
                prob = jnp.where(allowed, prob, 0.0)
                new_v.append(dvs[h] + dot_plain(prob.astype(BF16), grad))
                dprob = dot_right(v_ref[there, lanes], grad)
                dscore = (dprob * (prob - prob * prob)).astype(BF16)
                new_k.append(dks[h] + dot_plain(dscore, query))
                dq_s[here, lanes] += dot_left(dscore, k_ref[there, lanes])
            return (tuple(new_k), tuple(new_v))

        zero = (jnp.zeros((BLOCK, HEAD_DIM), F32),) * heads
        dks, dvs = lax.fori_loop(j, last[j], query_block, (zero, zero))
        cosine = cos_ref[there, :]
        sine = sin_ref[there, :]
        for h in range(heads):
            lanes = slice(h * HEAD_DIM, (h + 1) * HEAD_DIM)
            more = slice(wide + h * HEAD_DIM, wide + (h + 1) * HEAD_DIM)
            most = slice(2 * wide + h * HEAD_DIM, 2 * wide + (h + 1) * HEAD_DIM)
            out_s[there, lanes] = turn(dq_s[there, lanes] * scale, cosine, -sine).astype(BF16)
            out_s[there, more] = turn(dks[h] * scale, cosine, -sine).astype(BF16)
            out_s[there, most] = dvs[h].astype(BF16)
        return carry

    lax.fori_loop(0, length // BLOCK, key_block, 0)
    for b in range(parts):
        store(b).start()
    for b in range(parts):
        store(b).wait()


def attend_backward(source, last, q, k, v, grad, cosine, sine, doc_col, doc_row):
    length, wide = v.shape
    heads = wide // HEAD_DIM
    parts = source.shape[0]
    vmem = pl.BlockSpec(memory_space=pltpu.VMEM)
    smem = pl.BlockSpec(memory_space=pltpu.SMEM)
    hbm = pl.BlockSpec(memory_space=pl.ANY)
    return pl.pallas_call(
        functools.partial(
            backward_kernel, heads, parts, length, 1.0 / math.sqrt(HEAD_DIM), math.log(length)
        ),
        name="attend_backward",
        out_shape=jax.ShapeDtypeStruct((length, 3 * wide), BF16),
        in_specs=[smem, smem, vmem, vmem, vmem, hbm, vmem, vmem, vmem, vmem],
        out_specs=hbm,
        scratch_shapes=[
            pltpu.VMEM((length, wide), BF16),
            pltpu.VMEM((length, wide), F32),
            pltpu.VMEM((length, 3 * wide), BF16),
            pltpu.SemaphoreType.DMA((2, parts)),
        ],
        cost_estimate=pl.CostEstimate(
            flops=5 * length * length * wide,
            transcendentals=length * length * heads,
            bytes_accessed=length * wide * 14,
        ),
    )(source, last, q, k, v, grad, cosine, sine, doc_col, doc_row)


def per_device(
    tokens,
    doc_ids,
    w_query,
    w_key,
    w_value,
    w_out,
    gain_attn,
    gain_ffn,
    w_gate,
    w_up,
    w_down,
    cotangent,
):
    ring = lax.axis_size("seq")
    group = lax.axis_size("kv")
    seqs, local, width = tokens.shape
    length = local * group
    piece = w_query.shape[0]
    heads = width // HEAD_DIM
    planes = heads // ring
    share = group // planes
    mine = ring // share
    wide = mine * HEAD_DIM
    pairs = [[j * share + c for c in range(share)] for j in range(planes)]

    def chunk_rows(values, start, stop):
        return values[start * local : stop * local]

    flat16 = tokens.reshape(local, width)
    flat = flat16.astype(F32)
    dy16 = cotangent.reshape(local, width)

    gate_w = lax.all_gather(w_gate, "seq", axis=0, tiled=True)
    w_three = jnp.stack([w_query, w_key, w_value])
    w_three = w_three.reshape(3, piece, share, mine, planes, HEAD_DIM)
    w_three = w_three.transpose(4, 2, 1, 0, 3, 5).reshape(group, piece, 3 * wide)
    w_three = lax.all_to_all(w_three, "kv", 0, 0).reshape(group * piece, 3 * wide)
    w_three = lax.all_gather(w_three, "seq", axis=0, tiled=True)
    out_w = lax.all_gather(w_out, "seq", axis=0, tiled=False)
    out_w = lax.all_to_all(
        out_w.reshape(share, mine, piece, width), "kv", 0, 0, axis_index_groups=pairs
    )
    out_w = out_w.transpose(1, 0, 2, 3).reshape(wide, width)
    up_w = lax.all_gather(w_up, "seq", axis=0, tiled=True)
    down_w = lax.all_gather(w_down, "seq", axis=1, tiled=True)

    gains = spread_small(spread_small(jnp.stack([gain_attn, gain_ffn]), "kv"), "seq")
    gains = gains.transpose(2, 0, 1, 3).reshape(2, width).astype(F32)
    ids = spread_small(doc_ids.reshape(local), "kv")

    half = local // 2
    by_pos = jnp.concatenate([ids[:, :half], ids[::-1, half:]], axis=0).reshape(length)
    blocks = length // BLOCK
    starts = by_pos.reshape(blocks, BLOCK)[:, 0]
    ends = by_pos.reshape(blocks, BLOCK)[:, -1]
    first = jnp.sum((by_pos[None] < starts[:, None]).astype(jnp.int32), axis=1) // BLOCK
    last = (jnp.sum((by_pos[None] <= ends[:, None]).astype(jnp.int32), axis=1) + BLOCK - 1) // BLOCK
    doc_col = by_pos.reshape(length, 1)
    doc_row = by_pos.reshape(1, length)
    order = jnp.argsort(owners()).astype(jnp.int32) if group != 8 else None
    if group == 8:
        where = [ORDER.index(m) for m in range(8)]
        order = jnp.array(where, jnp.int32)[
            lax.axis_index("kv").astype(jnp.int32) ^ jnp.arange(8, dtype=jnp.int32)
        ]
    source = jnp.concatenate([2 * order, 2 * order[::-1] + 1])

    angle = jnp.arange(length, dtype=F32)[:, None] * jnp.exp(
        jnp.arange(HEAD_DIM // 2, dtype=F32) * (-2.0 * math.log(10000.0) / HEAD_DIM)
    )
    cosine = jnp.cos(angle)
    sine = jnp.sin(angle)
    cosine = jnp.concatenate([cosine, cosine], axis=1)
    sine = jnp.concatenate([-sine, sine], axis=1)

    all_tokens = gather_rows(flat16)
    normed = rms_norm(all_tokens.astype(F32), gains[0]).astype(BF16)
    qk = dot_plain(normed, w_three[:, : 2 * wide])
    v = dot_plain(normed, w_three[:, 2 * wide :]).astype(BF16)
    q, k, v, mass, mixed = attend_forward(source, first, qk, v, cosine, sine, doc_col, doc_row)

    def partial_hidden(start, stop):
        return dot_plain(chunk_rows(mixed, start, stop), out_w).astype(BF16)

    hidden = flat + scatter_rows(partial_hidden)
    masses = lax.all_to_all(mass.reshape(group, local), "kv", 0, 0)
    peak = jnp.max(jnp.sum(masses, axis=0)).reshape(1)
    peak = jnp.max(spread_small(peak, "kv")).reshape(1)
    summary = jnp.max(spread_small(peak, "seq")).reshape(1)

    second16 = rms_norm(hidden, gains[1]).astype(BF16)
    dy_all = gather_rows(dy16)
    second_all = gather_rows(second16)
    gate = dot_plain(second_all, gate_w)
    up = dot_plain(second_all, up_w)
    gate_sigmoid = jax.nn.sigmoid(gate)
    swish = gate * gate_sigmoid
    inner = (swish * up).astype(BF16)
    grad_down = dot_left(dy_all, inner).astype(BF16)
    grads_down = lax.psum_scatter(grad_down, "seq", scatter_dimension=0, tiled=True)
    grad_inner = dot_right(dy_all, down_w)
    dgate = (grad_inner * up * (gate_sigmoid * (1.0 + gate * (1.0 - gate_sigmoid)))).astype(BF16)
    dup = (grad_inner * swish).astype(BF16)

    def partial_second(start, stop):
        return (
            dot_right(chunk_rows(dgate, start, stop), gate_w)
            + dot_right(chunk_rows(dup, start, stop), up_w)
        ).astype(BF16)

    grad_second = scatter_rows(partial_second)
    grads_gate = lax.psum_scatter(
        dot_left(second_all, dgate).astype(BF16), "seq", scatter_dimension=0, tiled=True
    ).astype(F32)
    grads_up = lax.psum_scatter(
        dot_left(second_all, dup).astype(BF16), "seq", scatter_dimension=0, tiled=True
    ).astype(F32)
    grads_down = grads_down.astype(F32).T

    def partial_result(start, stop):
        return dot_plain(chunk_rows(inner, start, stop), down_w).astype(BF16)

    result = hidden + scatter_rows(partial_result)

    grad_hidden = dy16.astype(F32) + rms_back(hidden, gains[1], grad_second)
    dh_all = gather_rows(grad_hidden.astype(BF16))
    dmixed = dot_right(dh_all, out_w).astype(BF16)
    grad_w_out = dot_left(mixed, dh_all).astype(BF16)
    dqkv = attend_backward(source, last, q, k, v, dmixed, cosine, sine, doc_col, doc_row)

    def partial_normed(start, stop):
        return dot_right(chunk_rows(dqkv, start, stop), w_three).astype(BF16)

    grad_normed = scatter_rows(partial_normed)
    grad_input = grad_hidden + rms_back(flat, gains[0], grad_normed)

    grad_w_out = grad_w_out.reshape(mine, share, piece, width).transpose(1, 0, 2, 3)
    grad_w_out = lax.all_to_all(grad_w_out, "kv", 0, 0, axis_index_groups=pairs)
    grad_w_out = lax.psum_scatter(
        grad_w_out.reshape(ring * piece, width), "seq", scatter_dimension=0, tiled=True
    ).astype(F32)
    grad_three = lax.psum_scatter(
        dot_left(normed, dqkv).astype(BF16), "seq", scatter_dimension=0, tiled=True
    )
    grad_three = lax.all_to_all(grad_three.reshape(group, piece, 3 * wide), "kv", 0, 0)
    grad_three = grad_three.reshape(planes, share, piece, 3, mine, HEAD_DIM)
    grad_three = grad_three.transpose(3, 2, 1, 4, 0, 5).reshape(3, piece, width).astype(F32)

    grad_gain1 = jnp.sum(
        w_query.astype(F32) * grad_three[0]
        + w_key.astype(F32) * grad_three[1]
        + w_value.astype(F32) * grad_three[2],
        axis=1,
    ) / gain_attn.astype(F32)
    part2 = jnp.sum(w_gate.astype(F32) * grads_gate + w_up.astype(F32) * grads_up, axis=1)
    part2 = lax.all_to_all(part2.reshape(group, -1), "kv", 0, 0)
    grad_gain2 = jnp.sum(part2, axis=0) / gain_ffn.astype(F32)

    return (
        result.reshape(seqs, local, width).astype(BF16),
        grad_input.reshape(seqs, local, width),
        grad_three[0],
        grad_three[1],
        grad_three[2],
        grad_w_out,
        grad_gain1,
        grad_gain2,
        grads_gate,
        grads_up,
        grads_down,
        summary,
    )


def solution(mesh):
    tokens = P("seq", "kv", None)
    rows = P(("seq", "kv"), None)
    vector = P(("seq", "kv"))
    grid = P("seq", "kv")
    in_specs = (
        tokens, P("seq", "kv"), rows, rows, rows, rows, vector, vector, grid, grid,
        P("kv", "seq"), tokens,
    )
    out_specs = (
        tokens, tokens, rows, rows, rows, rows, vector, vector, grid, grid, P("kv", "seq"), P(),
    )
    return jax.shard_map(
        per_device, mesh=mesh, in_specs=in_specs, out_specs=out_specs, check_vma=False
    )
```

time: 2300 us -> 746 us (0.32)
  waiting for transfers between devices: 1690 us -> 264 us
  matrix products: 283 us -> 152 us
  blocking collectives: 145 us -> 55.7 us
  starting transfers between devices: 2.12 us -> 60.2 us
  local copies, waits for them, and re-layouts: 122 us -> 73.5 us
  other arithmetic: 36.4 us -> 77.1 us
  Pallas kernels: 0 us -> 37.7 us
    reduce_scatter x11 -> x5, waiting for transfers between devices: 1140 us -> 0.02 us  [the longest x1 0.01 us: per_device(): lax.psum_scatter(dot_left(normed, dqkv).astype(BF16), 'seq', scatter_dime...]
    all_gather x11 -> x5, waiting for transfers between devices: 533 us -> 62.2 us  [the longest x1 62.2 us: per_device(): down_w = lax.all_gather(w_down, 'seq', axis=1, tiled=True)]
    ppermute x0 -> x56, waiting for transfers between devices: none -> 177 us  [swap(): return lax.ppermute(values, 'kv', [(i, i ^ mask) for i in range(size)])]
    unnamed x3 -> x0, blocking collectives: 102 us -> none
    dot_general x28 -> x8, matrix products: 148 us -> 50 us  [dot_plain(): return jnp.dot(left, right, preferred_element_type=F32)]
    all_to_all x0 -> x5, blocking collectives: none -> 55.7 us  [the longest x1 17.6 us: per_device(): lax.all_to_all(w_three, 'kv', 0, 0).reshape(group * piece, 3 * wide)]
    dynamic_update_slice x15 -> x0, local copies, waits for them, and re-layouts: 45.7 us -> none  [forward_blocks(): lax.map(forward_one_block, (q_seq.reshape(count, block, nheads * HEAD_DIM...]
    pmax x1 -> x0, blocking collectives: 43 us -> none  [per_device(): peak = lax.pmax(jnp.max(mass), ('seq', 'kv'))]
  transfers between devices with their start and end apart: 23 -> 72, of which waited for: 23 -> 27; matrix products, arithmetic and copies ran while one was open for 12% -> 35% of each run, Pallas kernels for 0% -> 5%
where the time goes in v1:
time: 746 us; the launch traced here: 736 us
  waiting for transfers between devices  264 us (35%)
  matrix products  152 us (20%)
  other arithmetic  77.1 us (10%)
  local copies, waits for them, and re-layouts  73.5 us (10%)
  starting transfers between devices  60.2 us (8%)
  blocking collectives  55.7 us (7%)
  Pallas kernels  37.7 us (5%)
  between operations  15.5 us (2%)
    ppermute x56, waiting for transfers between devices, swap(): return lax.ppermute(values, 'kv', [(i, i ^ mask) for i in range(size)])  177 us
    all_gather x1, waiting for transfers between devices, per_device(): down_w = lax.all_gather(w_down, 'seq', axis=1, tiled=True)  62.2 us
    dot_general x8, matrix products, dot_right(): lax.dot_general(left, right, (((1,), (1,)), ((), ())), preferred_element_...  58.3 us
    dot_general x8, matrix products, dot_plain(): return jnp.dot(left, right, preferred_element_type=F32)  50 us
    unnamed x134, local copies, waits for them, and re-layouts  45.2 us
    dot_general x5, matrix products, dot_left(): lax.dot_general(left, right, (((0,), (0,)), ((), ())), preferred_element_...  44 us
    ppermute x56, starting transfers between devices, swap(): return lax.ppermute(values, 'kv', [(i, i ^ mask) for i in range(size)])  35.1 us
    pallas_call x1, Pallas kernels, attend_backward(): pl.pallas_call(functools.partial(backward_kernel, heads, parts, length, 1...  20.3 us
  transfers between devices with their start and end apart: 72, of which 27 were waited for; matrix products, arithmetic and copies ran while one was open for 35% of the time, Pallas kernels for 5%

profile of v1, /device:TPU:0, one launch (start us, length us, event | category | flops | bytes accessed | tf_op | source)
XLA Modules:
  0.0 736.3 jit_solution(7171928243931529492)
XLA Ops:
  13.6 17.6 %all_to_all.70 = bf16[8,64,768]{2,1,0:T(8,128)(2,1)} all-to-all(bf16[8,64,768]{2,1,0:T(8,128)(2,1)S(1)} %reshape.360), channel_id=1, replica_groups=mesh['seq'=4,'kv'=8] {'kv'}, dimensions={0} | all-to-all | bytes 1572864 | tf_op jit(solution)/shard_map/all_to_all | solution.py:362
  33.9 3.6 all-to-all-start.1
  39.9 2.9 fusion.31
  44.5 8.8 %all-to-all-done.1 = bf16[8,2,64]{2,1,0:T(2,128)(2,1)S(1)} async-done(((bf16[8,2,64]{2,1,0:T(2,128)(2,1)}), bf16[8,2,64]{2,1,0:T(2,128)(2,1)S(1)}, u32[]{:S(2)}, u32[]{:S(2)}) %all-to-all-start.1) | async-done | bytes 2080 | tf_op jit(solution)/shard_map/all_to_all | solution.py:110
  53.8 3.3 all-to-all-start
  58.5 3.4 all-to-all-done
  61.8 4.9 all-to-all-start.2
  70.6 2.7 all-to-all-done.2
  81.5 2.8 collective-permute-done.3
  89.3 6.1 all_to_all.71
  103.8 4.1 fusion
  107.9 6.0 convolution_convert_fusion.12.v_hbm
  113.9 8.3 %fusion.4.qk_hbm = f32[1536,512]{1,0:T(8,128)} fusion(bf16[2048,768]{1,0:T(8,128)(2,1)S(1)} %copy-done.36, bf16[1536,2048]{1,0:T(8,128)(2,1)} %constant_dynamic-update-slice_fusion, f32[2048]{0:T(1024)S(1)} %mul.290, f32[1536]{0:T(1024)S(1)} %add_rsqrt_fusion), kind=kOutput, calls=%fused_computation.29 | convolution fusion | flops 3233808384 | bytes 11550720 | tf_op jit(solution)/shard_map/dot_general | solution.py:20
  122.2 17.4 %attend_forward.1 = (bf16[1536,256]{1,0:T(8,128)(2,1)}, bf16[1536,256]{1,0:T(8,128)(2,1)}, bf16[1536,256]{1,0:T(8,128)(2,1)}, f32[1536,1]{1,0:T(8,128)}, bf16[1536,256]{1,0:T(8,128)(2,1)}) custom-call(s32[16]{0:T(128)} %pad_add_fusion.1.source, s32[6]{0:T(128)} %and_select_fusion.1.first, f32[1536,512]{1,0:T(8,128)} %fusion.4.qk_hbm, ...), custom_call_target="tpu_custom_call" | custom-call | flops 1207959552 | bytes 7077888 | tf_op jit(solution)/shard_map/attend_forward/pallas_call | solution.py:203
  142.9 4.5 collective-permute-done.9
  152.0 17.7 %collective-permute-done.10 = bf16[192,2048]{1,0:T(8,128)(2,1)} collective-permute-done((bf16[192,2048]{1,0:T(8,128)(2,1)}, bf16[192,2048]{1,0:T(8,128)(2,1)}, u32[]{:S(2)}, u32[]{:S(2)}) %collective-permute-start.10) | collective-permute-done | bytes 786464 | tf_op jit(solution)/shard_map/ppermute | solution.py:47
  176.8 9.7 %collective-permute-done.28 = bf16[192,2048]{1,0:T(8,128)(2,1)} collective-permute-done((bf16[192,2048]{1,0:T(8,128)(2,1)S(1)}, bf16[192,2048]{1,0:T(8,128)(2,1)}, u32[]{:S(2)}, u32[]{:S(2)}) %collective-permute-start.28) | collective-permute-done | bytes 786464 | tf_op jit(solution)/shard_map/ppermute | solution.py:47
  192.7 9.1 %collective-permute-done.30 = bf16[96,2048]{1,0:T(8,128)(2,1)S(1)} collective-permute-done((bf16[96,2048]{1,0:T(8,128)(2,1)S(1)}, bf16[96,2048]{1,0:T(8,128)(2,1)S(1)}, u32[]{:S(2)}, u32[]{:S(2)}) %collective-permute-start.30) | collective-permute-done | bytes 393248 | tf_op jit(solution)/shard_map/ppermute | solution.py:47
  203.0 4.8 collective-permute-done.11
  214.6 6.9 collective-permute-done.13
  230.0 13.6 %collective-permute-done.15 = bf16[192,2048]{1,0:T(8,128)(2,1)S(1)} collective-permute-done((bf16[192,2048]{1,0:T(8,128)(2,1)S(1)}, bf16[192,2048]{1,0:T(8,128)(2,1)S(1)}, u32[]{:S(2)}, u32[]{:S(2)}) %collective-permute-start.15) | collective-permute-done | bytes 786464 | tf_op jit(solution)/shard_map/ppermute | solution.py:47
  248.4 5.4 collective-permute-done.17
  261.1 11.7 %fusion.39 = f32[1536,1024]{1,0:T(8,128)} fusion(bf16[1536,2048]{1,0:T(8,128)(2,1)} %constant_dynamic-update-slice_fusion.10, bf16[2048,1024]{1,0:T(8,128)(2,1)} %all-gather.11.cloned.1.call-done), kind=kOutput, calls=%fused_computation.210 | convolution fusion | flops 6442450944 | bytes 16777216 | tf_op jit(solution)/shard_map/dot_general | solution.py:20
  272.8 12.2 %fusion.38 = f32[1536,1024]{1,0:T(8,128)} fusion(bf16[1536,2048]{1,0:T(8,128)(2,1)} %constant_dynamic-update-slice_fusion.10, bf16[2048,1024]{1,0:T(8,128)(2,1)} %all-gather.9.cloned.1.call-done), kind=kOutput, calls=%fused_computation.209 | convolution fusion | flops 6442450944 | bytes 16777216 | tf_op jit(solution)/shard_map/dot_general | solution.py:20
  285.0 62.2 %all-gather.13.cloned.1.call-done = bf16[1024,2048]{1,0:T(8,128)(2,1)} async-done(((bf16[1024,512]{1,0:T(8,128)(2,1)}), bf16[1024,2048]{1,0:T(8,128)(2,1)}) %all-gather.13.cloned.1.call-update) | async-done | bytes 4194320 | tf_op jit(solution)/shard_map/all_gather | solution.py:370
  347.2 17.5 %multiply_convert_fusion = (bf16[1536,1024]{1,0:T(8,128)(2,1)}, bf16[1536,1024]{1,0:T(8,128)(2,1)S(1)}, bf16[1536,1024]{1,0:T(8,128)(2,1)}) fusion(f32[1536,1024]{1,0:T(8,128)} %fusion.38, f32[1536,1024]{1,0:T(8,128)} %fusion.39, bf16[1536,2048]{1,0:T(8,128)(2,1)} %constant_dynamic-update-slice_fusion.20, bf16[1024,2048]{1,0:T(8,128)(2,1)} %all-gather.13.cloned.1.call-done), kind=kOutput, calls=%fused_computation.8 | convolution fusion | flops 6466043904 | bytes 32505856 | tf_op jit(solution)/shard_map/dot_general | solution.py:28
  366.4 11.4 %convolution_convert_fusion.2 = bf16[2048,1024]{1,0:T(8,128)(2,1)} fusion(bf16[1536,2048]{1,0:T(8,128)(2,1)} %constant_dynamic-update-slice_fusion.10, bf16[1536,1024]{1,0:T(8,128)(2,1)S(1)} %get-tuple-element.110), kind=kOutput, calls=%fused_computation.15 | convolution fusion | flops 6444548096 | bytes 13631488 | tf_op jit(solution)/shard_map/dot_general | solution.py:24
  377.8 11.2 %convolution_convert_fusion.1 = bf16[2048,1024]{1,0:T(8,128)(2,1)} fusion(bf16[1536,2048]{1,0:T(8,128)(2,1)} %constant_dynamic-update-slice_fusion.10, bf16[1536,1024]{1,0:T(8,128)(2,1)} %get-tuple-element.109), kind=kOutput, calls=%fused_computation.14 | convolution fusion | flops 6444548096 | bytes 13631488 | tf_op jit(solution)/shard_map/dot_general | solution.py:24
  389.1 6.4 fusion.12
  395.5 4.8 add_convert_fusion
  400.4 7.0 fusion.15
  407.3 6.2 add_convert_fusion.1
  418.4 8.4 %convolution_convert_fusion = bf16[2048,1024]{1,0:T(8,128)(2,1)} fusion(bf16[1536,2048]{1,0:T(8,128)(2,1)S(1)} %bitcast.110, bf16[1536,1024]{1,0:T(8,128)(2,1)S(1)} %copy-done.43), kind=kOutput, calls=%fused_computation.13 | convolution fusion | flops 6444548096 | bytes 13631488 | tf_op jit(solution)/shard_map/dot_general | solution.py:24
  426.8 10.1 %collective-permute-done.38 = bf16[192,2048]{1,0:T(8,128)(2,1)} collective-permute-done((bf16[192,2048]{1,0:T(8,128)(2,1)S(1)}, bf16[192,2048]{1,0:T(8,128)(2,1)}, u32[]{:S(2)}, u32[]{:S(2)}) %collective-permute-start.38) | collective-permute-done | bytes 786464 | tf_op jit(solution)/shard_map/ppermute | solution.py:47
  441.3 5.2 convolution_convert_fusion.5
  446.6 4.5 collective-permute-done.39
  451.1 15.5 %collective-permute-done.40 = bf16[192,2048]{1,0:T(8,128)(2,1)S(1)} collective-permute-done((bf16[192,2048]{1,0:T(8,128)(2,1)S(1)}, bf16[192,2048]{1,0:T(8,128)(2,1)S(1)}, u32[]{:S(2)}, u32[]{:S(2)}) %collective-permute-start.40) | collective-permute-done | bytes 786464 | tf_op jit(solution)/shard_map/ppermute | solution.py:47
  470.7 7.9 %collective-permute-done.41 = bf16[96,2048]{1,0:T(8,128)(2,1)S(1)} collective-permute-done((bf16[96,2048]{1,0:T(8,128)(2,1)S(1)}, bf16[96,2048]{1,0:T(8,128)(2,1)S(1)}, u32[]{:S(2)}, u32[]{:S(2)}) %collective-permute-start.41) | collective-permute-done | bytes 393248 | tf_op jit(solution)/shard_map/ppermute | solution.py:47
  484.4 3.6 convolution_convert_fusion.6
  490.1 8.9 %collective-permute-done.43 = bf16[192,2048]{1,0:T(8,128)(2,1)S(1)} collective-permute-done((bf16[192,2048]{1,0:T(8,128)(2,1)S(1)}, bf16[192,2048]{1,0:T(8,128)(2,1)S(1)}, u32[]{:S(2)}, u32[]{:S(2)}) %collective-permute-start.43) | collective-permute-done | bytes 786464 | tf_op jit(solution)/shard_map/ppermute | solution.py:47
  500.6 2.7 collective-permute-done.42
  504.2 21.3 %collective-permute-done.45 = bf16[96,2048]{1,0:T(8,128)(2,1)S(1)} collective-permute-done((bf16[96,2048]{1,0:T(8,128)(2,1)S(1)}, bf16[96,2048]{1,0:T(8,128)(2,1)S(1)}, u32[]{:S(2)}, u32[]{:S(2)}) %collective-permute-start.45) | collective-permute-done | bytes 393248 | tf_op jit(solution)/shard_map/ppermute | solution.py:47
  532.7 4.4 all-to-all-start.6
  537.1 5.8 convolution_convert_fusion.11.g_hbm
  543.0 20.3 %attend_backward.1 = bf16[1536,768]{1,0:T(8,128)(2,1)} custom-call(s32[16]{0:T(128)} %pad_add_fusion.1.source, s32[6]{0:T(128)} %and_select_fusion.last, bf16[1536,256]{1,0:T(8,128)(2,1)} %get-tuple-element.18.q_ref, bf16[1536,256]{1,0:T(8,128)(2,1)} %get-tuple-element.19.k_ref, bf16[1536,256]{1,0:T(8,128)(2,1)} %get-tuple-element.20.v_ref, ...), custom_call_target="tpu_custom_call" | custom-call | flops 3019898880 | bytes 5505024 | tf_op jit(solution)/shard_map/attend_backward/pallas_call | solution.py:303
  563.3 6.5 convolution_convert_fusion.3
  570.3 3.2 add_convert_fusion.28
  576.5 11.2 %convolution_convert_fusion.9 = bf16[2048,768]{1,0:T(8,128)(2,1)} fusion(bf16[1536,768]{1,0:T(8,128)(2,1)S(1)} %copy-done.41, bf16[1536,2048]{1,0:T(8,128)(2,1)} %constant_dynamic-update-slice_fusion, f32[2048]{0:T(1024)S(1)} %copy-done.24, f32[1536]{0:T(1024)S(1)} %copy-done.29), kind=kOutput, calls=%fused_computation.22 | convolution fusion | flops 4845993984 | bytes 11810816 | tf_op jit(solution)/shard_map/dot_general | solution.py:24
  587.8 13.9 %collective-permute-done.26 = bf16[192,2048]{1,0:T(8,128)(2,1)} collective-permute-done((bf16[192,2048]{1,0:T(8,128)(2,1)}, bf16[192,2048]{1,0:T(8,128)(2,1)}, u32[]{:S(2)}, u32[]{:S(2)}) %collective-permute-start.26) | collective-permute-done | bytes 786464 | tf_op jit(solution)/shard_map/ppermute | solution.py:47
  601.7 3.0 add_bitcast_fusion.1
  606.2 4.2 convolution_convert_fusion.4
  618.3 15.1 %all_to_all.72 = f32[8,1,192]{2,1,0:T(1,128)} all-to-all(f32[8,1,192]{2,1,0:T(1,128)} %all_to_all.58), channel_id=1, replica_groups=mesh['seq'=4,'kv'=8] {'kv'}, dimensions={0} | all-to-all | bytes 12288 | tf_op jit(solution)/shard_map/all_to_all | solution.py:411
  636.7 7.5 %all_to_all.73 = f32[8,1,1]{2,1,0:T(1,128)} all-to-all(f32[8,1,1]{2,1,0:T(1,128)S(1)} %broadcast_in_dim.13), channel_id=1, replica_groups=mesh['seq'=4,'kv'=8] {'kv'}, dimensions={0} | all-to-all | bytes 64 | tf_op jit(solution)/shard_map/all_to_all | solution.py:110
  646.2 9.3 %all_to_all.74 = f32[4,1,1]{2,1,0:T(1,128)} all-to-all(f32[4,1,1]{2,1,0:T(1,128)S(1)} %broadcast_in_dim.14), channel_id=1, replica_groups=mesh['seq'=4,'kv'=8] {'seq'}, dimensions={0} | all-to-all | bytes 32 | tf_op jit(solution)/shard_map/all_to_all | solution.py:110
  665.2 5.3 add_reduce_fusion
  671.9 4.1 all-to-all-start.7
  676.1 12.0 %collective-permute-done.53 = bf16[96,2048]{1,0:T(8,128)(2,1)} collective-permute-done((bf16[96,2048]{1,0:T(8,128)(2,1)S(1)}, bf16[96,2048]{1,0:T(8,128)(2,1)}, u32[]{:S(2)}, u32[]{:S(2)}) %collective-permute-start.53) | collective-permute-done | bytes 393248 | tf_op jit(solution)/shard_map/ppermute | solution.py:47
  688.1 3.2 convert_add_fusion.3
  691.4 2.9 convert_bitcast_fusion
  694.3 2.9 copy.77
  704.1 4.2 all-to-all-start.5
  708.4 4.1 fusion.8
  712.5 8.5 %all-to-all-done.5 = bf16[8,64,768]{2,1,0:T(8,128)(2,1)} async-done(((bf16[8,64,768]{2,1,0:T(8,128)(2,1)}), bf16[8,64,768]{2,1,0:T(8,128)(2,1)}, u32[]{:S(2)}, u32[]{:S(2)}) %all-to-all-start.5) | async-done | bytes 786464 | tf_op jit(solution)/shard_map/all_to_all | solution.py:470
  721.0 2.8 reshape.369
  (362 shorter events, 164.0 us)
Async XLA Ops:
  7.2 82.1 %all-gather.15.cloned.1.call-start = ((), (), s32[]{:S(2)}) async-start(), calls=%async_computation.25 | async-start | bytes 1310720 | tf_op jit(solution)/shard_map/all_gather | solution.py:364
  7.9 100.0 %all-gather.7.cloned.1.call-start = ((), (), s32[]{:S(2)}) async-start(), calls=%async_computation.16 | async-start | bytes 3932160 | tf_op jit(solution)/shard_map/all_gather | solution.py:363
  31.2 229.9 %all-gather.11.cloned.1.call-start = ((), (), s32[]{:S(2)}) async-start(), calls=%async_computation.18 | async-start | bytes 5242880 | tf_op jit(solution)/shard_map/all_gather | solution.py:369
  32.0 56.4 %collective-permute-start.4 = (bf16[192,2048]{1,0:T(8,128)(2,1)S(1)}, bf16[192,2048]{1,0:T(8,128)(2,1)S(1)}, u32[]{:S(2)}, u32[]{:S(2)}) collective-permute-start(bf16[192,2048]{1,0:T(8,128)(2,1)S(1)} %bitcast.85), channel_id=1, source_target_pairs={{0,1},{1,0},{2,3},{3,2},{4,5},{5,4},{6,7},{7,6},{8,9},{9,8},{10,11... | collective-permute-start | bytes 2359304 | tf_op jit(solution)/shard_map/ppermute | solution.py:47
  32.1 42.1 %collective-permute-start.1 = (bf16[192,2048]{1,0:T(8,128)(2,1)S(1)}, bf16[192,2048]{1,0:T(8,128)(2,1)}, u32[]{:S(2)}, u32[]{:S(2)}) collective-permute-start(bf16[192,2048]{1,0:T(8,128)(2,1)S(1)} %bitcast.86), channel_id=1, source_target_pairs={{0,4},{1,5},{2,6},{3,7},{4,0},{5,1},{6,2},{7,3},{8,12},{9,13},{10,... | collective-permute-start | bytes 2359304 | tf_op jit(solution)/shard_map/ppermute | solution.py:47
  32.7 42.6 %collective-permute-start = (bf16[192,2048]{1,0:T(8,128)(2,1)S(1)}, bf16[192,2048]{1,0:T(8,128)(2,1)}, u32[]{:S(2)}, u32[]{:S(2)}) collective-permute-start(bf16[192,2048]{1,0:T(8,128)(2,1)S(1)} %bitcast.87), channel_id=1, source_target_pairs={{0,2},{1,3},{2,0},{3,1},{4,6},{5,7},{6,4},{7,5},{8,10},{9,11},{10,... | collective-permute-start | bytes 2359304 | tf_op jit(solution)/shard_map/ppermute | solution.py:47
  33.9 19.4 %all-to-all-start.1 = ((bf16[8,2,64]{2,1,0:T(2,128)(2,1)}), bf16[8,2,64]{2,1,0:T(2,128)(2,1)S(1)}, u32[]{:S(2)}, u32[]{:S(2)}) async-start(bf16[8,2,64]{2,1,0:T(2,128)(2,1)} %broadcast_in_dim.11), calls=%async_computation.1 | async-start | bytes 8192 | tf_op jit(solution)/shard_map/all_to_all | solution.py:110
  37.5 235.3 %all-gather.9.cloned.1.call-start = ((), (), s32[]{:S(2)}) async-start(), calls=%async_computation.17 | async-start | bytes 5242880 | tf_op jit(solution)/shard_map/all_gather | solution.py:358
  61.8 11.5 %all-to-all-start.2 = ((bf16[4,2,512]{2,1,0:T(2,128)(2,1)}), bf16[4,2,512]{2,1,0:T(2,128)(2,1)S(1)}, u32[]{:S(2)}, u32[]{:S(2)}) async-start(bf16[4,2,512]{2,1,0:T(2,128)(2,1)} %reshape.395), calls=%async_computation.2 | async-start | bytes 16384 | tf_op jit(solution)/shard_map/all_to_all | solution.py:110
  66.7 280.5 %all-gather.13.cloned.1.call-start = ((), (), s32[]{:S(2)}) async-start(), calls=%async_computation.19 | async-start | bytes 5242880 | tf_op jit(solution)/shard_map/all_gather | solution.py:370
  76.3 9.4 %collective-permute-start.2 = (bf16[96,2048]{1,0:T(8,128)(2,1)S(1)}, bf16[96,2048]{1,0:T(8,128)(2,1)}, u32[]{:S(2)}, u32[]{:S(2)}) collective-permute-start(bf16[96,2048]{1,0:T(8,128)(2,1)S(1)} %slice.451), channel_id=1, source_target_pairs={{0,4},{1,5},{2,6},{3,7},{4,0},{5,1},{6,2},{7,3},{8,12},{9,13},{10,... | collective-permute-start | bytes 1179656 | tf_op jit(solution)/shard_map/ppermute | solution.py:47
  76.7 21.3 %collective-permute-start.6 = (bf16[192,2048]{1,0:T(8,128)(2,1)}, bf16[192,2048]{1,0:T(8,128)(2,1)}, u32[]{:S(2)}, u32[]{:S(2)}) collective-permute-start(bf16[192,2048]{1,0:T(8,128)(2,1)} %collective-permute-done.1), channel_id=1, source_target_pairs={{0,1},{1,0},{2,3},{3,2},{4,5},{5,4},{6,7},{7,6},{8,9},{9,8},{10,11... | collective-permute-start | bytes 2359304 | tf_op jit(solution)/shard_map/ppermute | solution.py:47
  76.8 18.8 %collective-permute-start.5 = (bf16[192,2048]{1,0:T(8,128)(2,1)}, bf16[192,2048]{1,0:T(8,128)(2,1)}, u32[]{:S(2)}, u32[]{:S(2)}) collective-permute-start(bf16[192,2048]{1,0:T(8,128)(2,1)} %collective-permute-done), channel_id=1, source_target_pairs={{0,1},{1,0},{2,3},{3,2},{4,5},{5,4},{6,7},{7,6},{8,9},{9,8},{10,11... | collective-permute-start | bytes 2359304 | tf_op jit(solution)/shard_map/ppermute | solution.py:47
  84.3 17.6 %collective-permute-start.8 = (bf16[96,2048]{1,0:T(8,128)(2,1)S(1)}, bf16[96,2048]{1,0:T(8,128)(2,1)}, u32[]{:S(2)}, u32[]{:S(2)}) collective-permute-start(bf16[96,2048]{1,0:T(8,128)(2,1)S(1)} %collective-permute-done.3), channel_id=1, source_target_pairs={{0,1},{1,0},{2,3},{3,2},{4,5},{5,4},{6,7},{7,6},{8,9},{9,8},{10,11... | collective-permute-start | bytes 1179656 | tf_op jit(solution)/shard_map/ppermute | solution.py:47
  85.8 14.4 %collective-permute-start.7 = (bf16[96,2048]{1,0:T(8,128)(2,1)}, bf16[96,2048]{1,0:T(8,128)(2,1)}, u32[]{:S(2)}, u32[]{:S(2)}) collective-permute-start(bf16[96,2048]{1,0:T(8,128)(2,1)} %collective-permute-done.2), channel_id=1, source_target_pairs={{0,1},{1,0},{2,3},{3,2},{4,5},{5,4},{6,7},{7,6},{8,9},{9,8},{10,11... | collective-permute-start | bytes 1179656 | tf_op jit(solution)/shard_map/ppermute | solution.py:47
  148.9 20.7 %collective-permute-start.10 = (bf16[192,2048]{1,0:T(8,128)(2,1)}, bf16[192,2048]{1,0:T(8,128)(2,1)}, u32[]{:S(2)}, u32[]{:S(2)}) collective-permute-start(bf16[192,2048]{1,0:T(8,128)(2,1)} %pad_maximum_fusion.2), channel_id=1, source_target_pairs={{0,2},{1,3},{2,0},{3,1},{4,6},{5,7},{6,4},{7,5},{8,10},{9,11},{10,... | collective-permute-start | bytes 2359304 | tf_op jit(solution)/shard_map/ppermute | solution.py:47
  150.5 61.8 %collective-permute-start.32 = (bf16[192,2048]{1,0:T(8,128)(2,1)S(1)}, bf16[192,2048]{1,0:T(8,128)(2,1)}, u32[]{:S(2)}, u32[]{:S(2)}) collective-permute-start(bf16[192,2048]{1,0:T(8,128)(2,1)S(1)} %bitcast.97), channel_id=1, source_target_pairs={{0,1},{1,0},{2,3},{3,2},{4,5},{5,4},{6,7},{7,6},{8,9},{9,8},{10,11... | collective-permute-start | bytes 2359304 | tf_op jit(solution)/shard_map/ppermute | solution.py:47
  150.5 24.8 %collective-permute-start.29 = (bf16[192,2048]{1,0:T(8,128)(2,1)S(1)}, bf16[192,2048]{1,0:T(8,128)(2,1)S(1)}, u32[]{:S(2)}, u32[]{:S(2)}) collective-permute-start(bf16[192,2048]{1,0:T(8,128)(2,1)S(1)} %bitcast.98), channel_id=1, source_target_pairs={{0,4},{1,5},{2,6},{3,7},{4,0},{5,1},{6,2},{7,3},{8,12},{9,13},{10,... | collective-permute-start | bytes 2359304 | tf_op jit(solution)/shard_map/ppermute | solution.py:47
  151.1 35.4 %collective-permute-start.28 = (bf16[192,2048]{1,0:T(8,128)(2,1)S(1)}, bf16[192,2048]{1,0:T(8,128)(2,1)}, u32[]{:S(2)}, u32[]{:S(2)}) collective-permute-start(bf16[192,2048]{1,0:T(8,128)(2,1)S(1)} %bitcast.99), channel_id=1, source_target_pairs={{0,2},{1,3},{2,0},{3,1},{4,6},{5,7},{6,4},{7,5},{8,10},{9,11},{10,... | collective-permute-start | bytes 2359304 | tf_op jit(solution)/shard_map/ppermute | solution.py:47
  151.7 513.5 %reduce-scatter.10.cloned.1.call-start = ((), (), s32[]{:S(2)}) async-start(), calls=%async_computation.22 | async-start | bytes 5242880 | tf_op jit(solution)/shard_map/reduce_scatter | solution.py:437
  172.8 35.0 %collective-permute-start.12 = (bf16[192,2048]{1,0:T(8,128)(2,1)}, bf16[192,2048]{1,0:T(8,128)(2,1)}, u32[]{:S(2)}, u32[]{:S(2)}) collective-permute-start(bf16[192,2048]{1,0:T(8,128)(2,1)} %pad_maximum_fusion.3), channel_id=1, source_target_pairs={{0,4},{1,5},{2,6},{3,7},{4,0},{5,1},{6,2},{7,3},{8,12},{9,13},{10,... | collective-permute-start | bytes 2359304 | tf_op jit(solution)/shard_map/ppermute | solution.py:47
  175.3 27.2 %collective-permute-start.31 = (bf16[96,2048]{1,0:T(8,128)(2,1)S(1)}, bf16[96,2048]{1,0:T(8,128)(2,1)S(1)}, u32[]{:S(2)}, u32[]{:S(2)}) collective-permute-start(bf16[96,2048]{1,0:T(8,128)(2,1)S(1)} %slice.502), channel_id=1, source_target_pairs={{0,2},{1,3},{2,0},{3,1},{4,6},{5,7},{6,4},{7,5},{8,10},{9,11},{10,... | collective-permute-start | bytes 1179656 | tf_op jit(solution)/shard_map/ppermute | solution.py:47
  187.5 14.2 %collective-permute-start.30 = (bf16[96,2048]{1,0:T(8,128)(2,1)S(1)}, bf16[96,2048]{1,0:T(8,128)(2,1)S(1)}, u32[]{:S(2)}, u32[]{:S(2)}) collective-permute-start(bf16[96,2048]{1,0:T(8,128)(2,1)S(1)} %slice.501), channel_id=1, source_target_pairs={{0,4},{1,5},{2,6},{3,7},{4,0},{5,1},{6,2},{7,3},{8,12},{9,13},{10,... | collective-permute-start | bytes 1179656 | tf_op jit(solution)/shard_map/ppermute | solution.py:47
  190.4 17.5 %collective-permute-start.11 = (bf16[96,2048]{1,0:T(8,128)(2,1)S(1)}, bf16[96,2048]{1,0:T(8,128)(2,1)S(1)}, u32[]{:S(2)}, u32[]{:S(2)}) collective-permute-start(bf16[96,2048]{1,0:T(8,128)(2,1)S(1)} %get-tuple-element.135), channel_id=1, source_target_pairs={{0,4},{1,5},{2,6},{3,7},{4,0},{5,1},{6,2},{7,3},{8,12},{9,13},{10,... | collective-permute-start | bytes 1179656 | tf_op jit(solution)/shard_map/ppermute | solution.py:47
  201.7 25.8 %collective-permute-start.34 = (bf16[192,2048]{1,0:T(8,128)(2,1)S(1)}, bf16[192,2048]{1,0:T(8,128)(2,1)S(1)}, u32[]{:S(2)}, u32[]{:S(2)}) collective-permute-start(bf16[192,2048]{1,0:T(8,128)(2,1)S(1)} %collective-permute-done.29), channel_id=1, source_target_pairs={{0,1},{1,0},{2,3},{3,2},{4,5},{5,4},{6,7},{7,6},{8,9},{9,8},{10,11... | collective-permute-start | bytes 2359304 | tf_op jit(solution)/shard_map/ppermute | solution.py:47
  202.5 22.6 %collective-permute-start.33 = (bf16[192,2048]{1,0:T(8,128)(2,1)}, bf16[192,2048]{1,0:T(8,128)(2,1)S(1)}, u32[]{:S(2)}, u32[]{:S(2)}) collective-permute-start(bf16[192,2048]{1,0:T(8,128)(2,1)} %collective-permute-done.28), channel_id=1, source_target_pairs={{0,1},{1,0},{2,3},{3,2},{4,5},{5,4},{6,7},{7,6},{8,9},{9,8},{10,11... | collective-permute-start | bytes 2359304 | tf_op jit(solution)/shard_map/ppermute | solution.py:47
  207.8 21.4 %collective-permute-start.36 = (bf16[96,2048]{1,0:T(8,128)(2,1)S(1)}, bf16[96,2048]{1,0:T(8,128)(2,1)S(1)}, u32[]{:S(2)}, u32[]{:S(2)}) collective-permute-start(bf16[96,2048]{1,0:T(8,128)(2,1)S(1)} %collective-permute-done.31), channel_id=1, source_target_pairs={{0,1},{1,0},{2,3},{3,2},{4,5},{5,4},{6,7},{7,6},{8,9},{9,8},{10,11... | collective-permute-start | bytes 1179656 | tf_op jit(solution)/shard_map/ppermute | solution.py:47
  209.9 11.6 %collective-permute-start.13 = (bf16[96,2048]{1,0:T(8,128)(2,1)S(1)}, bf16[96,2048]{1,0:T(8,128)(2,1)S(1)}, u32[]{:S(2)}, u32[]{:S(2)}) collective-permute-start(bf16[96,2048]{1,0:T(8,128)(2,1)S(1)} %get-tuple-element.134), channel_id=1, source_target_pairs={{0,2},{1,3},{2,0},{3,1},{4,6},{5,7},{6,4},{7,5},{8,10},{9,11},{10,... | collective-permute-start | bytes 1179656 | tf_op jit(solution)/shard_map/ppermute | solution.py:47
  212.2 16.2 %collective-permute-start.35 = (bf16[96,2048]{1,0:T(8,128)(2,1)S(1)}, bf16[96,2048]{1,0:T(8,128)(2,1)S(1)}, u32[]{:S(2)}, u32[]{:S(2)}) collective-permute-start(bf16[96,2048]{1,0:T(8,128)(2,1)S(1)} %collective-permute-done.30), channel_id=1, source_target_pairs={{0,1},{1,0},{2,3},{3,2},{4,5},{5,4},{6,7},{7,6},{8,9},{9,8},{10,11... | collective-permute-start | bytes 1179656 | tf_op jit(solution)/shard_map/ppermute | solution.py:47
  224.4 19.2 %collective-permute-start.15 = (bf16[192,2048]{1,0:T(8,128)(2,1)S(1)}, bf16[192,2048]{1,0:T(8,128)(2,1)S(1)}, u32[]{:S(2)}, u32[]{:S(2)}) collective-permute-start(bf16[192,2048]{1,0:T(8,128)(2,1)S(1)} %get-tuple-element.108), channel_id=1, source_target_pairs={{0,4},{1,5},{2,6},{3,7},{4,0},{5,1},{6,2},{7,3},{8,12},{9,13},{10,... | collective-permute-start | bytes 2359304 | tf_op jit(solution)/shard_map/ppermute | solution.py:47
  225.1 20.1 %collective-permute-start.14 = (bf16[192,2048]{1,0:T(8,128)(2,1)S(1)}, bf16[192,2048]{1,0:T(8,128)(2,1)S(1)}, u32[]{:S(2)}, u32[]{:S(2)}) collective-permute-start(bf16[192,2048]{1,0:T(8,128)(2,1)S(1)} %get-tuple-element.108), channel_id=1, source_target_pairs={{0,2},{1,3},{2,0},{3,1},{4,6},{5,7},{6,4},{7,5},{8,10},{9,11},{10,... | collective-permute-start | bytes 2359304 | tf_op jit(solution)/shard_map/ppermute | solution.py:47
  230.0 26.6 %collective-permute-start.18 = (bf16[192,2048]{1,0:T(8,128)(2,1)S(1)}, bf16[192,2048]{1,0:T(8,128)(2,1)S(1)}, u32[]{:S(2)}, u32[]{:S(2)}) collective-permute-start(bf16[192,2048]{1,0:T(8,128)(2,1)S(1)} %get-tuple-element.108), channel_id=1, source_target_pairs={{0,1},{1,0},{2,3},{3,2},{4,5},{5,4},{6,7},{7,6},{8,9},{9,8},{10,11... | collective-permute-start | bytes 2359304 | tf_op jit(solution)/shard_map/ppermute | solution.py:47
  243.6 10.1 %collective-permute-start.17 = (bf16[96,2048]{1,0:T(8,128)(2,1)S(1)}, bf16[96,2048]{1,0:T(8,128)(2,1)S(1)}, u32[]{:S(2)}, u32[]{:S(2)}) collective-permute-start(bf16[96,2048]{1,0:T(8,128)(2,1)S(1)} %slice.478), channel_id=1, source_target_pairs={{0,2},{1,3},{2,0},{3,1},{4,6},{5,7},{6,4},{7,5},{8,10},{9,11},{10,... | collective-permute-start | bytes 1179656 | tf_op jit(solution)/shard_map/ppermute | solution.py:47
  245.2 9.8 %collective-permute-start.16 = (bf16[96,2048]{1,0:T(8,128)(2,1)S(1)}, bf16[96,2048]{1,0:T(8,128)(2,1)S(1)}, u32[]{:S(2)}, u32[]{:S(2)}) collective-permute-start(bf16[96,2048]{1,0:T(8,128)(2,1)S(1)} %slice.477), channel_id=1, source_target_pairs={{0,4},{1,5},{2,6},{3,7},{4,0},{5,1},{6,2},{7,3},{8,12},{9,13},{10,... | collective-permute-start | bytes 1179656 | tf_op jit(solution)/shard_map/ppermute | solution.py:47
  245.9 12.7 %collective-permute-start.20 = (bf16[192,2048]{1,0:T(8,128)(2,1)S(1)}, bf16[192,2048]{1,0:T(8,128)(2,1)S(1)}, u32[]{:S(2)}, u32[]{:S(2)}) collective-permute-start(bf16[192,2048]{1,0:T(8,128)(2,1)S(1)} %collective-permute-done.15), channel_id=1, source_target_pairs={{0,1},{1,0},{2,3},{3,2},{4,5},{5,4},{6,7},{7,6},{8,9},{9,8},{10,11... | collective-permute-start | bytes 2359304 | tf_op jit(solution)/shard_map/ppermute | solution.py:47
  245.9 11.7 %collective-permute-start.19 = (bf16[192,2048]{1,0:T(8,128)(2,1)S(1)}, bf16[192,2048]{1,0:T(8,128)(2,1)S(1)}, u32[]{:S(2)}, u32[]{:S(2)}) collective-permute-start(bf16[192,2048]{1,0:T(8,128)(2,1)S(1)} %collective-permute-done.14), channel_id=1, source_target_pairs={{0,1},{1,0},{2,3},{3,2},{4,5},{5,4},{6,7},{7,6},{8,9},{9,8},{10,11... | collective-permute-start | bytes 2359304 | tf_op jit(solution)/shard_map/ppermute | solution.py:47
  377.8 287.5 %reduce-scatter.12.cloned.1.call-start = ((), (), s32[]{:S(2)}) async-start(), calls=%async_computation.23 | async-start | bytes 5242880 | tf_op jit(solution)/shard_map/reduce_scatter | solution.py:440
  389.0 302.4 %reduce-scatter.14.cloned.1.call-start = ((), (), s32[]{:S(2)}) async-start(), calls=%async_computation.24 | async-start | bytes 5242880 | tf_op jit(solution)/shard_map/reduce_scatter | solution.py:425
  400.4 13.2 %collective-permute-start.37 = (bf16[768,2048]{1,0:T(8,128)(2,1)}, bf16[768,2048]{1,0:T(8,128)(2,1)S(1)}, u32[]{:S(2)}, u32[]{:S(2)}) collective-permute-start(bf16[768,2048]{1,0:T(8,128)(2,1)} %add_convert_fusion), channel_id=1, source_target_pairs={{0,1},{1,0},{2,3},{3,2},{4,5},{5,4},{6,7},{7,6},{8,9},{9,8},{10,11... | collective-permute-start | bytes 9437192 | tf_op jit(solution)/shard_map/ppermute | solution.py:47
  416.8 20.1 %collective-permute-start.38 = (bf16[192,2048]{1,0:T(8,128)(2,1)S(1)}, bf16[192,2048]{1,0:T(8,128)(2,1)}, u32[]{:S(2)}, u32[]{:S(2)}) collective-permute-start(bf16[192,2048]{1,0:T(8,128)(2,1)S(1)} %pad_maximum_fusion.6), channel_id=1, source_target_pairs={{0,2},{1,3},{2,0},{3,1},{4,6},{5,7},{6,4},{7,5},{8,10},{9,11},{10,... | collective-permute-start | bytes 2359304 | tf_op jit(solution)/shard_map/ppermute | solution.py:47
  439.1 12.1 %collective-permute-start.39 = (bf16[96,2048]{1,0:T(8,128)(2,1)S(1)}, bf16[96,2048]{1,0:T(8,128)(2,1)S(1)}, u32[]{:S(2)}, u32[]{:S(2)}) collective-permute-start(bf16[96,2048]{1,0:T(8,128)(2,1)S(1)} %get-tuple-element.121), channel_id=1, source_target_pairs={{0,4},{1,5},{2,6},{3,7},{4,0},{5,1},{6,2},{7,3},{8,12},{9,13},{10,... | collective-permute-start | bytes 1179656 | tf_op jit(solution)/shard_map/ppermute | solution.py:47
  440.7 26.0 %collective-permute-start.40 = (bf16[192,2048]{1,0:T(8,128)(2,1)S(1)}, bf16[192,2048]{1,0:T(8,128)(2,1)S(1)}, u32[]{:S(2)}, u32[]{:S(2)}) collective-permute-start(bf16[192,2048]{1,0:T(8,128)(2,1)S(1)} %pad_maximum_fusion.7), channel_id=1, source_target_pairs={{0,4},{1,5},{2,6},{3,7},{4,0},{5,1},{6,2},{7,3},{8,12},{9,13},{10,... | collective-permute-start | bytes 2359304 | tf_op jit(solution)/shard_map/ppermute | solution.py:47
  446.6 41.5 %collective-permute-start.23 = (bf16[768,2048]{1,0:T(8,128)(2,1)S(1)}, bf16[768,2048]{1,0:T(8,128)(2,1)S(1)}, u32[]{:S(2)}, u32[]{:S(2)}) collective-permute-start(bf16[768,2048]{1,0:T(8,128)(2,1)S(1)} %convolution_convert_fusion.5), channel_id=1, source_target_pairs={{0,1},{1,0},{2,3},{3,2},{4,5},{5,4},{6,7},{7,6},{8,9},{9,8},{10,11... | collective-permute-start | bytes 9437192 | tf_op jit(solution)/shard_map/ppermute | solution.py:47
  468.6 10.0 %collective-permute-start.41 = (bf16[96,2048]{1,0:T(8,128)(2,1)S(1)}, bf16[96,2048]{1,0:T(8,128)(2,1)S(1)}, u32[]{:S(2)}, u32[]{:S(2)}) collective-permute-start(bf16[96,2048]{1,0:T(8,128)(2,1)S(1)} %get-tuple-element.120), channel_id=1, source_target_pairs={{0,2},{1,3},{2,0},{3,1},{4,6},{5,7},{6,4},{7,5},{8,10},{9,11},{10,... | collective-permute-start | bytes 1179656 | tf_op jit(solution)/shard_map/ppermute | solution.py:47
  481.4 17.6 %collective-permute-start.43 = (bf16[192,2048]{1,0:T(8,128)(2,1)S(1)}, bf16[192,2048]{1,0:T(8,128)(2,1)S(1)}, u32[]{:S(2)}, u32[]{:S(2)}) collective-permute-start(bf16[192,2048]{1,0:T(8,128)(2,1)S(1)} %get-tuple-element.106), channel_id=1, source_target_pairs={{0,4},{1,5},{2,6},{3,7},{4,0},{5,1},{6,2},{7,3},{8,12},{9,13},{10,... | collective-permute-start | bytes 2359304 | tf_op jit(solution)/shard_map/ppermute | solution.py:47
  483.0 20.4 %collective-permute-start.42 = (bf16[192,2048]{1,0:T(8,128)(2,1)S(1)}, bf16[192,2048]{1,0:T(8,128)(2,1)S(1)}, u32[]{:S(2)}, u32[]{:S(2)}) collective-permute-start(bf16[192,2048]{1,0:T(8,128)(2,1)S(1)} %get-tuple-element.106), channel_id=1, source_target_pairs={{0,2},{1,3},{2,0},{3,1},{4,6},{5,7},{6,4},{7,5},{8,10},{9,11},{10,... | collective-permute-start | bytes 2359304 | tf_op jit(solution)/shard_map/ppermute | solution.py:47
  489.6 80.7 %collective-permute-start.24 = (bf16[192,2048]{1,0:T(8,128)(2,1)}, bf16[192,2048]{1,0:T(8,128)(2,1)}, u32[]{:S(2)}, u32[]{:S(2)}) collective-permute-start(bf16[192,2048]{1,0:T(8,128)(2,1)} %pad_maximum_fusion.4), channel_id=1, source_target_pairs={{0,2},{1,3},{2,0},{3,1},{4,6},{5,7},{6,4},{7,5},{8,10},{9,11},{10,... | collective-permute-start | bytes 2359304 | tf_op jit(solution)/shard_map/ppermute | solution.py:47
  490.1 36.0 %collective-permute-start.46 = (bf16[192,2048]{1,0:T(8,128)(2,1)S(1)}, bf16[192,2048]{1,0:T(8,128)(2,1)S(1)}, u32[]{:S(2)}, u32[]{:S(2)}) collective-permute-start(bf16[192,2048]{1,0:T(8,128)(2,1)S(1)} %get-tuple-element.106), channel_id=1, source_target_pairs={{0,1},{1,0},{2,3},{3,2},{4,5},{5,4},{6,7},{7,6},{8,9},{9,8},{10,11... | collective-permute-start | bytes 2359304 | tf_op jit(solution)/shard_map/ppermute | solution.py:47
  499.1 26.4 %collective-permute-start.45 = (bf16[96,2048]{1,0:T(8,128)(2,1)S(1)}, bf16[96,2048]{1,0:T(8,128)(2,1)S(1)}, u32[]{:S(2)}, u32[]{:S(2)}) collective-permute-start(bf16[96,2048]{1,0:T(8,128)(2,1)S(1)} %slice.529), channel_id=1, source_target_pairs={{0,2},{1,3},{2,0},{3,1},{4,6},{5,7},{6,4},{7,5},{8,10},{9,11},{10,... | collective-permute-start | bytes 1179656 | tf_op jit(solution)/shard_map/ppermute | solution.py:47
  503.4 22.1 %collective-permute-start.44 = (bf16[96,2048]{1,0:T(8,128)(2,1)S(1)}, bf16[96,2048]{1,0:T(8,128)(2,1)S(1)}, u32[]{:S(2)}, u32[]{:S(2)}) collective-permute-start(bf16[96,2048]{1,0:T(8,128)(2,1)S(1)} %slice.528), channel_id=1, source_target_pairs={{0,4},{1,5},{2,6},{3,7},{4,0},{5,1},{6,2},{7,3},{8,12},{9,13},{10,... | collective-permute-start | bytes 1179656 | tf_op jit(solution)/shard_map/ppermute | solution.py:47
  504.0 22.3 %collective-permute-start.47 = (bf16[192,2048]{1,0:T(8,128)(2,1)S(1)}, bf16[192,2048]{1,0:T(8,128)(2,1)S(1)}, u32[]{:S(2)}, u32[]{:S(2)}) collective-permute-start(bf16[192,2048]{1,0:T(8,128)(2,1)S(1)} %collective-permute-done.42), channel_id=1, source_target_pairs={{0,1},{1,0},{2,3},{3,2},{4,5},{5,4},{6,7},{7,6},{8,9},{9,8},{10,11... | collective-permute-start | bytes 2359304 | tf_op jit(solution)/shard_map/ppermute | solution.py:47
  532.7 10.3 %all-to-all-start.6 = ((bf16[2,2,64,2048]{3,2,1,0:T(8,128)(2,1)}), bf16[2,2,64,2048]{3,2,1,0:T(8,128)(2,1)}, u32[]{:S(2)}, u32[]{:S(2)}) async-start(bf16[2,2,64,2048]{3,2,1,0:T(8,128)(2,1)} %bitcast.103), calls=%async_computation.7 | async-start | bytes 2097152 | tf_op jit(solution)/shard_map/all_to_all | solution.py:463
  537.1 162.5 %reduce-scatter.8.cloned.1.call-start = ((), (), s32[]{:S(2)}) async-start(), calls=%async_computation.21 | async-start | bytes 1310720 | tf_op jit(solution)/shard_map/reduce_scatter | solution.py:464
  543.0 161.2 %reduce-scatter.6.cloned.1.call-start = ((), (), s32[]{:S(2)}) async-start(), calls=%async_computation.20 | async-start | bytes 3932160 | tf_op jit(solution)/shard_map/reduce_scatter | solution.py:467
  569.9 40.5 %collective-permute-start.51 = (bf16[768,2048]{1,0:T(8,128)(2,1)}, bf16[768,2048]{1,0:T(8,128)(2,1)}, u32[]{:S(2)}, u32[]{:S(2)}) collective-permute-start(bf16[768,2048]{1,0:T(8,128)(2,1)} %convolution_convert_fusion.3), channel_id=1, source_target_pairs={{0,1},{1,0},{2,3},{3,2},{4,5},{5,4},{6,7},{7,6},{8,9},{9,8},{10,11... | collective-permute-start | bytes 9437192 | tf_op jit(solution)/shard_map/ppermute | solution.py:47
  573.6 14.2 %collective-permute-start.25 = (bf16[96,2048]{1,0:T(8,128)(2,1)}, bf16[96,2048]{1,0:T(8,128)(2,1)S(1)}, u32[]{:S(2)}, u32[]{:S(2)}) collective-permute-start(bf16[96,2048]{1,0:T(8,128)(2,1)} %get-tuple-element.128), channel_id=1, source_target_pairs={{0,4},{1,5},{2,6},{3,7},{4,0},{5,1},{6,2},{7,3},{8,12},{9,13},{10,... | collective-permute-start | bytes 1179656 | tf_op jit(solution)/shard_map/ppermute | solution.py:47
  575.1 26.6 %collective-permute-start.26 = (bf16[192,2048]{1,0:T(8,128)(2,1)}, bf16[192,2048]{1,0:T(8,128)(2,1)}, u32[]{:S(2)}, u32[]{:S(2)}) collective-permute-start(bf16[192,2048]{1,0:T(8,128)(2,1)} %pad_maximum_fusion.5), channel_id=1, source_target_pairs={{0,4},{1,5},{2,6},{3,7},{4,0},{5,1},{6,2},{7,3},{8,12},{9,13},{10,... | collective-permute-start | bytes 2359304 | tf_op jit(solution)/shard_map/ppermute | solution.py:47
  604.7 52.0 %collective-permute-start.27 = (bf16[96,2048]{1,0:T(8,128)(2,1)}, bf16[96,2048]{1,0:T(8,128)(2,1)S(1)}, u32[]{:S(2)}, u32[]{:S(2)}) collective-permute-start(bf16[96,2048]{1,0:T(8,128)(2,1)} %get-tuple-element.127), channel_id=1, source_target_pairs={{0,2},{1,3},{2,0},{3,1},{4,6},{5,7},{6,4},{7,5},{8,10},{9,11},{10,... | collective-permute-start | bytes 1179656 | tf_op jit(solution)/shard_map/ppermute | solution.py:47
  614.5 43.7 %collective-permute-start.52 = (bf16[192,2048]{1,0:T(8,128)(2,1)}, bf16[192,2048]{1,0:T(8,128)(2,1)}, u32[]{:S(2)}, u32[]{:S(2)}) collective-permute-start(bf16[192,2048]{1,0:T(8,128)(2,1)} %pad_maximum_fusion.8), channel_id=1, source_target_pairs={{0,2},{1,3},{2,0},{3,1},{4,6},{5,7},{6,4},{7,5},{8,10},{9,11},{10,... | collective-permute-start | bytes 2359304 | tf_op jit(solution)/shard_map/ppermute | solution.py:47
  661.4 26.7 %collective-permute-start.54 = (bf16[192,2048]{1,0:T(8,128)(2,1)}, bf16[192,2048]{1,0:T(8,128)(2,1)}, u32[]{:S(2)}, u32[]{:S(2)}) collective-permute-start(bf16[192,2048]{1,0:T(8,128)(2,1)} %pad_maximum_fusion.9), channel_id=1, source_target_pairs={{0,4},{1,5},{2,6},{3,7},{4,0},{5,1},{6,2},{7,3},{8,12},{9,13},{10,... | collective-permute-start | bytes 2359304 | tf_op jit(solution)/shard_map/ppermute | solution.py:47
  664.4 23.7 %collective-permute-start.53 = (bf16[96,2048]{1,0:T(8,128)(2,1)S(1)}, bf16[96,2048]{1,0:T(8,128)(2,1)}, u32[]{:S(2)}, u32[]{:S(2)}) collective-permute-start(bf16[96,2048]{1,0:T(8,128)(2,1)S(1)} %get-tuple-element.114), channel_id=1, source_target_pairs={{0,4},{1,5},{2,6},{3,7},{4,0},{5,1},{6,2},{7,3},{8,12},{9,13},{10,... | collective-permute-start | bytes 1179656 | tf_op jit(solution)/shard_map/ppermute | solution.py:47
  671.9 25.3 %all-to-all-start.7 = ((f32[8,1,64]{2,1,0:T(1,128)}), f32[8,1,64]{2,1,0:T(1,128)}, u32[]{:S(2)}, u32[]{:S(2)}) async-start(f32[8,1,64]{2,1,0:T(1,128)} %all_to_all.52), calls=%async_computation.11 | async-start | bytes 8192 | tf_op jit(solution)/shard_map/all_to_all | solution.py:481
  691.3 10.2 %collective-permute-start.55 = (bf16[96,2048]{1,0:T(8,128)(2,1)}, bf16[96,2048]{1,0:T(8,128)(2,1)S(1)}, u32[]{:S(2)}, u32[]{:S(2)}) collective-permute-start(bf16[96,2048]{1,0:T(8,128)(2,1)} %get-tuple-element.113), channel_id=1, source_target_pairs={{0,2},{1,3},{2,0},{3,1},{4,6},{5,7},{6,4},{7,5},{8,10},{9,11},{10,... | collective-permute-start | bytes 1179656 | tf_op jit(solution)/shard_map/ppermute | solution.py:47
  704.1 16.8 %all-to-all-start.5 = ((bf16[8,64,768]{2,1,0:T(8,128)(2,1)}), bf16[8,64,768]{2,1,0:T(8,128)(2,1)}, u32[]{:S(2)}, u32[]{:S(2)}) async-start(bf16[8,64,768]{2,1,0:T(8,128)(2,1)} %bitcast.108), calls=%async_computation.6 | async-start | bytes 1572864 | tf_op jit(solution)/shard_map/all_to_all | solution.py:470
  (56 other events, 998.3 us)
Sparse Core Ops, SparseCore 0:
  9.6 30.7 all-gather.14
  41.9 62.9 all-gather.6
  106.5 79.2 all-gather.10
  187.2 79.2 all-gather.8
  267.9 79.2 all-gather.12
  377.9 75.2 reduce-scatter.9
  455.5 77.2 reduce-scatter.11
  535.2 77.2 reduce-scatter.13
  614.8 27.7 reduce-scatter.7
  644.8 58.9 reduce-scatter.5

commit v2 on v1

--- a/solution.py
+++ b/solution.py
@@ -37,6 +37,11 @@
     scaled = grad * gain
     moment = jnp.mean(values * scaled, axis=-1, keepdims=True)
     return inverse * scaled - values * (inverse * inverse * inverse) * moment
+
+
+def gain_rows(values, grad):
+    inverse = lax.rsqrt(jnp.mean(values * values, axis=-1, keepdims=True) + EPSILON)
+    return jnp.sum(grad * values * inverse, axis=0)
 
 
 ORDER = (0, 2, 4, 6, 1, 3, 5, 7)
@@ -94,15 +99,35 @@
         rows = slice(chunk * local + low * half, chunk * local + (low + 1) * half)
         return add16(even[rows], theirs[rows])
 
-    send_x = jnp.concatenate([both(1, 0), both(3, 0)], axis=0)
-    send_y = jnp.concatenate([both(2, 1), both(3, 1)], axis=0)
-    from_x = swap(send_x, 2)
-    from_y = swap(send_y, 4)
-    last_y = swap(add16(both(2, 0), from_x[half:]), 4)
-    last_x = swap(add16(both(1, 1), from_y[half:]), 2)
+    send_x, send_y = lax.optimization_barrier(
+        (
+            jnp.concatenate([both(1, 0), both(3, 0)], axis=0),
+            jnp.concatenate([both(2, 1), both(3, 1)], axis=0),
+        )
+    )
+    from_x, from_y = lax.optimization_barrier((swap(send_x, 2), swap(send_y, 4)))
+    send_y, send_x = lax.optimization_barrier(
+        (add16(both(2, 0), from_x[half:]), add16(both(1, 1), from_y[half:]))
+    )
+    last_y, last_x = lax.optimization_barrier((swap(send_y, 4), swap(send_x, 2)))
     top = both(0, 0).astype(F32) + from_x[:half].astype(F32) + last_y.astype(F32)
     low = both(0, 1).astype(F32) + from_y[:half].astype(F32) + last_x.astype(F32)
     return jnp.concatenate([top, low], axis=0)
+
+
+def after(values, *others):
+    return lax.optimization_barrier((values,) + tuple(others))[0]
+
+
+def exchange(values):
+    size = lax.axis_size("kv")
+    if size != 8:
+        return lax.all_to_all(values, "kv", 0, 0)
+    index = lax.axis_index("kv").astype(jnp.int32)
+    relative = index ^ jnp.arange(size, dtype=jnp.int32)
+    ordered = values[relative]
+    moved = jnp.stack([ordered[0]] + [swap(ordered[m], m) for m in range(1, size)])
+    return moved[relative]
 
 
 def spread_small(values, axis):
@@ -355,17 +380,17 @@
     flat = flat16.astype(F32)
     dy16 = cotangent.reshape(local, width)
 
-    gate_w = lax.all_gather(w_gate, "seq", axis=0, tiled=True)
     w_three = jnp.stack([w_query, w_key, w_value])
     w_three = w_three.reshape(3, piece, share, mine, planes, HEAD_DIM)
     w_three = w_three.transpose(4, 2, 1, 0, 3, 5).reshape(group, piece, 3 * wide)
-    w_three = lax.all_to_all(w_three, "kv", 0, 0).reshape(group * piece, 3 * wide)
+    w_three = exchange(w_three).reshape(group * piece, 3 * wide)
     w_three = lax.all_gather(w_three, "seq", axis=0, tiled=True)
     out_w = lax.all_gather(w_out, "seq", axis=0, tiled=False)
     out_w = lax.all_to_all(
         out_w.reshape(share, mine, piece, width), "kv", 0, 0, axis_index_groups=pairs
     )
     out_w = out_w.transpose(1, 0, 2, 3).reshape(wide, width)
+    gate_w = lax.all_gather(w_gate, "seq", axis=0, tiled=True)
     up_w = lax.all_gather(w_up, "seq", axis=0, tiled=True)
     down_w = lax.all_gather(w_down, "seq", axis=1, tiled=True)
 
@@ -398,8 +423,12 @@
     cosine = jnp.concatenate([cosine, cosine], axis=1)
     sine = jnp.concatenate([-sine, sine], axis=1)
 
-    all_tokens = gather_rows(flat16)
+    token_chunks = gather_chunks(flat16)
+    all_tokens = jnp.concatenate(token_chunks, axis=0)
+    dy_chunks = gather_chunks(after(dy16, *token_chunks[-2:]))
+    dy_all = jnp.concatenate(dy_chunks, axis=0)
     normed = rms_norm(all_tokens.astype(F32), gains[0]).astype(BF16)
+    normed = after(normed, *dy_chunks[-4:])
     qk = dot_plain(normed, w_three[:, : 2 * wide])
     v = dot_plain(normed, w_three[:, 2 * wide :]).astype(BF16)
     q, k, v, mass, mixed = attend_forward(source, first, qk, v, cosine, sine, doc_col, doc_row)
@@ -408,47 +437,52 @@
         return dot_plain(chunk_rows(mixed, start, stop), out_w).astype(BF16)
 
     hidden = flat + scatter_rows(partial_hidden)
-    masses = lax.all_to_all(mass.reshape(group, local), "kv", 0, 0)
-    peak = jnp.max(jnp.sum(masses, axis=0)).reshape(1)
-    peak = jnp.max(spread_small(peak, "kv")).reshape(1)
-    summary = jnp.max(spread_small(peak, "seq")).reshape(1)
 
     second16 = rms_norm(hidden, gains[1]).astype(BF16)
-    dy_all = gather_rows(dy16)
-    second_all = gather_rows(second16)
+    masses = lax.all_to_all(after(mass, second16).reshape(group, local), "kv", 0, 0)
+    peak = jnp.max(jnp.sum(masses, axis=0)).reshape(1, 1)
+    everyone = jnp.broadcast_to(peak, (ring * group, 1))
+    summary = jnp.max(lax.all_to_all(everyone, ("seq", "kv"), 0, 0)).reshape(1)
+    second_all = after(gather_rows(second16), summary)
     gate = dot_plain(second_all, gate_w)
     up = dot_plain(second_all, up_w)
-    gate_sigmoid = jax.nn.sigmoid(gate)
-    swish = gate * gate_sigmoid
-    inner = (swish * up).astype(BF16)
+    sig = jax.nn.sigmoid(gate)
+    inner = (gate * sig * up).astype(BF16)
     grad_down = dot_left(dy_all, inner).astype(BF16)
     grads_down = lax.psum_scatter(grad_down, "seq", scatter_dimension=0, tiled=True)
-    grad_inner = dot_right(dy_all, down_w)
-    dgate = (grad_inner * up * (gate_sigmoid * (1.0 + gate * (1.0 - gate_sigmoid)))).astype(BF16)
-    dup = (grad_inner * swish).astype(BF16)
+    dinner = dot_right(after(dy_all, grad_down), down_w)
+    dgate = (dinner * up * (sig * (1.0 + gate * (1.0 - sig)))).astype(BF16)
+    dup = (dinner * (gate * sig)).astype(BF16)
+    partials = []
 
     def partial_second(start, stop):
-        return (
-            dot_right(chunk_rows(dgate, start, stop), gate_w)
-            + dot_right(chunk_rows(dup, start, stop), up_w)
-        ).astype(BF16)
+        partials.append(
+            (
+                dot_right(chunk_rows(dgate, start, stop), gate_w)
+                + dot_right(chunk_rows(dup, start, stop), up_w)
+            ).astype(BF16)
+        )
+        return partials[-1]
 
     grad_second = scatter_rows(partial_second)
+    second_later = after(second_all, *partials)
     grads_gate = lax.psum_scatter(
-        dot_left(second_all, dgate).astype(BF16), "seq", scatter_dimension=0, tiled=True
-    ).astype(F32)
+        dot_left(second_later, dgate).astype(BF16), "seq", scatter_dimension=0, tiled=True
+    )
     grads_up = lax.psum_scatter(
-        dot_left(second_all, dup).astype(BF16), "seq", scatter_dimension=0, tiled=True
-    ).astype(F32)
+        dot_left(second_later, dup).astype(BF16), "seq", scatter_dimension=0, tiled=True
+    )
+
+    grad_hidden = dy16.astype(F32) + rms_back(hidden, gains[1], grad_second)
+    dh_chunks = gather_chunks(after(grad_hidden.astype(BF16), grads_down))
     grads_down = grads_down.astype(F32).T
+    dh_all = jnp.concatenate(dh_chunks, axis=0)
 
     def partial_result(start, stop):
-        return dot_plain(chunk_rows(inner, start, stop), down_w).astype(BF16)
+        product = dot_plain(after(chunk_rows(inner, start, stop), *partials), down_w)
+        return after(product.astype(BF16), *dh_chunks[-2:])
 
     result = hidden + scatter_rows(partial_result)
-
-    grad_hidden = dy16.astype(F32) + rms_back(hidden, gains[1], grad_second)
-    dh_all = gather_rows(grad_hidden.astype(BF16))
     dmixed = dot_right(dh_all, out_w).astype(BF16)
     grad_w_out = dot_left(mixed, dh_all).astype(BF16)
     dqkv = attend_backward(source, last, q, k, v, dmixed, cosine, sine, doc_col, doc_row)
@@ -458,28 +492,22 @@
 
     grad_normed = scatter_rows(partial_normed)
     grad_input = grad_hidden + rms_back(flat, gains[0], grad_normed)
+    grads_gate, grads_up = after((grads_gate, grads_up), grad_input, result)
 
     grad_w_out = grad_w_out.reshape(mine, share, piece, width).transpose(1, 0, 2, 3)
     grad_w_out = lax.all_to_all(grad_w_out, "kv", 0, 0, axis_index_groups=pairs)
-    grad_w_out = lax.psum_scatter(
-        grad_w_out.reshape(ring * piece, width), "seq", scatter_dimension=0, tiled=True
-    ).astype(F32)
-    grad_three = lax.psum_scatter(
-        dot_left(normed, dqkv).astype(BF16), "seq", scatter_dimension=0, tiled=True
-    )
+    grad_w_out = grad_w_out.reshape(ring * group * piece, width // group)
+    grad_four = jnp.concatenate([dot_left(normed, dqkv).astype(BF16), grad_w_out], axis=1)
+    grad_four = lax.psum_scatter(grad_four, "seq", scatter_dimension=0, tiled=True)
+    grad_w_out = grad_four[:, 3 * wide :].reshape(piece, width).astype(F32)
+    grad_three = grad_four[:, : 3 * wide]
     grad_three = lax.all_to_all(grad_three.reshape(group, piece, 3 * wide), "kv", 0, 0)
     grad_three = grad_three.reshape(planes, share, piece, 3, mine, HEAD_DIM)
     grad_three = grad_three.transpose(3, 2, 1, 4, 0, 5).reshape(3, piece, width).astype(F32)
 
-    grad_gain1 = jnp.sum(
-        w_query.astype(F32) * grad_three[0]
-        + w_key.astype(F32) * grad_three[1]
-        + w_value.astype(F32) * grad_three[2],
-        axis=1,
-    ) / gain_attn.astype(F32)
-    part2 = jnp.sum(w_gate.astype(F32) * grads_gate + w_up.astype(F32) * grads_up, axis=1)
-    part2 = lax.all_to_all(part2.reshape(group, -1), "kv", 0, 0)
-    grad_gain2 = jnp.sum(part2, axis=0) / gain_ffn.astype(F32)
+    scales = jnp.stack([gain_rows(flat, grad_normed), gain_rows(hidden, grad_second)], axis=1)
+    scales = lax.all_to_all(scales.reshape(ring * group, piece, 2), ("seq", "kv"), 0, 0)
+    scales = jnp.sum(scales, axis=0)
 
     return (
         result.reshape(seqs, local, width).astype(BF16),
@@ -488,10 +516,10 @@
         grad_three[1],
         grad_three[2],
         grad_w_out,
-        grad_gain1,
-        grad_gain2,
-        grads_gate,
-        grads_up,
+        scales[:, 0],
+        scales[:, 1],
+        grads_gate.astype(F32),
+        grads_up.astype(F32),
         grads_down,
         summary,
     )

time: 746 us -> 716 us (0.960)
  blocking collectives: 55.7 us -> 5.55 us
  starting transfers between devices: 60.2 us -> 78.1 us
  local copies, waits for them, and re-layouts: 73.5 us -> 89 us
  waiting for transfers between devices: 264 us -> 256 us
    all_to_all x5 -> x1, blocking collectives: 55.7 us -> 5.55 us  [per_device(): grad_w_out = lax.all_to_all(grad_w_out, 'kv', 0, 0, axis_index_groups=pairs)]
    ppermute x56 -> x63, waiting for transfers between devices: 177 us -> 127 us  [swap(): return lax.ppermute(values, 'kv', [(i, i ^ mask) for i in range(size)])]
    reduce_scatter x4 -> x3, waiting for transfers between devices: 0.02 us -> 41.1 us  [the longest x1 41.1 us: per_device(): lax.psum_scatter(dot_left(second_later, dgate).astype(BF16), 'seq', scatt...]
    convert_element_type x1 -> x5, other arithmetic: 1.85 us -> 15.3 us  [the longest x1 7.15 us: per_device(): normed = rms_norm(all_tokens.astype(F32), gains[0]).astype(BF16)]
    all_to_all x2 -> x4, waiting for transfers between devices: 0.01 us -> 11.5 us  [the longest x1 5.79 us: per_device(): lax.all_to_all(after(mass, second16).reshape(group, local), 'kv', 0, 0)]
    ppermute x56 -> x63, starting transfers between devices: 35.1 us -> 45.3 us  [swap(): return lax.ppermute(values, 'kv', [(i, i ^ mask) for i in range(size)])]
    slice x0 -> x5, local copies, waits for them, and re-layouts: none -> 8.97 us  [the longest x2 4.45 us: per_device(): grad_three = grad_four[:, :3 * wide]]
    reduce_sum x6 -> x4, other arithmetic: 10.5 us -> 1.89 us  [the longest x2 1.82 us: gain_rows(): return jnp.sum(grad * values * inverse, axis=0)]
  transfers between devices with their start and end apart: 72 -> 80, of which waited for: 27 -> 35; matrix products, arithmetic and copies ran while one was open for 35% -> 42% of each run, Pallas kernels for 5% -> 5%
where the time goes in v2:
time: 716 us; the launch traced here: 708 us
  waiting for transfers between devices  256 us (36%)
  matrix products  151 us (21%)
  local copies, waits for them, and re-layouts  89 us (12%)
  starting transfers between devices  78.1 us (11%)
  other arithmetic  77.7 us (11%)
  Pallas kernels  34.6 us (5%)
  between operations  15.4 us (2%)
    ppermute x63, waiting for transfers between devices, swap(): return lax.ppermute(values, 'kv', [(i, i ^ mask) for i in range(size)])  127 us
    dot_general x8, matrix products, dot_plain(): return jnp.dot(left, right, preferred_element_type=F32)  56.5 us
    all_gather x1, waiting for transfers between devices, per_device(): down_w = lax.all_gather(w_down, 'seq', axis=1, tiled=True)  54.7 us
    dot_general x8, matrix products, dot_right(): lax.dot_general(left, right, (((1,), (1,)), ((), ())), preferred_element_...  53 us
    ppermute x63, starting transfers between devices, swap(): return lax.ppermute(values, 'kv', [(i, i ^ mask) for i in range(size)])  45.3 us
    unnamed x167, local copies, waits for them, and re-layouts  43.9 us
    dot_general x5, matrix products, dot_left(): lax.dot_general(left, right, (((0,), (0,)), ((), ())), preferred_element_...  41.7 us
    reduce_scatter x1, waiting for transfers between devices, per_device(): lax.psum_scatter(dot_left(second_later, dgate).astype(BF16), 'seq', scatt...  41.1 us
  transfers between devices with their start and end apart: 80, of which 35 were waited for; matrix products, arithmetic and copies ran while one was open for 42% of the time, Pallas kernels for 5%

profile of v2, /device:TPU:0, one launch (start us, length us, event | category | flops | bytes accessed | tf_op | source)
XLA Modules:
  0.0 707.8 jit_solution(6907139558383826013)
XLA Ops:
  14.1 2.6 collective-permute-start.18
  18.6 2.7 collective-permute-start.22
  22.1 5.7 collective-permute-done.21
  33.7 3.3 all-to-all-start.1
  39.4 2.9 fusion.31
  44.0 7.3 %all-to-all-done.1 = bf16[8,2,64]{2,1,0:T(2,128)(2,1)S(1)} async-done(((bf16[8,2,64]{2,1,0:T(2,128)(2,1)}), bf16[8,2,64]{2,1,0:T(2,128)(2,1)S(1)}, u32[]{:S(2)}, u32[]{:S(2)}) %all-to-all-start.1) | async-done | bytes 2080 | tf_op jit(solution)/shard_map/all_to_all | solution.py:135
  51.9 3.3 all-to-all-start
  56.6 3.4 all-to-all-done
  59.9 5.0 all-to-all-start.2
  74.8 5.8 collective-permute-done.2
  91.0 13.9 %collective-permute-done.9 = bf16[192,2048]{1,0:T(8,128)(2,1)S(1)} collective-permute-done((bf16[192,2048]{1,0:T(8,128)(2,1)S(1)}, bf16[192,2048]{1,0:T(8,128)(2,1)S(1)}, u32[]{:S(2)}, u32[]{:S(2)}) %collective-permute-start.9) | collective-permute-done | bytes 786464 | tf_op jit(solution)/shard_map/ppermute | solution.py:52
  108.8 4.1 fusion
  112.9 3.6 all-to-all-start.3
  118.0 7.2 %fusion.2 = bf16[1536,2048]{1,0:T(8,128)(2,1)} fusion(bf16[1536,2048]{1,0:T(8,128)(2,1)} %constant_dynamic-update-slice_fusion, f32[2048]{0:T(1024)S(1)} %mul.298, f32[1536]{0:T(1024)S(1)} %add_rsqrt_fusion), kind=kLoop, calls=%fused_computation.7 | loop fusion | flops 12582912 | bytes 12597248 | tf_op jit(solution)/shard_map/convert_element_type | solution.py:430
  127.5 6.1 convolution_convert_fusion.12.v_hbm
  133.7 7.9 %fusion.4.qk_hbm = f32[1536,512]{1,0:T(8,128)} fusion(bf16[1536,2048]{1,0:T(8,128)(2,1)} %fusion.2, bf16[2048,768]{1,0:T(8,128)(2,1)S(1)} %copy-done.50), kind=kOutput, calls=%fused_computation.33 | convolution fusion | flops 3221225472 | bytes 11534336 | tf_op jit(solution)/shard_map/dot_general | solution.py:20
  141.6 16.3 %attend_forward.1 = (bf16[1536,256]{1,0:T(8,128)(2,1)}, bf16[1536,256]{1,0:T(8,128)(2,1)}, bf16[1536,256]{1,0:T(8,128)(2,1)}, f32[1536,1]{1,0:T(8,128)}, bf16[1536,256]{1,0:T(8,128)(2,1)}) custom-call(s32[16]{0:T(128)} %pad_add_fusion.1.source, s32[6]{0:T(128)} %and_select_fusion.1.first, f32[1536,512]{1,0:T(8,128)} %fusion.4.qk_hbm, ...), custom_call_target="tpu_custom_call" | custom-call | flops 1207959552 | bytes 7077888 | tf_op jit(solution)/shard_map/attend_forward/pallas_call | solution.py:228
  158.0 3.8 convolution_convert_fusion.7
  163.4 4.5 collective-permute-done.24
  176.7 13.2 %collective-permute-done.25 = bf16[192,2048]{1,0:T(8,128)(2,1)S(1)} collective-permute-done((bf16[192,2048]{1,0:T(8,128)(2,1)S(1)}, bf16[192,2048]{1,0:T(8,128)(2,1)S(1)}, u32[]{:S(2)}, u32[]{:S(2)}) %collective-permute-start.25) | collective-permute-done | bytes 786464 | tf_op jit(solution)/shard_map/ppermute | solution.py:52
  197.5 5.0 collective-permute-done.27
  215.1 3.3 all-to-all-start.4
  220.2 5.8 all-to-all-done.4
  227.9 4.9 all-to-all-start.5
  234.8 5.7 all-to-all-done.5
  247.2 5.9 collective-permute-done.31
  260.9 12.0 %fusion.36 = f32[1536,1024]{1,0:T(8,128)} fusion(bf16[1536,2048]{1,0:T(8,128)(2,1)} %constant_dynamic-update-slice_fusion.17, bf16[2048,1024]{1,0:T(8,128)(2,1)} %all-gather.9.cloned.1.call-done), kind=kOutput, calls=%fused_computation.231 | convolution fusion | flops 6442450944 | bytes 16777216 | tf_op jit(solution)/shard_map/dot_general | solution.py:20
  275.2 12.9 %multiply_convert_fusion.2 = (bf16[1536,1024]{1,0:T(8,128)(2,1)S(1)}, f32[1536,1024]{1,0:T(8,128)}) fusion(f32[1536,1024]{1,0:T(8,128)} %fusion.36, bf16[1536,2048]{1,0:T(8,128)(2,1)} %constant_dynamic-update-slice_fusion.17, bf16[2048,1024]{1,0:T(8,128)(2,1)} %all-gather.11.cloned.1.call-done), kind=kOutput, calls=%fused_computation.12 | convolution fusion | flops 6451888128 | bytes 26214400 | tf_op jit(solution)/shard_map/dot_general | solution.py:20
  289.8 11.3 %convolution_convert_fusion.2 = bf16[2048,1024]{1,0:T(8,128)(2,1)} fusion(bf16[1536,2048]{1,0:T(8,128)(2,1)} %constant_dynamic-update-slice_fusion.27, bf16[1536,1024]{1,0:T(8,128)(2,1)S(1)} %get-tuple-element.255), kind=kOutput, calls=%fused_computation.18 | convolution fusion | flops 6444548096 | bytes 13631488 | tf_op jit(solution)/shard_map/dot_general | solution.py:24
  301.2 54.7 %all-gather.13.cloned.1.call-done = bf16[1024,2048]{1,0:T(8,128)(2,1)} async-done(((bf16[1024,512]{1,0:T(8,128)(2,1)}), bf16[1024,2048]{1,0:T(8,128)(2,1)}) %all-gather.13.cloned.1.call-update) | async-done | bytes 4194320 | tf_op jit(solution)/shard_map/all_gather | solution.py:395
  355.9 17.4 %multiply_convert_fusion = (bf16[1536,1024]{1,0:T(8,128)(2,1)}, bf16[1536,1024]{1,0:T(8,128)(2,1)S(1)}) fusion(f32[1536,1024]{1,0:T(8,128)} %fusion.36, f32[1536,1024]{1,0:T(8,128)} %get-tuple-element.256, bf16[1536,2048]{1,0:T(8,128)(2,1)} %constant_dynamic-update-slice_fusion.27, bf16[1024,2048]{1,0:T(8,128)(2,1)} %all-gather.13.cloned.1.call-done), kind=kOutput, calls=%fused_computation.10 | convolution fusion | flops 6462898176 | bytes 29360128 | tf_op jit(solution)/shard_map/dot_general | solution.py:28
  375.0 5.3 fusion.14
  380.3 5.0 fusion.17
  385.4 8.0 %add_convert_fusion = bf16[768,2048]{1,0:T(8,128)(2,1)} fusion(f32[768,2048]{1,0:T(8,128)} %fusion.14, bf16[2048,1024]{1,0:T(8,128)(2,1)S(1)} %copy-done.48, bf16[1536,1024]{1,0:T(8,128)(2,1)} %get-tuple-element.197), kind=kOutput, calls=%fused_computation.8 | convolution fusion | flops 3224371200 | bytes 15204352 | tf_op jit(solution)/shard_map/dot_general | solution.py:28
  393.3 4.9 add_convert_fusion.1
  398.2 8.6 %convolution_convert_fusion = bf16[2048,1024]{1,0:T(8,128)(2,1)} fusion(bf16[1536,2048]{1,0:T(8,128)(2,1)S(1)} %bitcast.152, bf16[1536,1024]{1,0:T(8,128)(2,1)S(1)} %copy-done.57), kind=kOutput, calls=%fused_computation.16 | convolution fusion | flops 6444548096 | bytes 13631488 | tf_op jit(solution)/shard_map/dot_general | solution.py:24
  406.9 5.9 collective-permute-done.39
  412.8 3.1 add_convert_fusion.29
  418.6 17.0 %collective-permute-done.40 = bf16[192,2048]{1,0:T(8,128)(2,1)S(1)} collective-permute-done((bf16[192,2048]{1,0:T(8,128)(2,1)S(1)}, bf16[192,2048]{1,0:T(8,128)(2,1)S(1)}, u32[]{:S(2)}, u32[]{:S(2)}) %collective-permute-start.40) | collective-permute-done | bytes 786464 | tf_op jit(solution)/shard_map/ppermute | solution.py:52
  440.4 12.0 %convolution_convert_fusion.1 = bf16[2048,1024]{1,0:T(8,128)(2,1)} fusion(bf16[1536,2048]{1,0:T(8,128)(2,1)} %constant_dynamic-update-slice_fusion.17, bf16[1536,1024]{1,0:T(8,128)(2,1)S(1)} %copy-done.56), kind=kOutput, calls=%fused_computation.17 | convolution fusion | flops 6444548096 | bytes 13631488 | tf_op jit(solution)/shard_map/dot_general | solution.py:24
  459.4 3.8 fusion.33
  463.3 11.8 %collective-permute-done.44 = bf16[192,2048]{1,0:T(8,128)(2,1)S(1)} collective-permute-done((bf16[192,2048]{1,0:T(8,128)(2,1)}, bf16[192,2048]{1,0:T(8,128)(2,1)S(1)}, u32[]{:S(2)}, u32[]{:S(2)}) %collective-permute-start.44) | collective-permute-done | bytes 786464 | tf_op jit(solution)/shard_map/ppermute | solution.py:52
  478.5 6.0 collective-permute-done.45
  486.8 2.9 convolution_convert_fusion.11.g_hbm
  489.7 18.3 %attend_backward.1 = bf16[1536,768]{1,0:T(8,128)(2,1)} custom-call(s32[16]{0:T(128)} %pad_add_fusion.1.source, s32[6]{0:T(128)} %and_select_fusion.last, bf16[1536,256]{1,0:T(8,128)(2,1)} %get-tuple-element.98.q_ref, bf16[1536,256]{1,0:T(8,128)(2,1)} %get-tuple-element.99.k_ref, bf16[1536,256]{1,0:T(8,128)(2,1)} %get-tuple-element.100.v_ref, ...), custom_call_target="tpu_custom_call" | custom-call | flops 3019898880 | bytes 5505024 | tf_op jit(solution)/shard_map/attend_backward/pallas_call | solution.py:328
  508.0 6.7 convolution_convert_fusion.3
  516.7 5.6 all_to_all.55
  526.9 8.0 %convolution_convert_fusion.9 = bf16[2048,768]{0,1:T(8,128)(2,1)S(1)} fusion(bf16[1536,2048]{1,0:T(8,128)(2,1)} %fusion.2, bf16[1536,768]{1,0:T(8,128)(2,1)} %attend_backward.1), kind=kOutput, calls=%fused_computation.25 | convolution fusion | flops 4833411072 | bytes 11796480 | tf_op jit(solution)/shard_map/dot_general | solution.py:24
  537.3 7.9 %convolution_convert_fusion.5 = bf16[768,2048]{1,0:T(8,128)(2,1)} fusion(bf16[768,1024]{1,0:T(8,128)(2,1)} %get-tuple-element.88, bf16[1024,2048]{1,0:T(8,128)(2,1)} %all-gather.13.cloned.1.call-done), kind=kOutput, calls=%fused_computation.21 | convolution fusion | flops 3222798336 | bytes 8912896 | tf_op jit(solution)/shard_map/dot_general | solution.py:20
  545.4 4.8 convolution_convert_fusion.6
  551.5 41.1 %reduce-scatter.9.cloned.1.call-done = bf16[512,1024]{1,0:T(8,128)(2,1)} async-done(((bf16[2048,1024]{1,0:T(8,128)(2,1)}), bf16[512,1024]{1,0:T(8,128)(2,1)}) %reduce-scatter.9.cloned.1.call-update) | async-done | bytes 1048592 | tf_op jit(solution)/shard_map/reduce_scatter | solution.py:469
  592.6 2.9 convert_element_type.732
  595.5 2.8 convert_element_type.733
  598.3 2.9 convolution_convert_fusion.4
  601.2 3.1 add_convert_fusion.9
  615.8 3.1 copy.102
  618.9 8.2 %collective-permute-done.59 = bf16[192,2048]{1,0:T(8,128)(2,1)} collective-permute-done((bf16[192,2048]{1,0:T(8,128)(2,1)}, bf16[192,2048]{1,0:T(8,128)(2,1)}, u32[]{:S(2)}, u32[]{:S(2)}) %collective-permute-start.59) | collective-permute-done | bytes 786464 | tf_op jit(solution)/shard_map/ppermute | solution.py:52
  632.6 11.3 %collective-permute-done.51 = bf16[192,2048]{1,0:T(8,128)(2,1)} collective-permute-done((bf16[192,2048]{1,0:T(8,128)(2,1)}, bf16[192,2048]{1,0:T(8,128)(2,1)}, u32[]{:S(2)}, u32[]{:S(2)}) %collective-permute-start.51) | collective-permute-done | bytes 786464 | tf_op jit(solution)/shard_map/ppermute | solution.py:52
  645.4 2.9 add_convert_fusion.14
  650.3 3.4 collective-permute-done.61
  662.1 4.3 all-to-all-start.8
  667.4 3.4 add_bitcast_fusion.1
  677.6 4.2 all-to-all-start.7
  688.9 5.6 all-to-all-done.7
  (420 shorter events, 186.2 us)
Async XLA Ops:
  7.2 105.7 %all-gather.15.cloned.1.call-start = ((), (), s32[]{:S(2)}) async-start(), calls=%async_computation.21 | async-start | bytes 1310720 | tf_op jit(solution)/shard_map/all_gather | solution.py:388
  18.5 9.3 %collective-permute-start.21 = (bf16[64,768]{1,0:T(8,128)(2,1)S(1)}, bf16[64,768]{1,0:T(8,128)(2,1)S(1)}, u32[]{:S(2)}, u32[]{:S(2)}) collective-permute-start(bf16[64,768]{1,0:T(8,128)(2,1)S(1)} %get-tuple-element.238), channel_id=1, source_target_pairs={{0,5},{1,4},{2,7},{3,6},{4,1},{5,0},{6,3},{7,2},{8,13},{9,12},{10,... | collective-permute-start | bytes 294920 | tf_op jit(solution)/shard_map/ppermute | solution.py:52
  18.5 109.0 %all-gather.7.cloned.1.call-start = ((), (), s32[]{:S(2)}) async-start(), calls=%async_computation.13 | async-start | bytes 3932160 | tf_op jit(solution)/shard_map/all_gather | solution.py:387
  18.6 9.2 %collective-permute-start.22 = (bf16[64,768]{1,0:T(8,128)(2,1)S(1)}, bf16[64,768]{1,0:T(8,128)(2,1)S(1)}, u32[]{:S(2)}, u32[]{:S(2)}) collective-permute-start(bf16[64,768]{1,0:T(8,128)(2,1)S(1)} %get-tuple-element.237), channel_id=1, source_target_pairs={{0,6},{1,7},{2,4},{3,5},{4,2},{5,3},{6,0},{7,1},{8,14},{9,15},{10,... | collective-permute-start | bytes 294920 | tf_op jit(solution)/shard_map/ppermute | solution.py:52
  29.4 231.5 %all-gather.9.cloned.1.call-start = ((), (), s32[]{:S(2)}) async-start(), calls=%async_computation.14 | async-start | bytes 5242880 | tf_op jit(solution)/shard_map/all_gather | solution.py:393
  30.1 41.0 %collective-permute-start = (bf16[192,2048]{1,0:T(8,128)(2,1)S(1)}, bf16[192,2048]{1,0:T(8,128)(2,1)S(1)}, u32[]{:S(2)}, u32[]{:S(2)}) collective-permute-start(bf16[192,2048]{1,0:T(8,128)(2,1)S(1)} %bitcast.125), channel_id=1, source_target_pairs={{0,2},{1,3},{2,0},{3,1},{4,6},{5,7},{6,4},{7,5},{8,10},{9,11},{10,... | collective-permute-start | bytes 2359304 | tf_op jit(solution)/shard_map/ppermute | solution.py:52
  31.7 40.0 %collective-permute-start.1 = (bf16[192,2048]{1,0:T(8,128)(2,1)S(1)}, bf16[192,2048]{1,0:T(8,128)(2,1)S(1)}, u32[]{:S(2)}, u32[]{:S(2)}) collective-permute-start(bf16[192,2048]{1,0:T(8,128)(2,1)S(1)} %bitcast.126), channel_id=1, source_target_pairs={{0,4},{1,5},{2,6},{3,7},{4,0},{5,1},{6,2},{7,3},{8,12},{9,13},{10,... | collective-permute-start | bytes 2359304 | tf_op jit(solution)/shard_map/ppermute | solution.py:52
  33.1 49.6 %collective-permute-start.4 = (bf16[192,2048]{1,0:T(8,128)(2,1)S(1)}, bf16[192,2048]{1,0:T(8,128)(2,1)}, u32[]{:S(2)}, u32[]{:S(2)}) collective-permute-start(bf16[192,2048]{1,0:T(8,128)(2,1)S(1)} %bitcast.127), channel_id=1, source_target_pairs={{0,1},{1,0},{2,3},{3,2},{4,5},{5,4},{6,7},{7,6},{8,9},{9,8},{10,11... | collective-permute-start | bytes 2359304 | tf_op jit(solution)/shard_map/ppermute | solution.py:52
  33.7 17.6 %all-to-all-start.1 = ((bf16[8,2,64]{2,1,0:T(2,128)(2,1)}), bf16[8,2,64]{2,1,0:T(2,128)(2,1)S(1)}, u32[]{:S(2)}, u32[]{:S(2)}) async-start(bf16[8,2,64]{2,1,0:T(2,128)(2,1)} %broadcast_in_dim.9), calls=%async_computation.1 | async-start | bytes 8192 | tf_op jit(solution)/shard_map/all_to_all | solution.py:135
  37.1 238.2 %all-gather.11.cloned.1.call-start = ((), (), s32[]{:S(2)}) async-start(), calls=%async_computation.15 | async-start | bytes 5242880 | tf_op jit(solution)/shard_map/all_gather | solution.py:394
  51.9 8.0 %all-to-all-start = ((s32[8,1,192]{2,1,0:T(1,128)}), s32[8,1,192]{2,1,0:T(1,128)S(1)}, u32[]{:S(2)}, u32[]{:S(2)}) async-start(s32[8,1,192]{2,1,0:T(1,128)} %broadcast_in_dim.8), calls=%async_computation | async-start | bytes 16384 | tf_op jit(solution)/shard_map/all_to_all | solution.py:135
  59.9 10.9 %all-to-all-start.2 = ((bf16[4,2,512]{2,1,0:T(2,128)(2,1)}), bf16[4,2,512]{2,1,0:T(2,128)(2,1)S(1)}, u32[]{:S(2)}, u32[]{:S(2)}) async-start(bf16[4,2,512]{2,1,0:T(2,128)(2,1)} %reshape.411), calls=%async_computation.2 | async-start | bytes 16384 | tf_op jit(solution)/shard_map/all_to_all | solution.py:135
  71.1 9.5 %collective-permute-start.2 = (bf16[96,2048]{1,0:T(8,128)(2,1)S(1)}, bf16[96,2048]{1,0:T(8,128)(2,1)S(1)}, u32[]{:S(2)}, u32[]{:S(2)}) collective-permute-start(bf16[96,2048]{1,0:T(8,128)(2,1)S(1)} %slice.500), channel_id=1, source_target_pairs={{0,4},{1,5},{2,6},{3,7},{4,0},{5,1},{6,2},{7,3},{8,12},{9,13},{10,... | collective-permute-start | bytes 1179656 | tf_op jit(solution)/shard_map/ppermute | solution.py:52
  71.7 10.3 %collective-permute-start.3 = (bf16[96,2048]{1,0:T(8,128)(2,1)S(1)}, bf16[96,2048]{1,0:T(8,128)(2,1)S(1)}, u32[]{:S(2)}, u32[]{:S(2)}) collective-permute-start(bf16[96,2048]{1,0:T(8,128)(2,1)S(1)} %slice.501), channel_id=1, source_target_pairs={{0,2},{1,3},{2,0},{3,1},{4,6},{5,7},{6,4},{7,5},{8,10},{9,11},{10,... | collective-permute-start | bytes 1179656 | tf_op jit(solution)/shard_map/ppermute | solution.py:52
  72.4 15.0 %collective-permute-start.5 = (bf16[192,2048]{1,0:T(8,128)(2,1)S(1)}, bf16[192,2048]{1,0:T(8,128)(2,1)S(1)}, u32[]{:S(2)}, u32[]{:S(2)}) collective-permute-start(bf16[192,2048]{1,0:T(8,128)(2,1)S(1)} %collective-permute-done), channel_id=1, source_target_pairs={{0,1},{1,0},{2,3},{3,2},{4,5},{5,4},{6,7},{7,6},{8,9},{9,8},{10,11... | collective-permute-start | bytes 2359304 | tf_op jit(solution)/shard_map/ppermute | solution.py:52
  72.4 16.0 %collective-permute-start.6 = (bf16[192,2048]{1,0:T(8,128)(2,1)S(1)}, bf16[192,2048]{1,0:T(8,128)(2,1)S(1)}, u32[]{:S(2)}, u32[]{:S(2)}) collective-permute-start(bf16[192,2048]{1,0:T(8,128)(2,1)S(1)} %collective-permute-done.1), channel_id=1, source_target_pairs={{0,1},{1,0},{2,3},{3,2},{4,5},{5,4},{6,7},{7,6},{8,9},{9,8},{10,11... | collective-permute-start | bytes 2359304 | tf_op jit(solution)/shard_map/ppermute | solution.py:52
  84.8 20.0 %collective-permute-start.9 = (bf16[192,2048]{1,0:T(8,128)(2,1)S(1)}, bf16[192,2048]{1,0:T(8,128)(2,1)S(1)}, u32[]{:S(2)}, u32[]{:S(2)}) collective-permute-start(bf16[192,2048]{1,0:T(8,128)(2,1)S(1)} %bitcast.139), channel_id=1, source_target_pairs={{0,2},{1,3},{2,0},{3,1},{4,6},{5,7},{6,4},{7,5},{8,10},{9,11},{10,... | collective-permute-start | bytes 2359304 | tf_op jit(solution)/shard_map/ppermute | solution.py:52
  86.3 20.3 %collective-permute-start.11 = (bf16[192,2048]{1,0:T(8,128)(2,1)S(1)}, bf16[192,2048]{1,0:T(8,128)(2,1)S(1)}, u32[]{:S(2)}, u32[]{:S(2)}) collective-permute-start(bf16[192,2048]{1,0:T(8,128)(2,1)S(1)} %bitcast.140), channel_id=1, source_target_pairs={{0,4},{1,5},{2,6},{3,7},{4,0},{5,1},{6,2},{7,3},{8,12},{9,13},{10,... | collective-permute-start | bytes 2359304 | tf_op jit(solution)/shard_map/ppermute | solution.py:52
  105.7 11.5 %collective-permute-start.13 = (bf16[96,2048]{1,0:T(8,128)(2,1)}, bf16[96,2048]{1,0:T(8,128)(2,1)}, u32[]{:S(2)}, u32[]{:S(2)}) collective-permute-start(bf16[96,2048]{1,0:T(8,128)(2,1)} %slice.503), channel_id=1, source_target_pairs={{0,4},{1,5},{2,6},{3,7},{4,0},{5,1},{6,2},{7,3},{8,12},{9,13},{10,... | collective-permute-start | bytes 1179656 | tf_op jit(solution)/shard_map/ppermute | solution.py:52
  107.7 10.3 %collective-permute-start.15 = (bf16[96,2048]{1,0:T(8,128)(2,1)}, bf16[96,2048]{1,0:T(8,128)(2,1)}, u32[]{:S(2)}, u32[]{:S(2)}) collective-permute-start(bf16[96,2048]{1,0:T(8,128)(2,1)} %slice.504), channel_id=1, source_target_pairs={{0,2},{1,3},{2,0},{3,1},{4,6},{5,7},{6,4},{7,5},{8,10},{9,11},{10,... | collective-permute-start | bytes 1179656 | tf_op jit(solution)/shard_map/ppermute | solution.py:52
  112.9 12.3 %all-to-all-start.3 = ((bf16[2,2,64,2048]{3,2,1,0:T(8,128)(2,1)}), bf16[2,2,64,2048]{3,2,1,0:T(8,128)(2,1)S(1)}, u32[]{:S(2)}, u32[]{:S(2)}) async-start(bf16[2,2,64,2048]{3,2,1,0:T(8,128)(2,1)} %bitcast.149), calls=%async_computation.3 | async-start | bytes 2097152 | tf_op jit(solution)/shard_map/all_to_all | solution.py:389
  116.5 239.4 %all-gather.13.cloned.1.call-start = ((), (), s32[]{:S(2)}) async-start(), calls=%async_computation.16 | async-start | bytes 5242880 | tf_op jit(solution)/shard_map/all_gather | solution.py:395
  116.6 10.9 %collective-permute-start.10 = (bf16[192,2048]{1,0:T(8,128)(2,1)S(1)}, bf16[192,2048]{1,0:T(8,128)(2,1)}, u32[]{:S(2)}, u32[]{:S(2)}) collective-permute-start(bf16[192,2048]{1,0:T(8,128)(2,1)S(1)} %copy-done.26), channel_id=1, source_target_pairs={{0,1},{1,0},{2,3},{3,2},{4,5},{5,4},{6,7},{7,6},{8,9},{9,8},{10,11... | collective-permute-start | bytes 2359304 | tf_op jit(solution)/shard_map/ppermute | solution.py:52
  117.1 10.4 %collective-permute-start.12 = (bf16[192,2048]{1,0:T(8,128)(2,1)}, bf16[192,2048]{1,0:T(8,128)(2,1)}, u32[]{:S(2)}, u32[]{:S(2)}) collective-permute-start(bf16[192,2048]{1,0:T(8,128)(2,1)} %copy-done.28), channel_id=1, source_target_pairs={{0,1},{1,0},{2,3},{3,2},{4,5},{5,4},{6,7},{7,6},{8,9},{9,8},{10,11... | collective-permute-start | bytes 2359304 | tf_op jit(solution)/shard_map/ppermute | solution.py:52
  117.1 10.3 %collective-permute-start.14 = (bf16[96,2048]{1,0:T(8,128)(2,1)}, bf16[96,2048]{1,0:T(8,128)(2,1)}, u32[]{:S(2)}, u32[]{:S(2)}) collective-permute-start(bf16[96,2048]{1,0:T(8,128)(2,1)} %collective-permute-done.13), channel_id=1, source_target_pairs={{0,1},{1,0},{2,3},{3,2},{4,5},{5,4},{6,7},{7,6},{8,9},{9,8},{10,11... | collective-permute-start | bytes 1179656 | tf_op jit(solution)/shard_map/ppermute | solution.py:52
  118.0 9.5 %collective-permute-start.16 = (bf16[96,2048]{1,0:T(8,128)(2,1)}, bf16[96,2048]{1,0:T(8,128)(2,1)}, u32[]{:S(2)}, u32[]{:S(2)}) collective-permute-start(bf16[96,2048]{1,0:T(8,128)(2,1)} %collective-permute-done.15), channel_id=1, source_target_pairs={{0,1},{1,0},{2,3},{3,2},{4,5},{5,4},{6,7},{7,6},{8,9},{9,8},{10,11... | collective-permute-start | bytes 1179656 | tf_op jit(solution)/shard_map/ppermute | solution.py:52
  170.0 19.9 %collective-permute-start.25 = (bf16[192,2048]{1,0:T(8,128)(2,1)S(1)}, bf16[192,2048]{1,0:T(8,128)(2,1)S(1)}, u32[]{:S(2)}, u32[]{:S(2)}) collective-permute-start(bf16[192,2048]{1,0:T(8,128)(2,1)S(1)} %pad_maximum_fusion.5), channel_id=1, source_target_pairs={{0,2},{1,3},{2,0},{3,1},{4,6},{5,7},{6,4},{7,5},{8,10},{9,11},{10,... | collective-permute-start | bytes 2359304 | tf_op jit(solution)/shard_map/ppermute | solution.py:52
  171.0 19.5 %collective-permute-start.26 = (bf16[192,2048]{1,0:T(8,128)(2,1)S(1)}, bf16[192,2048]{1,0:T(8,128)(2,1)S(1)}, u32[]{:S(2)}, u32[]{:S(2)}) collective-permute-start(bf16[192,2048]{1,0:T(8,128)(2,1)S(1)} %pad_maximum_fusion.6), channel_id=1, source_target_pairs={{0,4},{1,5},{2,6},{3,7},{4,0},{5,1},{6,2},{7,3},{8,12},{9,13},{10,... | collective-permute-start | bytes 2359304 | tf_op jit(solution)/shard_map/ppermute | solution.py:52
  173.1 23.5 %collective-permute-start.38 = (bf16[192,2048]{1,0:T(8,128)(2,1)S(1)}, bf16[192,2048]{1,0:T(8,128)(2,1)S(1)}, u32[]{:S(2)}, u32[]{:S(2)}) collective-permute-start(bf16[192,2048]{1,0:T(8,128)(2,1)S(1)} %bitcast.142), channel_id=1, source_target_pairs={{0,1},{1,0},{2,3},{3,2},{4,5},{5,4},{6,7},{7,6},{8,9},{9,8},{10,11... | collective-permute-start | bytes 2359304 | tf_op jit(solution)/shard_map/ppermute | solution.py:52
  192.1 10.4 %collective-permute-start.27 = (bf16[96,2048]{1,0:T(8,128)(2,1)S(1)}, bf16[96,2048]{1,0:T(8,128)(2,1)S(1)}, u32[]{:S(2)}, u32[]{:S(2)}) collective-permute-start(bf16[96,2048]{1,0:T(8,128)(2,1)S(1)} %get-tuple-element.69), channel_id=1, source_target_pairs={{0,4},{1,5},{2,6},{3,7},{4,0},{5,1},{6,2},{7,3},{8,12},{9,13},{10,... | collective-permute-start | bytes 1179656 | tf_op jit(solution)/shard_map/ppermute | solution.py:52
  193.2 10.1 %collective-permute-start.28 = (bf16[96,2048]{1,0:T(8,128)(2,1)S(1)}, bf16[96,2048]{1,0:T(8,128)(2,1)S(1)}, u32[]{:S(2)}, u32[]{:S(2)}) collective-permute-start(bf16[96,2048]{1,0:T(8,128)(2,1)S(1)} %get-tuple-element.70), channel_id=1, source_target_pairs={{0,2},{1,3},{2,0},{3,1},{4,6},{5,7},{6,4},{7,5},{8,10},{9,11},{10,... | collective-permute-start | bytes 1179656 | tf_op jit(solution)/shard_map/ppermute | solution.py:52
  206.8 34.4 %collective-permute-start.29 = (bf16[192,2048]{1,0:T(8,128)(2,1)}, bf16[192,2048]{1,0:T(8,128)(2,1)}, u32[]{:S(2)}, u32[]{:S(2)}) collective-permute-start(bf16[192,2048]{1,0:T(8,128)(2,1)} %get-tuple-element.196), channel_id=1, source_target_pairs={{0,2},{1,3},{2,0},{3,1},{4,6},{5,7},{6,4},{7,5},{8,10},{9,11},{10,... | collective-permute-start | bytes 2359304 | tf_op jit(solution)/shard_map/ppermute | solution.py:52
  208.3 34.7 %collective-permute-start.30 = (bf16[192,2048]{1,0:T(8,128)(2,1)}, bf16[192,2048]{1,0:T(8,128)(2,1)S(1)}, u32[]{:S(2)}, u32[]{:S(2)}) collective-permute-start(bf16[192,2048]{1,0:T(8,128)(2,1)} %get-tuple-element.196), channel_id=1, source_target_pairs={{0,4},{1,5},{2,6},{3,7},{4,0},{5,1},{6,2},{7,3},{8,12},{9,13},{10,... | collective-permute-start | bytes 2359304 | tf_op jit(solution)/shard_map/ppermute | solution.py:52
  215.1 10.9 %all-to-all-start.4 = ((f32[8,1,192]{2,1,0:T(1,128)}), f32[8,1,192]{2,1,0:T(1,128)S(1)}, u32[]{:S(2)}, u32[]{:S(2)}) async-start(f32[8,1,192]{2,1,0:T(1,128)} %all_to_all.45), calls=%async_computation.4 | async-start | bytes 16384 | tf_op jit(solution)/shard_map/all_to_all | solution.py:442
  227.9 12.7 %all-to-all-start.5 = ((f32[32,1,1]{2,1,0:T(1,128)}), f32[32,1,1]{2,1,0:T(1,128)S(1)}, u32[]{:S(2)}, u32[]{:S(2)}) async-start(f32[32,1,1]{2,1,0:T(1,128)} %broadcast_in_dim.11), calls=%async_computation.5 | async-start | bytes 32768 | tf_op jit(solution)/shard_map/all_to_all | solution.py:445
  232.7 224.8 %reduce-scatter.5.cloned.1.call-start = ((), (), s32[]{:S(2)}) async-start(), calls=%async_computation.17 | async-start | bytes 5242880 | tf_op jit(solution)/shard_map/reduce_scatter | solution.py:452
  234.6 20.6 %collective-permute-start.33 = (bf16[192,2048]{1,0:T(8,128)(2,1)}, bf16[192,2048]{1,0:T(8,128)(2,1)}, u32[]{:S(2)}, u32[]{:S(2)}) collective-permute-start(bf16[192,2048]{1,0:T(8,128)(2,1)} %get-tuple-element.196), channel_id=1, source_target_pairs={{0,1},{1,0},{2,3},{3,2},{4,5},{5,4},{6,7},{7,6},{8,9},{9,8},{10,11... | collective-permute-start | bytes 2359304 | tf_op jit(solution)/shard_map/ppermute | solution.py:52
  242.2 10.9 %collective-permute-start.31 = (bf16[96,2048]{1,0:T(8,128)(2,1)S(1)}, bf16[96,2048]{1,0:T(8,128)(2,1)S(1)}, u32[]{:S(2)}, u32[]{:S(2)}) collective-permute-start(bf16[96,2048]{1,0:T(8,128)(2,1)S(1)} %slice.532), channel_id=1, source_target_pairs={{0,4},{1,5},{2,6},{3,7},{4,0},{5,1},{6,2},{7,3},{8,12},{9,13},{10,... | collective-permute-start | bytes 1179656 | tf_op jit(solution)/shard_map/ppermute | solution.py:52
  243.0 11.0 %collective-permute-start.32 = (bf16[96,2048]{1,0:T(8,128)(2,1)S(1)}, bf16[96,2048]{1,0:T(8,128)(2,1)S(1)}, u32[]{:S(2)}, u32[]{:S(2)}) collective-permute-start(bf16[96,2048]{1,0:T(8,128)(2,1)S(1)} %slice.533), channel_id=1, source_target_pairs={{0,2},{1,3},{2,0},{3,1},{4,6},{5,7},{6,4},{7,5},{8,10},{9,11},{10,... | collective-permute-start | bytes 1179656 | tf_op jit(solution)/shard_map/ppermute | solution.py:52
  243.6 13.7 %collective-permute-start.34 = (bf16[192,2048]{1,0:T(8,128)(2,1)}, bf16[192,2048]{1,0:T(8,128)(2,1)S(1)}, u32[]{:S(2)}, u32[]{:S(2)}) collective-permute-start(bf16[192,2048]{1,0:T(8,128)(2,1)} %collective-permute-done.29), channel_id=1, source_target_pairs={{0,1},{1,0},{2,3},{3,2},{4,5},{5,4},{6,7},{7,6},{8,9},{9,8},{10,11... | collective-permute-start | bytes 2359304 | tf_op jit(solution)/shard_map/ppermute | solution.py:52
  243.6 14.7 %collective-permute-start.35 = (bf16[192,2048]{1,0:T(8,128)(2,1)S(1)}, bf16[192,2048]{1,0:T(8,128)(2,1)S(1)}, u32[]{:S(2)}, u32[]{:S(2)}) collective-permute-start(bf16[192,2048]{1,0:T(8,128)(2,1)S(1)} %collective-permute-done.30), channel_id=1, source_target_pairs={{0,1},{1,0},{2,3},{3,2},{4,5},{5,4},{6,7},{7,6},{8,9},{9,8},{10,11... | collective-permute-start | bytes 2359304 | tf_op jit(solution)/shard_map/ppermute | solution.py:52
  301.1 250.4 %reduce-scatter.11.cloned.1.call-start = ((), (), s32[]{:S(2)}) async-start(), calls=%async_computation.20 | async-start | bytes 5242880 | tf_op jit(solution)/shard_map/reduce_scatter | solution.py:472
  406.8 185.8 %reduce-scatter.9.cloned.1.call-start = ((), (), s32[]{:S(2)}) async-start(), calls=%async_computation.19 | async-start | bytes 5242880 | tf_op jit(solution)/shard_map/reduce_scatter | solution.py:469
  416.0 19.6 %collective-permute-start.40 = (bf16[192,2048]{1,0:T(8,128)(2,1)S(1)}, bf16[192,2048]{1,0:T(8,128)(2,1)S(1)}, u32[]{:S(2)}, u32[]{:S(2)}) collective-permute-start(bf16[192,2048]{1,0:T(8,128)(2,1)S(1)} %pad_maximum_fusion.7), channel_id=1, source_target_pairs={{0,2},{1,3},{2,0},{3,1},{4,6},{5,7},{6,4},{7,5},{8,10},{9,11},{10,... | collective-permute-start | bytes 2359304 | tf_op jit(solution)/shard_map/ppermute | solution.py:52
  417.2 19.3 %collective-permute-start.41 = (bf16[192,2048]{1,0:T(8,128)(2,1)S(1)}, bf16[192,2048]{1,0:T(8,128)(2,1)S(1)}, u32[]{:S(2)}, u32[]{:S(2)}) collective-permute-start(bf16[192,2048]{1,0:T(8,128)(2,1)S(1)} %pad_maximum_fusion.8), channel_id=1, source_target_pairs={{0,4},{1,5},{2,6},{3,7},{4,0},{5,1},{6,2},{7,3},{8,12},{9,13},{10,... | collective-permute-start | bytes 2359304 | tf_op jit(solution)/shard_map/ppermute | solution.py:52
  438.3 14.6 %collective-permute-start.42 = (bf16[96,2048]{1,0:T(8,128)(2,1)S(1)}, bf16[96,2048]{1,0:T(8,128)(2,1)S(1)}, u32[]{:S(2)}, u32[]{:S(2)}) collective-permute-start(bf16[96,2048]{1,0:T(8,128)(2,1)S(1)} %get-tuple-element.82), channel_id=1, source_target_pairs={{0,4},{1,5},{2,6},{3,7},{4,0},{5,1},{6,2},{7,3},{8,12},{9,13},{10,... | collective-permute-start | bytes 1179656 | tf_op jit(solution)/shard_map/ppermute | solution.py:52
  439.8 13.1 %collective-permute-start.43 = (bf16[96,2048]{1,0:T(8,128)(2,1)S(1)}, bf16[96,2048]{1,0:T(8,128)(2,1)}, u32[]{:S(2)}, u32[]{:S(2)}) collective-permute-start(bf16[96,2048]{1,0:T(8,128)(2,1)S(1)} %get-tuple-element.83), channel_id=1, source_target_pairs={{0,2},{1,3},{2,0},{3,1},{4,6},{5,7},{6,4},{7,5},{8,10},{9,11},{10,... | collective-permute-start | bytes 1179656 | tf_op jit(solution)/shard_map/ppermute | solution.py:52
  452.4 220.8 %reduce-scatter.7.cloned.1.call-start = ((), (), s32[]{:S(2)}) async-start(), calls=%async_computation.18 | async-start | bytes 5242880 | tf_op jit(solution)/shard_map/reduce_scatter | solution.py:501
  457.5 17.6 %collective-permute-start.44 = (bf16[192,2048]{1,0:T(8,128)(2,1)}, bf16[192,2048]{1,0:T(8,128)(2,1)S(1)}, u32[]{:S(2)}, u32[]{:S(2)}) collective-permute-start(bf16[192,2048]{1,0:T(8,128)(2,1)} %add_convert_fusion.2), channel_id=1, source_target_pairs={{0,2},{1,3},{2,0},{3,1},{4,6},{5,7},{6,4},{7,5},{8,10},{9,11},{10,... | collective-permute-start | bytes 2359304 | tf_op jit(solution)/shard_map/ppermute | solution.py:52
  458.8 18.2 %collective-permute-start.47 = (bf16[192,2048]{1,0:T(8,128)(2,1)}, bf16[192,2048]{1,0:T(8,128)(2,1)S(1)}, u32[]{:S(2)}, u32[]{:S(2)}) collective-permute-start(bf16[192,2048]{1,0:T(8,128)(2,1)} %add_convert_fusion.2), channel_id=1, source_target_pairs={{0,4},{1,5},{2,6},{3,7},{4,0},{5,1},{6,2},{7,3},{8,12},{9,13},{10,... | collective-permute-start | bytes 2359304 | tf_op jit(solution)/shard_map/ppermute | solution.py:52
  463.2 21.9 %collective-permute-start.55 = (bf16[192,2048]{1,0:T(8,128)(2,1)S(1)}, bf16[192,2048]{1,0:T(8,128)(2,1)S(1)}, u32[]{:S(2)}, u32[]{:S(2)}) collective-permute-start(bf16[192,2048]{1,0:T(8,128)(2,1)S(1)} %copy-done.24), channel_id=1, source_target_pairs={{0,1},{1,0},{2,3},{3,2},{4,5},{5,4},{6,7},{7,6},{8,9},{9,8},{10,11... | collective-permute-start | bytes 2359304 | tf_op jit(solution)/shard_map/ppermute | solution.py:52
  475.2 9.3 %collective-permute-start.45 = (bf16[96,2048]{1,0:T(8,128)(2,1)S(1)}, bf16[96,2048]{1,0:T(8,128)(2,1)S(1)}, u32[]{:S(2)}, u32[]{:S(2)}) collective-permute-start(bf16[96,2048]{1,0:T(8,128)(2,1)S(1)} %slice.555), channel_id=1, source_target_pairs={{0,4},{1,5},{2,6},{3,7},{4,0},{5,1},{6,2},{7,3},{8,12},{9,13},{10,... | collective-permute-start | bytes 1179656 | tf_op jit(solution)/shard_map/ppermute | solution.py:52
  514.7 86.5 %collective-permute-start.58 = (bf16[768,2048]{1,0:T(8,128)(2,1)}, bf16[768,2048]{1,0:T(8,128)(2,1)}, u32[]{:S(2)}, u32[]{:S(2)}) collective-permute-start(bf16[768,2048]{1,0:T(8,128)(2,1)} %convolution_convert_fusion.3), channel_id=1, source_target_pairs={{0,1},{1,0},{2,3},{3,2},{4,5},{5,4},{6,7},{7,6},{8,9},{9,8},{10,11... | collective-permute-start | bytes 9437192 | tf_op jit(solution)/shard_map/ppermute | solution.py:52
  545.2 64.1 %collective-permute-start.50 = (bf16[768,2048]{1,0:T(8,128)(2,1)}, bf16[768,2048]{1,0:T(8,128)(2,1)}, u32[]{:S(2)}, u32[]{:S(2)}) collective-permute-start(bf16[768,2048]{1,0:T(8,128)(2,1)} %convolution_convert_fusion.5), channel_id=1, source_target_pairs={{0,1},{1,0},{2,3},{3,2},{4,5},{5,4},{6,7},{7,6},{8,9},{9,8},{10,11... | collective-permute-start | bytes 9437192 | tf_op jit(solution)/shard_map/ppermute | solution.py:52
  606.3 20.7 %collective-permute-start.59 = (bf16[192,2048]{1,0:T(8,128)(2,1)}, bf16[192,2048]{1,0:T(8,128)(2,1)}, u32[]{:S(2)}, u32[]{:S(2)}) collective-permute-start(bf16[192,2048]{1,0:T(8,128)(2,1)} %pad_maximum_fusion.11), channel_id=1, source_target_pairs={{0,2},{1,3},{2,0},{3,1},{4,6},{5,7},{6,4},{7,5},{8,10},{9,11},{10,... | collective-permute-start | bytes 2359304 | tf_op jit(solution)/shard_map/ppermute | solution.py:52
  607.8 20.7 %collective-permute-start.60 = (bf16[192,2048]{1,0:T(8,128)(2,1)}, bf16[192,2048]{1,0:T(8,128)(2,1)}, u32[]{:S(2)}, u32[]{:S(2)}) collective-permute-start(bf16[192,2048]{1,0:T(8,128)(2,1)} %pad_maximum_fusion.12), channel_id=1, source_target_pairs={{0,4},{1,5},{2,6},{3,7},{4,0},{5,1},{6,2},{7,3},{8,12},{9,13},{10,... | collective-permute-start | bytes 2359304 | tf_op jit(solution)/shard_map/ppermute | solution.py:52
  613.1 30.8 %collective-permute-start.51 = (bf16[192,2048]{1,0:T(8,128)(2,1)}, bf16[192,2048]{1,0:T(8,128)(2,1)}, u32[]{:S(2)}, u32[]{:S(2)}) collective-permute-start(bf16[192,2048]{1,0:T(8,128)(2,1)} %pad_maximum_fusion.9), channel_id=1, source_target_pairs={{0,2},{1,3},{2,0},{3,1},{4,6},{5,7},{6,4},{7,5},{8,10},{9,11},{10,... | collective-permute-start | bytes 2359304 | tf_op jit(solution)/shard_map/ppermute | solution.py:52
  613.7 31.7 %collective-permute-start.52 = (bf16[192,2048]{1,0:T(8,128)(2,1)}, bf16[192,2048]{1,0:T(8,128)(2,1)}, u32[]{:S(2)}, u32[]{:S(2)}) collective-permute-start(bf16[192,2048]{1,0:T(8,128)(2,1)} %pad_maximum_fusion.10), channel_id=1, source_target_pairs={{0,4},{1,5},{2,6},{3,7},{4,0},{5,1},{6,2},{7,3},{8,12},{9,13},{10,... | collective-permute-start | bytes 2359304 | tf_op jit(solution)/shard_map/ppermute | solution.py:52
  630.5 23.2 %collective-permute-start.61 = (bf16[96,2048]{1,0:T(8,128)(2,1)S(1)}, bf16[96,2048]{1,0:T(8,128)(2,1)S(1)}, u32[]{:S(2)}, u32[]{:S(2)}) collective-permute-start(bf16[96,2048]{1,0:T(8,128)(2,1)S(1)} %get-tuple-element.105), channel_id=1, source_target_pairs={{0,4},{1,5},{2,6},{3,7},{4,0},{5,1},{6,2},{7,3},{8,12},{9,13},{10,... | collective-permute-start | bytes 1179656 | tf_op jit(solution)/shard_map/ppermute | solution.py:52
  632.1 21.6 %collective-permute-start.62 = (bf16[96,2048]{1,0:T(8,128)(2,1)S(1)}, bf16[96,2048]{1,0:T(8,128)(2,1)S(1)}, u32[]{:S(2)}, u32[]{:S(2)}) collective-permute-start(bf16[96,2048]{1,0:T(8,128)(2,1)S(1)} %get-tuple-element.106), channel_id=1, source_target_pairs={{0,2},{1,3},{2,0},{3,1},{4,6},{5,7},{6,4},{7,5},{8,10},{9,11},{10,... | collective-permute-start | bytes 1179656 | tf_op jit(solution)/shard_map/ppermute | solution.py:52
  648.2 18.3 %collective-permute-start.53 = (bf16[96,2048]{1,0:T(8,128)(2,1)}, bf16[96,2048]{1,0:T(8,128)(2,1)S(1)}, u32[]{:S(2)}, u32[]{:S(2)}) collective-permute-start(bf16[96,2048]{1,0:T(8,128)(2,1)} %get-tuple-element.94), channel_id=1, source_target_pairs={{0,4},{1,5},{2,6},{3,7},{4,0},{5,1},{6,2},{7,3},{8,12},{9,13},{10,... | collective-permute-start | bytes 1179656 | tf_op jit(solution)/shard_map/ppermute | solution.py:52
  649.7 16.8 %collective-permute-start.54 = (bf16[96,2048]{1,0:T(8,128)(2,1)}, bf16[96,2048]{1,0:T(8,128)(2,1)}, u32[]{:S(2)}, u32[]{:S(2)}) collective-permute-start(bf16[96,2048]{1,0:T(8,128)(2,1)} %get-tuple-element.95), channel_id=1, source_target_pairs={{0,2},{1,3},{2,0},{3,1},{4,6},{5,7},{6,4},{7,5},{8,10},{9,11},{10,... | collective-permute-start | bytes 1179656 | tf_op jit(solution)/shard_map/ppermute | solution.py:52
  662.1 15.5 %all-to-all-start.8 = ((f32[32,1,128]{2,1,0:T(1,128)}), f32[32,1,128]{2,1,0:T(1,128)}, u32[]{:S(2)}, u32[]{:S(2)}) async-start(f32[32,1,128]{2,1,0:T(1,128)} %reshape.413), calls=%async_computation.10 | async-start | bytes 32768 | tf_op jit(solution)/shard_map/all_to_all | solution.py:509
  677.6 16.8 %all-to-all-start.7 = ((bf16[8,64,768]{2,1,0:T(8,128)(2,1)}), bf16[8,64,768]{2,1,0:T(8,128)(2,1)}, u32[]{:S(2)}, u32[]{:S(2)}) async-start(bf16[8,64,768]{2,1,0:T(8,128)(2,1)} %bitcast.148), calls=%async_computation.9 | async-start | bytes 1572864 | tf_op jit(solution)/shard_map/all_to_all | solution.py:504
  (76 other events, 1138.5 us)
Sparse Core Ops, SparseCore 0:
  18.6 29.4 all-gather.14
  50.3 62.9 all-gather.6
  114.9 79.3 all-gather.8
  195.7 79.5 all-gather.10
  276.7 79.1 all-gather.12
  358.0 75.2 reduce-scatter.4
  435.6 77.2 reduce-scatter.10
  515.3 77.2 reduce-scatter.8
  594.9 77.4 reduce-scatter.6

commit v3 on v2

--- a/solution.py
+++ b/solution.py
@@ -84,10 +84,11 @@
     return (left.astype(F32) + right.astype(F32)).astype(BF16)
 
 
-def scatter_rows(make):
+def scatter_rows(make, seen):
     size = lax.axis_size("kv")
     if size != 8:
         full = make(0, size)
+        seen.append(full)
         return lax.psum_scatter(full, "kv", scatter_dimension=0, tiled=True).astype(F32)
     odd = make(4, 8)
     theirs = swap(odd, 1)
@@ -110,6 +111,7 @@
         (add16(both(2, 0), from_x[half:]), add16(both(1, 1), from_y[half:]))
     )
     last_y, last_x = lax.optimization_barrier((swap(send_y, 4), swap(send_x, 2)))
+    seen += [last_y, last_x]
     top = both(0, 0).astype(F32) + from_x[:half].astype(F32) + last_y.astype(F32)
     low = both(0, 1).astype(F32) + from_y[:half].astype(F32) + last_x.astype(F32)
     return jnp.concatenate([top, low], axis=0)
@@ -117,17 +119,6 @@
 
 def after(values, *others):
     return lax.optimization_barrier((values,) + tuple(others))[0]
-
-
-def exchange(values):
-    size = lax.axis_size("kv")
-    if size != 8:
-        return lax.all_to_all(values, "kv", 0, 0)
-    index = lax.axis_index("kv").astype(jnp.int32)
-    relative = index ^ jnp.arange(size, dtype=jnp.int32)
-    ordered = values[relative]
-    moved = jnp.stack([ordered[0]] + [swap(ordered[m], m) for m in range(1, size)])
-    return moved[relative]
 
 
 def spread_small(values, axis):
@@ -383,7 +374,7 @@
     w_three = jnp.stack([w_query, w_key, w_value])
     w_three = w_three.reshape(3, piece, share, mine, planes, HEAD_DIM)
     w_three = w_three.transpose(4, 2, 1, 0, 3, 5).reshape(group, piece, 3 * wide)
-    w_three = exchange(w_three).reshape(group * piece, 3 * wide)
+    w_three = lax.all_to_all(w_three, "kv", 0, 0).reshape(group * piece, 3 * wide)
     w_three = lax.all_gather(w_three, "seq", axis=0, tiled=True)
     out_w = lax.all_gather(w_out, "seq", axis=0, tiled=False)
     out_w = lax.all_to_all(
@@ -436,7 +427,7 @@
     def partial_hidden(start, stop):
         return dot_plain(chunk_rows(mixed, start, stop), out_w).astype(BF16)
 
-    hidden = flat + scatter_rows(partial_hidden)
+    hidden = flat + scatter_rows(partial_hidden, [])
 
     second16 = rms_norm(hidden, gains[1]).astype(BF16)
     masses = lax.all_to_all(after(mass, second16).reshape(group, local), "kv", 0, 0)
@@ -464,15 +455,10 @@
         )
         return partials[-1]
 
-    grad_second = scatter_rows(partial_second)
-    second_later = after(second_all, *partials)
+    grad_second = scatter_rows(partial_second, [])
     grads_gate = lax.psum_scatter(
-        dot_left(second_later, dgate).astype(BF16), "seq", scatter_dimension=0, tiled=True
-    )
-    grads_up = lax.psum_scatter(
-        dot_left(second_later, dup).astype(BF16), "seq", scatter_dimension=0, tiled=True
-    )
-
+        dot_left(after(second_all, *partials), dgate).astype(BF16), "seq", scatter_dimension=0, tiled=True
+    )
     grad_hidden = dy16.astype(F32) + rms_back(hidden, gains[1], grad_second)
     dh_chunks = gather_chunks(after(grad_hidden.astype(BF16), grads_down))
     grads_down = grads_down.astype(F32).T
@@ -482,26 +468,33 @@
         product = dot_plain(after(chunk_rows(inner, start, stop), *partials), down_w)
         return after(product.astype(BF16), *dh_chunks[-2:])
 
-    result = hidden + scatter_rows(partial_result)
+    ends, normed_parts = [], []
+    result = hidden + scatter_rows(partial_result, ends)
     dmixed = dot_right(dh_all, out_w).astype(BF16)
     grad_w_out = dot_left(mixed, dh_all).astype(BF16)
     dqkv = attend_backward(source, last, q, k, v, dmixed, cosine, sine, doc_col, doc_row)
 
     def partial_normed(start, stop):
-        return dot_right(chunk_rows(dqkv, start, stop), w_three).astype(BF16)
-
-    grad_normed = scatter_rows(partial_normed)
+        product = dot_right(after(chunk_rows(dqkv, start, stop), grads_gate), w_three)
+        normed_parts.append(product.astype(BF16))
+        return normed_parts[-1]
+
+    grad_normed = scatter_rows(partial_normed, ends)
     grad_input = grad_hidden + rms_back(flat, gains[0], grad_normed)
-    grads_gate, grads_up = after((grads_gate, grads_up), grad_input, result)
 
     grad_w_out = grad_w_out.reshape(mine, share, piece, width).transpose(1, 0, 2, 3)
     grad_w_out = lax.all_to_all(grad_w_out, "kv", 0, 0, axis_index_groups=pairs)
     grad_w_out = grad_w_out.reshape(ring * group * piece, width // group)
     grad_four = jnp.concatenate([dot_left(normed, dqkv).astype(BF16), grad_w_out], axis=1)
     grad_four = lax.psum_scatter(grad_four, "seq", scatter_dimension=0, tiled=True)
+    grads_up = lax.psum_scatter(
+        dot_left(after(second_all, *normed_parts), dup).astype(BF16),
+        "seq", scatter_dimension=0, tiled=True,
+    )
     grad_w_out = grad_four[:, 3 * wide :].reshape(piece, width).astype(F32)
     grad_three = grad_four[:, : 3 * wide]
     grad_three = lax.all_to_all(grad_three.reshape(group, piece, 3 * wide), "kv", 0, 0)
+    grads_up = after(grads_up, grad_three, *ends)
     grad_three = grad_three.reshape(planes, share, piece, 3, mine, HEAD_DIM)
     grad_three = grad_three.transpose(3, 2, 1, 4, 0, 5).reshape(3, piece, width).astype(F32)
 

time: 716 us -> 690 us (0.964)
  waiting for transfers between devices: 256 us -> 215 us
  blocking collectives: 5.55 us -> 23.5 us
  starting transfers between devices: 78.1 us -> 69.8 us
    all_to_all x0 -> x1, blocking collectives: none -> 17.6 us  [per_device(): lax.all_to_all(w_three, 'kv', 0, 0).reshape(group * piece, 3 * wide)]
    reduce_scatter x2, waiting for transfers between devices: 41.1 us -> 27.4 us  [the longest x1 27.4 us: per_device(): lax.psum_scatter(dot_left(after(second_all, *normed_parts), dup).astype(B...]
    ppermute x63 -> x56, starting transfers between devices: 45.3 us -> 34.8 us  [swap(): return lax.ppermute(values, 'kv', [(i, i ^ mask) for i in range(size)])]
    ppermute x63 -> x56, waiting for transfers between devices: 127 us -> 117 us  [swap(): return lax.ppermute(values, 'kv', [(i, i ^ mask) for i in range(size)])]
    all_gather x1, waiting for transfers between devices: 54.7 us -> 45.3 us  [per_device(): down_w = lax.all_gather(w_down, 'seq', axis=1, tiled=True)]
    unnamed x167 -> x165, local copies, waits for them, and re-layouts: 43.9 us -> 51.1 us
  transfers between devices with their start and end apart: 80 -> 73, of which waited for: 35 -> 32; matrix products, arithmetic and copies ran while one was open for 42% -> 45% of each run, Pallas kernels for 5% -> 5%
where the time goes in v3:
time: 690 us; the launch traced here: 681 us
  waiting for transfers between devices  215 us (31%)
  matrix products  148 us (21%)
  local copies, waits for them, and re-layouts  95.3 us (14%)
  other arithmetic  80.5 us (12%)
  starting transfers between devices  69.8 us (10%)
  Pallas kernels  33.4 us (5%)
  blocking collectives  23.5 us (3%)
  between operations  15.3 us (2%)
    ppermute x56, waiting for transfers between devices, swap(): return lax.ppermute(values, 'kv', [(i, i ^ mask) for i in range(size)])  117 us
    dot_general x8, matrix products, dot_plain(): return jnp.dot(left, right, preferred_element_type=F32)  55 us
    dot_general x8, matrix products, dot_right(): lax.dot_general(left, right, (((1,), (1,)), ((), ())), preferred_element_...  54.3 us
    unnamed x165, local copies, waits for them, and re-layouts  51.1 us
    all_gather x1, waiting for transfers between devices, per_device(): down_w = lax.all_gather(w_down, 'seq', axis=1, tiled=True)  45.3 us
    dot_general x5, matrix products, dot_left(): lax.dot_general(left, right, (((0,), (0,)), ((), ())), preferred_element_...  38.5 us
    ppermute x56, starting transfers between devices, swap(): return lax.ppermute(values, 'kv', [(i, i ^ mask) for i in range(size)])  34.8 us
    reduce_scatter x1, waiting for transfers between devices, per_device(): lax.psum_scatter(dot_left(after(second_all, *normed_parts), dup).astype(B...  27.4 us
  transfers between devices with their start and end apart: 73, of which 32 were waited for; matrix products, arithmetic and copies ran while one was open for 45% of the time, Pallas kernels for 5%

profile of v3, /device:TPU:0, one launch (start us, length us, event | category | flops | bytes accessed | tf_op | source)
XLA Modules:
  0.0 681.1 jit_solution(10339734825445381688)
XLA Ops:
  13.6 17.6 %all_to_all.60 = bf16[8,64,768]{2,1,0:T(8,128)(2,1)} all-to-all(bf16[8,64,768]{2,1,0:T(8,128)(2,1)S(1)} %reshape.360), channel_id=1, replica_groups=mesh['seq'=4,'kv'=8] {'kv'}, dimensions={0} | all-to-all | bytes 1572864 | tf_op jit(solution)/shard_map/all_to_all | solution.py:377
  33.8 3.7 all-to-all-start.1
  39.2 3.7 fusion.29
  43.6 3.0 pad_maximum_fusion.3
  46.7 5.1 all-to-all-done.1
  52.4 3.3 all-to-all-start
  57.1 3.4 all-to-all-done
  60.4 4.9 all-to-all-start.2
  79.5 2.8 collective-permute-done.2
  92.5 14.4 %collective-permute-done.9 = bf16[192,2048]{1,0:T(8,128)(2,1)} collective-permute-done((bf16[192,2048]{1,0:T(8,128)(2,1)S(1)}, bf16[192,2048]{1,0:T(8,128)(2,1)}, u32[]{:S(2)}, u32[]{:S(2)}) %collective-permute-start.9) | collective-permute-done | bytes 786464 | tf_op jit(solution)/shard_map/ppermute | solution.py:52
  111.1 4.6 fusion
  115.8 3.6 all-to-all-start.4
  120.9 6.9 %fusion.2 = bf16[1536,2048]{1,0:T(8,128)(2,1)} fusion(bf16[1536,2048]{1,0:T(8,128)(2,1)} %constant_dynamic-update-slice_fusion, f32[2048]{0:T(1024)S(1)} %mul.298, f32[1536]{0:T(1024)S(1)} %add_rsqrt_fusion), kind=kLoop, calls=%fused_computation.5 | loop fusion | flops 12582912 | bytes 12597248 | tf_op jit(solution)/shard_map/convert_element_type | solution.py:421
  127.9 6.2 convolution_convert_fusion.12.v_hbm
  134.2 7.9 %fusion.4.qk_hbm = f32[1536,512]{1,0:T(8,128)} fusion(bf16[1536,2048]{1,0:T(8,128)(2,1)} %fusion.2, bf16[2048,768]{1,0:T(8,128)(2,1)S(1)} %copy-done.50), kind=kOutput, calls=%fused_computation.31 | convolution fusion | flops 3221225472 | bytes 11534336 | tf_op jit(solution)/shard_map/dot_general | solution.py:20
  142.1 16.1 %attend_forward.1 = (bf16[1536,256]{1,0:T(8,128)(2,1)}, bf16[1536,256]{1,0:T(8,128)(2,1)}, bf16[1536,256]{1,0:T(8,128)(2,1)}, f32[1536,1]{1,0:T(8,128)}, bf16[1536,256]{1,0:T(8,128)(2,1)}) custom-call(s32[16]{0:T(128)} %pad_add_fusion.1.source, s32[6]{0:T(128)} %and_select_fusion.1.first, f32[1536,512]{1,0:T(8,128)} %fusion.4.qk_hbm, ...), custom_call_target="tpu_custom_call" | custom-call | flops 1207959552 | bytes 7077888 | tf_op jit(solution)/shard_map/attend_forward/pallas_call | solution.py:219
  158.1 3.8 convolution_convert_fusion.7
  163.6 4.5 collective-permute-done.17
  179.5 10.6 %collective-permute-done.18 = bf16[192,2048]{1,0:T(8,128)(2,1)S(1)} collective-permute-done((bf16[192,2048]{1,0:T(8,128)(2,1)S(1)}, bf16[192,2048]{1,0:T(8,128)(2,1)S(1)}, u32[]{:S(2)}, u32[]{:S(2)}) %collective-permute-start.18) | collective-permute-done | bytes 786464 | tf_op jit(solution)/shard_map/ppermute | solution.py:52
  197.7 5.1 collective-permute-done.20
  215.6 3.3 all-to-all-start.5
  220.7 5.8 all-to-all-done.5
  229.7 5.3 all-to-all-start.6
  236.0 7.2 %all-to-all-done.6 = f32[32,1,1]{2,1,0:T(1,128)} async-done(((f32[32,1,1]{2,1,0:T(1,128)}), f32[32,1,1]{2,1,0:T(1,128)}, u32[]{:S(2)}, u32[]{:S(2)}) %all-to-all-start.6) | async-done | bytes 160 | tf_op jit(solution)/shard_map/all_to_all | solution.py:436
  250.7 5.8 collective-permute-done.24
  264.3 11.8 %fusion.35 = f32[1536,1024]{1,0:T(8,128)} fusion(bf16[1536,2048]{1,0:T(8,128)(2,1)} %constant_dynamic-update-slice_fusion.10, bf16[2048,1024]{1,0:T(8,128)(2,1)} %all-gather.9.cloned.1.call-done), kind=kOutput, calls=%fused_computation.213 | convolution fusion | flops 6442450944 | bytes 16777216 | tf_op jit(solution)/shard_map/dot_general | solution.py:20
  276.1 13.1 %multiply_convert_fusion.2 = (bf16[1536,1024]{1,0:T(8,128)(2,1)S(1)}, f32[1536,1024]{1,0:T(8,128)}) fusion(f32[1536,1024]{1,0:T(8,128)} %fusion.35, bf16[1536,2048]{1,0:T(8,128)(2,1)} %constant_dynamic-update-slice_fusion.10, bf16[2048,1024]{1,0:T(8,128)(2,1)} %all-gather.11.cloned.1.call-done), kind=kOutput, calls=%fused_computation.10 | convolution fusion | flops 6451888128 | bytes 26214400 | tf_op jit(solution)/shard_map/dot_general | solution.py:20
  290.8 11.3 %convolution_convert_fusion.2 = bf16[2048,1024]{1,0:T(8,128)(2,1)} fusion(bf16[1536,2048]{1,0:T(8,128)(2,1)} %constant_dynamic-update-slice_fusion.20, bf16[1536,1024]{1,0:T(8,128)(2,1)S(1)} %get-tuple-element.253), kind=kOutput, calls=%fused_computation.16 | convolution fusion | flops 6444548096 | bytes 13631488 | tf_op jit(solution)/shard_map/dot_general | solution.py:24
  302.2 45.3 %all-gather.13.cloned.1.call-done = bf16[1024,2048]{1,0:T(8,128)(2,1)} async-done(((bf16[1024,512]{1,0:T(8,128)(2,1)}), bf16[1024,2048]{1,0:T(8,128)(2,1)}) %all-gather.13.cloned.1.call-update) | async-done | bytes 4194320 | tf_op jit(solution)/shard_map/all_gather | solution.py:386
  347.5 17.5 %multiply_convert_fusion = (bf16[1536,1024]{1,0:T(8,128)(2,1)}, bf16[1536,1024]{1,0:T(8,128)(2,1)S(1)}) fusion(f32[1536,1024]{1,0:T(8,128)} %fusion.35, f32[1536,1024]{1,0:T(8,128)} %get-tuple-element.254, bf16[1536,2048]{1,0:T(8,128)(2,1)} %constant_dynamic-update-slice_fusion.20, bf16[1024,2048]{1,0:T(8,128)(2,1)} %all-gather.13.cloned.1.call-done), kind=kOutput, calls=%fused_computation.8 | convolution fusion | flops 6462898176 | bytes 29360128 | tf_op jit(solution)/shard_map/dot_general | solution.py:28
  365.0 3.4 fusion.17
  369.2 3.7 add_convert_fusion.1
  373.0 6.9 %fusion.14 = f32[768,2048]{1,0:T(8,128)} fusion(bf16[2048,1024]{1,0:T(8,128)(2,1)S(1)} %copy-done.47, bf16[1536,1024]{1,0:T(8,128)(2,1)} %copy-done.54), kind=kOutput, calls=%fused_computation.44 | convolution fusion | flops 3221225472 | bytes 12058624 | tf_op jit(solution)/shard_map/dot_general | solution.py:28
  379.9 6.2 add_convert_fusion
  393.8 8.6 %convolution_convert_fusion.1 = bf16[2048,1024]{1,0:T(8,128)(2,1)} fusion(bf16[1536,2048]{1,0:T(8,128)(2,1)S(1)} %bitcast.126, bf16[1536,1024]{1,0:T(8,128)(2,1)S(1)} %copy-done.55), kind=kOutput, calls=%fused_computation.15 | convolution fusion | flops 6444548096 | bytes 13631488 | tf_op jit(solution)/shard_map/dot_general | solution.py:24
  402.5 8.9 %collective-permute-done.33 = bf16[192,2048]{1,0:T(8,128)(2,1)S(1)} collective-permute-done((bf16[192,2048]{1,0:T(8,128)(2,1)}, bf16[192,2048]{1,0:T(8,128)(2,1)S(1)}, u32[]{:S(2)}, u32[]{:S(2)}) %collective-permute-start.33) | collective-permute-done | bytes 786464 | tf_op jit(solution)/shard_map/ppermute | solution.py:52
  416.3 8.3 %collective-permute-done.35 = bf16[96,2048]{1,0:T(8,128)(2,1)S(1)} collective-permute-done((bf16[96,2048]{1,0:T(8,128)(2,1)S(1)}, bf16[96,2048]{1,0:T(8,128)(2,1)S(1)}, u32[]{:S(2)}, u32[]{:S(2)}) %collective-permute-start.35) | collective-permute-done | bytes 393248 | tf_op jit(solution)/shard_map/ppermute | solution.py:52
  434.0 14.5 %collective-permute-done.37 = bf16[192,2048]{1,0:T(8,128)(2,1)S(1)} collective-permute-done((bf16[192,2048]{1,0:T(8,128)(2,1)}, bf16[192,2048]{1,0:T(8,128)(2,1)S(1)}, u32[]{:S(2)}, u32[]{:S(2)}) %collective-permute-start.37) | collective-permute-done | bytes 786464 | tf_op jit(solution)/shard_map/ppermute | solution.py:52
  451.2 6.7 collective-permute-done.38
  462.8 5.9 all_to_all.61
  473.2 5.8 convolution_convert_fusion.11.g_hbm
  479.1 17.3 %attend_backward.1 = bf16[1536,768]{1,0:T(8,128)(2,1)} custom-call(s32[16]{0:T(128)} %pad_add_fusion.1.source, s32[6]{0:T(128)} %and_select_fusion.last, bf16[1536,256]{1,0:T(8,128)(2,1)} %get-tuple-element.100.q_ref, bf16[1536,256]{1,0:T(8,128)(2,1)} %get-tuple-element.101.k_ref, bf16[1536,256]{1,0:T(8,128)(2,1)} %get-tuple-element.102.v_ref, ...), custom_call_target="tpu_custom_call" | custom-call | flops 3019898880 | bytes 5505024 | tf_op jit(solution)/shard_map/attend_backward/pallas_call | solution.py:319
  496.5 8.0 %convolution_convert_fusion.9 = bf16[2048,768]{0,1:T(8,128)(2,1)S(1)} fusion(bf16[1536,2048]{1,0:T(8,128)(2,1)} %fusion.2, bf16[1536,768]{1,0:T(8,128)(2,1)} %attend_backward.1), kind=kOutput, calls=%fused_computation.23 | convolution fusion | flops 4833411072 | bytes 11796480 | tf_op jit(solution)/shard_map/dot_general | solution.py:24
  504.5 2.3 pad_maximum_fusion
  507.0 3.5 fusion.31
  510.5 5.0 convolution_convert_fusion.5
  517.0 6.7 convolution_convert_fusion.3
  523.9 4.0 convolution_convert_fusion.4
  528.3 8.8 %convolution_convert_fusion = bf16[2048,1024]{1,0:T(8,128)(2,1)} fusion(bf16[1536,2048]{1,0:T(8,128)(2,1)S(1)} %bitcast.128, bf16[1536,1024]{1,0:T(8,128)(2,1)S(1)} %copy-done.57), kind=kOutput, calls=%fused_computation.14 | convolution fusion | flops 6444548096 | bytes 13631488 | tf_op jit(solution)/shard_map/dot_general | solution.py:24
  537.1 6.2 convolution_convert_fusion.6
  543.4 3.0 add_convert_fusion.9
  552.9 14.2 %collective-permute-done.52 = bf16[192,2048]{1,0:T(8,128)(2,1)S(1)} collective-permute-done((bf16[192,2048]{1,0:T(8,128)(2,1)S(1)}, bf16[192,2048]{1,0:T(8,128)(2,1)S(1)}, u32[]{:S(2)}, u32[]{:S(2)}) %collective-permute-start.52) | collective-permute-done | bytes 786464 | tf_op jit(solution)/shard_map/ppermute | solution.py:52
  568.0 2.7 add_convert_fusion.4
  572.4 11.5 %collective-permute-done.44 = bf16[192,2048]{1,0:T(8,128)(2,1)S(1)} collective-permute-done((bf16[192,2048]{1,0:T(8,128)(2,1)S(1)}, bf16[192,2048]{1,0:T(8,128)(2,1)S(1)}, u32[]{:S(2)}, u32[]{:S(2)}) %collective-permute-start.44) | collective-permute-done | bytes 786464 | tf_op jit(solution)/shard_map/ppermute | solution.py:52
  584.8 2.7 add_convert_fusion.14
  590.6 2.8 convert_bitcast_fusion
  593.4 3.3 copy.102
  596.7 2.8 convert_element_type.731
  609.3 5.7 all-to-all-start.9
  615.9 3.4 add_bitcast_fusion.1
  626.1 4.5 all-to-all-start.8
  630.6 2.3 fusion.19
  637.6 27.4 %reduce-scatter.11.cloned.1.call-done = bf16[512,1024]{1,0:T(8,128)(2,1)} async-done(((bf16[2048,1024]{1,0:T(8,128)(2,1)}), bf16[512,1024]{1,0:T(8,128)(2,1)}) %reduce-scatter.11.cloned.1.call-update) | async-done | bytes 1048592 | tf_op jit(solution)/shard_map/reduce_scatter | solution.py:490
  664.9 2.8 convert_element_type.733
  (402 shorter events, 178.1 us)
Async XLA Ops:
  7.2 108.6 %all-gather.15.cloned.1.call-start = ((), (), s32[]{:S(2)}) async-start(), calls=%async_computation.22 | async-start | bytes 1310720 | tf_op jit(solution)/shard_map/all_gather | solution.py:379
  7.9 120.0 %all-gather.7.cloned.1.call-start = ((), (), s32[]{:S(2)}) async-start(), calls=%async_computation.14 | async-start | bytes 3932160 | tf_op jit(solution)/shard_map/all_gather | solution.py:378
  31.3 233.0 %all-gather.9.cloned.1.call-start = ((), (), s32[]{:S(2)}) async-start(), calls=%async_computation.15 | async-start | bytes 5242880 | tf_op jit(solution)/shard_map/all_gather | solution.py:384
  32.0 39.3 %collective-permute-start = (bf16[192,2048]{1,0:T(8,128)(2,1)S(1)}, bf16[192,2048]{1,0:T(8,128)(2,1)}, u32[]{:S(2)}, u32[]{:S(2)}) collective-permute-start(bf16[192,2048]{1,0:T(8,128)(2,1)S(1)} %bitcast.99), channel_id=1, source_target_pairs={{0,2},{1,3},{2,0},{3,1},{4,6},{5,7},{6,4},{7,5},{8,10},{9,11},{10,... | collective-permute-start | bytes 2359304 | tf_op jit(solution)/shard_map/ppermute | solution.py:52
  32.6 40.4 %collective-permute-start.1 = (bf16[192,2048]{1,0:T(8,128)(2,1)S(1)}, bf16[192,2048]{1,0:T(8,128)(2,1)}, u32[]{:S(2)}, u32[]{:S(2)}) collective-permute-start(bf16[192,2048]{1,0:T(8,128)(2,1)S(1)} %bitcast.100), channel_id=1, source_target_pairs={{0,4},{1,5},{2,6},{3,7},{4,0},{5,1},{6,2},{7,3},{8,12},{9,13},{10,... | collective-permute-start | bytes 2359304 | tf_op jit(solution)/shard_map/ppermute | solution.py:52
  33.2 51.5 %collective-permute-start.4 = (bf16[192,2048]{1,0:T(8,128)(2,1)S(1)}, bf16[192,2048]{1,0:T(8,128)(2,1)}, u32[]{:S(2)}, u32[]{:S(2)}) collective-permute-start(bf16[192,2048]{1,0:T(8,128)(2,1)S(1)} %bitcast.101), channel_id=1, source_target_pairs={{0,1},{1,0},{2,3},{3,2},{4,5},{5,4},{6,7},{7,6},{8,9},{9,8},{10,11... | collective-permute-start | bytes 2359304 | tf_op jit(solution)/shard_map/ppermute | solution.py:52
  33.8 18.0 %all-to-all-start.1 = ((bf16[8,2,64]{2,1,0:T(2,128)(2,1)}), bf16[8,2,64]{2,1,0:T(2,128)(2,1)S(1)}, u32[]{:S(2)}, u32[]{:S(2)}) async-start(bf16[8,2,64]{2,1,0:T(2,128)(2,1)} %broadcast_in_dim.9), calls=%async_computation.1 | async-start | bytes 8192 | tf_op jit(solution)/shard_map/all_to_all | solution.py:126
  37.6 238.5 %all-gather.11.cloned.1.call-start = ((), (), s32[]{:S(2)}) async-start(), calls=%async_computation.16 | async-start | bytes 5242880 | tf_op jit(solution)/shard_map/all_gather | solution.py:385
  52.4 8.0 %all-to-all-start = ((s32[8,1,192]{2,1,0:T(1,128)}), s32[8,1,192]{2,1,0:T(1,128)S(1)}, u32[]{:S(2)}, u32[]{:S(2)}) async-start(s32[8,1,192]{2,1,0:T(1,128)} %broadcast_in_dim.8), calls=%async_computation | async-start | bytes 16384 | tf_op jit(solution)/shard_map/all_to_all | solution.py:126
  60.4 10.6 %all-to-all-start.2 = ((bf16[4,2,512]{2,1,0:T(2,128)(2,1)}), bf16[4,2,512]{2,1,0:T(2,128)(2,1)S(1)}, u32[]{:S(2)}, u32[]{:S(2)}) async-start(bf16[4,2,512]{2,1,0:T(2,128)(2,1)} %reshape.395), calls=%async_computation.2 | async-start | bytes 16384 | tf_op jit(solution)/shard_map/all_to_all | solution.py:126
  72.4 9.9 %collective-permute-start.2 = (bf16[96,2048]{1,0:T(8,128)(2,1)S(1)}, bf16[96,2048]{1,0:T(8,128)(2,1)S(1)}, u32[]{:S(2)}, u32[]{:S(2)}) collective-permute-start(bf16[96,2048]{1,0:T(8,128)(2,1)S(1)} %slice.464), channel_id=1, source_target_pairs={{0,4},{1,5},{2,6},{3,7},{4,0},{5,1},{6,2},{7,3},{8,12},{9,13},{10,... | collective-permute-start | bytes 1179656 | tf_op jit(solution)/shard_map/ppermute | solution.py:52
  74.1 9.8 %collective-permute-start.3 = (bf16[96,2048]{1,0:T(8,128)(2,1)S(1)}, bf16[96,2048]{1,0:T(8,128)(2,1)S(1)}, u32[]{:S(2)}, u32[]{:S(2)}) collective-permute-start(bf16[96,2048]{1,0:T(8,128)(2,1)S(1)} %slice.465), channel_id=1, source_target_pairs={{0,2},{1,3},{2,0},{3,1},{4,6},{5,7},{6,4},{7,5},{8,10},{9,11},{10,... | collective-permute-start | bytes 1179656 | tf_op jit(solution)/shard_map/ppermute | solution.py:52
  74.7 14.2 %collective-permute-start.5 = (bf16[192,2048]{1,0:T(8,128)(2,1)}, bf16[192,2048]{1,0:T(8,128)(2,1)S(1)}, u32[]{:S(2)}, u32[]{:S(2)}) collective-permute-start(bf16[192,2048]{1,0:T(8,128)(2,1)} %collective-permute-done), channel_id=1, source_target_pairs={{0,1},{1,0},{2,3},{3,2},{4,5},{5,4},{6,7},{7,6},{8,9},{9,8},{10,11... | collective-permute-start | bytes 2359304 | tf_op jit(solution)/shard_map/ppermute | solution.py:52
  74.7 15.2 %collective-permute-start.6 = (bf16[192,2048]{1,0:T(8,128)(2,1)}, bf16[192,2048]{1,0:T(8,128)(2,1)S(1)}, u32[]{:S(2)}, u32[]{:S(2)}) collective-permute-start(bf16[192,2048]{1,0:T(8,128)(2,1)} %collective-permute-done.1), channel_id=1, source_target_pairs={{0,1},{1,0},{2,3},{3,2},{4,5},{5,4},{6,7},{7,6},{8,9},{9,8},{10,11... | collective-permute-start | bytes 2359304 | tf_op jit(solution)/shard_map/ppermute | solution.py:52
  86.8 20.1 %collective-permute-start.9 = (bf16[192,2048]{1,0:T(8,128)(2,1)S(1)}, bf16[192,2048]{1,0:T(8,128)(2,1)}, u32[]{:S(2)}, u32[]{:S(2)}) collective-permute-start(bf16[192,2048]{1,0:T(8,128)(2,1)S(1)} %bitcast.113), channel_id=1, source_target_pairs={{0,2},{1,3},{2,0},{3,1},{4,6},{5,7},{6,4},{7,5},{8,10},{9,11},{10,... | collective-permute-start | bytes 2359304 | tf_op jit(solution)/shard_map/ppermute | solution.py:52
  88.4 20.8 %collective-permute-start.11 = (bf16[192,2048]{1,0:T(8,128)(2,1)S(1)}, bf16[192,2048]{1,0:T(8,128)(2,1)}, u32[]{:S(2)}, u32[]{:S(2)}) collective-permute-start(bf16[192,2048]{1,0:T(8,128)(2,1)S(1)} %bitcast.114), channel_id=1, source_target_pairs={{0,4},{1,5},{2,6},{3,7},{4,0},{5,1},{6,2},{7,3},{8,12},{9,13},{10,... | collective-permute-start | bytes 2359304 | tf_op jit(solution)/shard_map/ppermute | solution.py:52
  107.9 12.4 %collective-permute-start.13 = (bf16[96,2048]{1,0:T(8,128)(2,1)S(1)}, bf16[96,2048]{1,0:T(8,128)(2,1)}, u32[]{:S(2)}, u32[]{:S(2)}) collective-permute-start(bf16[96,2048]{1,0:T(8,128)(2,1)S(1)} %slice.467), channel_id=1, source_target_pairs={{0,4},{1,5},{2,6},{3,7},{4,0},{5,1},{6,2},{7,3},{8,12},{9,13},{10,... | collective-permute-start | bytes 1179656 | tf_op jit(solution)/shard_map/ppermute | solution.py:52
  110.3 10.6 %collective-permute-start.15 = (bf16[96,2048]{1,0:T(8,128)(2,1)S(1)}, bf16[96,2048]{1,0:T(8,128)(2,1)}, u32[]{:S(2)}, u32[]{:S(2)}) collective-permute-start(bf16[96,2048]{1,0:T(8,128)(2,1)S(1)} %slice.468), channel_id=1, source_target_pairs={{0,2},{1,3},{2,0},{3,1},{4,6},{5,7},{6,4},{7,5},{8,10},{9,11},{10,... | collective-permute-start | bytes 1179656 | tf_op jit(solution)/shard_map/ppermute | solution.py:52
  115.8 11.9 %all-to-all-start.4 = ((bf16[2,2,64,2048]{3,2,1,0:T(8,128)(2,1)}), bf16[2,2,64,2048]{3,2,1,0:T(8,128)(2,1)S(1)}, u32[]{:S(2)}, u32[]{:S(2)}) async-start(bf16[2,2,64,2048]{3,2,1,0:T(8,128)(2,1)} %bitcast.123), calls=%async_computation.4 | async-start | bytes 2097152 | tf_op jit(solution)/shard_map/all_to_all | solution.py:380
  119.4 228.1 %all-gather.13.cloned.1.call-start = ((), (), s32[]{:S(2)}) async-start(), calls=%async_computation.17 | async-start | bytes 5242880 | tf_op jit(solution)/shard_map/all_gather | solution.py:386
  119.8 8.1 %collective-permute-start.10 = (bf16[192,2048]{1,0:T(8,128)(2,1)}, bf16[192,2048]{1,0:T(8,128)(2,1)}, u32[]{:S(2)}, u32[]{:S(2)}) collective-permute-start(bf16[192,2048]{1,0:T(8,128)(2,1)} %collective-permute-done.9), channel_id=1, source_target_pairs={{0,1},{1,0},{2,3},{3,2},{4,5},{5,4},{6,7},{7,6},{8,9},{9,8},{10,11... | collective-permute-start | bytes 2359304 | tf_op jit(solution)/shard_map/ppermute | solution.py:52
  120.3 7.6 %collective-permute-start.12 = (bf16[192,2048]{1,0:T(8,128)(2,1)}, bf16[192,2048]{1,0:T(8,128)(2,1)}, u32[]{:S(2)}, u32[]{:S(2)}) collective-permute-start(bf16[192,2048]{1,0:T(8,128)(2,1)} %collective-permute-done.11), channel_id=1, source_target_pairs={{0,1},{1,0},{2,3},{3,2},{4,5},{5,4},{6,7},{7,6},{8,9},{9,8},{10,11... | collective-permute-start | bytes 2359304 | tf_op jit(solution)/shard_map/ppermute | solution.py:52
  170.2 19.9 %collective-permute-start.18 = (bf16[192,2048]{1,0:T(8,128)(2,1)S(1)}, bf16[192,2048]{1,0:T(8,128)(2,1)S(1)}, u32[]{:S(2)}, u32[]{:S(2)}) collective-permute-start(bf16[192,2048]{1,0:T(8,128)(2,1)S(1)} %pad_maximum_fusion.5), channel_id=1, source_target_pairs={{0,2},{1,3},{2,0},{3,1},{4,6},{5,7},{6,4},{7,5},{8,10},{9,11},{10,... | collective-permute-start | bytes 2359304 | tf_op jit(solution)/shard_map/ppermute | solution.py:52
  171.5 19.5 %collective-permute-start.19 = (bf16[192,2048]{1,0:T(8,128)(2,1)S(1)}, bf16[192,2048]{1,0:T(8,128)(2,1)S(1)}, u32[]{:S(2)}, u32[]{:S(2)}) collective-permute-start(bf16[192,2048]{1,0:T(8,128)(2,1)S(1)} %pad_maximum_fusion.6), channel_id=1, source_target_pairs={{0,4},{1,5},{2,6},{3,7},{4,0},{5,1},{6,2},{7,3},{8,12},{9,13},{10,... | collective-permute-start | bytes 2359304 | tf_op jit(solution)/shard_map/ppermute | solution.py:52
  173.5 23.2 %collective-permute-start.31 = (bf16[192,2048]{1,0:T(8,128)(2,1)S(1)}, bf16[192,2048]{1,0:T(8,128)(2,1)S(1)}, u32[]{:S(2)}, u32[]{:S(2)}) collective-permute-start(bf16[192,2048]{1,0:T(8,128)(2,1)S(1)} %bitcast.116), channel_id=1, source_target_pairs={{0,1},{1,0},{2,3},{3,2},{4,5},{5,4},{6,7},{7,6},{8,9},{9,8},{10,11... | collective-permute-start | bytes 2359304 | tf_op jit(solution)/shard_map/ppermute | solution.py:52
  192.5 10.3 %collective-permute-start.20 = (bf16[96,2048]{1,0:T(8,128)(2,1)S(1)}, bf16[96,2048]{1,0:T(8,128)(2,1)S(1)}, u32[]{:S(2)}, u32[]{:S(2)}) collective-permute-start(bf16[96,2048]{1,0:T(8,128)(2,1)S(1)} %get-tuple-element.71), channel_id=1, source_target_pairs={{0,4},{1,5},{2,6},{3,7},{4,0},{5,1},{6,2},{7,3},{8,12},{9,13},{10,... | collective-permute-start | bytes 1179656 | tf_op jit(solution)/shard_map/ppermute | solution.py:52
  193.7 10.0 %collective-permute-start.21 = (bf16[96,2048]{1,0:T(8,128)(2,1)S(1)}, bf16[96,2048]{1,0:T(8,128)(2,1)S(1)}, u32[]{:S(2)}, u32[]{:S(2)}) collective-permute-start(bf16[96,2048]{1,0:T(8,128)(2,1)S(1)} %get-tuple-element.72), channel_id=1, source_target_pairs={{0,2},{1,3},{2,0},{3,1},{4,6},{5,7},{6,4},{7,5},{8,10},{9,11},{10,... | collective-permute-start | bytes 1179656 | tf_op jit(solution)/shard_map/ppermute | solution.py:52
  207.6 37.0 %collective-permute-start.22 = (bf16[192,2048]{1,0:T(8,128)(2,1)}, bf16[192,2048]{1,0:T(8,128)(2,1)}, u32[]{:S(2)}, u32[]{:S(2)}) collective-permute-start(bf16[192,2048]{1,0:T(8,128)(2,1)} %get-tuple-element.200), channel_id=1, source_target_pairs={{0,2},{1,3},{2,0},{3,1},{4,6},{5,7},{6,4},{7,5},{8,10},{9,11},{10,... | collective-permute-start | bytes 2359304 | tf_op jit(solution)/shard_map/ppermute | solution.py:52
  208.8 37.7 %collective-permute-start.23 = (bf16[192,2048]{1,0:T(8,128)(2,1)}, bf16[192,2048]{1,0:T(8,128)(2,1)S(1)}, u32[]{:S(2)}, u32[]{:S(2)}) collective-permute-start(bf16[192,2048]{1,0:T(8,128)(2,1)} %get-tuple-element.200), channel_id=1, source_target_pairs={{0,4},{1,5},{2,6},{3,7},{4,0},{5,1},{6,2},{7,3},{8,12},{9,13},{10,... | collective-permute-start | bytes 2359304 | tf_op jit(solution)/shard_map/ppermute | solution.py:52
  215.6 10.9 %all-to-all-start.5 = ((f32[8,1,192]{2,1,0:T(1,128)}), f32[8,1,192]{2,1,0:T(1,128)S(1)}, u32[]{:S(2)}, u32[]{:S(2)}) async-start(f32[8,1,192]{2,1,0:T(1,128)} %all_to_all.49), calls=%async_computation.5 | async-start | bytes 16384 | tf_op jit(solution)/shard_map/all_to_all | solution.py:433
  229.7 13.6 %all-to-all-start.6 = ((f32[32,1,1]{2,1,0:T(1,128)}), f32[32,1,1]{2,1,0:T(1,128)}, u32[]{:S(2)}, u32[]{:S(2)}) async-start(f32[32,1,1]{2,1,0:T(1,128)} %broadcast_in_dim.11), calls=%async_computation.6 | async-start | bytes 32768 | tf_op jit(solution)/shard_map/all_to_all | solution.py:436
  235.0 195.6 %reduce-scatter.5.cloned.1.call-start = ((), (), s32[]{:S(2)}) async-start(), calls=%async_computation.18 | async-start | bytes 5242880 | tf_op jit(solution)/shard_map/reduce_scatter | solution.py:443
  235.9 22.8 %collective-permute-start.26 = (bf16[192,2048]{1,0:T(8,128)(2,1)}, bf16[192,2048]{1,0:T(8,128)(2,1)}, u32[]{:S(2)}, u32[]{:S(2)}) collective-permute-start(bf16[192,2048]{1,0:T(8,128)(2,1)} %get-tuple-element.200), channel_id=1, source_target_pairs={{0,1},{1,0},{2,3},{3,2},{4,5},{5,4},{6,7},{7,6},{8,9},{9,8},{10,11... | collective-permute-start | bytes 2359304 | tf_op jit(solution)/shard_map/ppermute | solution.py:52
  245.6 10.9 %collective-permute-start.24 = (bf16[96,2048]{1,0:T(8,128)(2,1)S(1)}, bf16[96,2048]{1,0:T(8,128)(2,1)S(1)}, u32[]{:S(2)}, u32[]{:S(2)}) collective-permute-start(bf16[96,2048]{1,0:T(8,128)(2,1)S(1)} %slice.488), channel_id=1, source_target_pairs={{0,4},{1,5},{2,6},{3,7},{4,0},{5,1},{6,2},{7,3},{8,12},{9,13},{10,... | collective-permute-start | bytes 1179656 | tf_op jit(solution)/shard_map/ppermute | solution.py:52
  246.6 10.8 %collective-permute-start.25 = (bf16[96,2048]{1,0:T(8,128)(2,1)S(1)}, bf16[96,2048]{1,0:T(8,128)(2,1)S(1)}, u32[]{:S(2)}, u32[]{:S(2)}) collective-permute-start(bf16[96,2048]{1,0:T(8,128)(2,1)S(1)} %slice.489), channel_id=1, source_target_pairs={{0,2},{1,3},{2,0},{3,1},{4,6},{5,7},{6,4},{7,5},{8,10},{9,11},{10,... | collective-permute-start | bytes 1179656 | tf_op jit(solution)/shard_map/ppermute | solution.py:52
  247.2 13.5 %collective-permute-start.27 = (bf16[192,2048]{1,0:T(8,128)(2,1)}, bf16[192,2048]{1,0:T(8,128)(2,1)S(1)}, u32[]{:S(2)}, u32[]{:S(2)}) collective-permute-start(bf16[192,2048]{1,0:T(8,128)(2,1)} %collective-permute-done.22), channel_id=1, source_target_pairs={{0,1},{1,0},{2,3},{3,2},{4,5},{5,4},{6,7},{7,6},{8,9},{9,8},{10,11... | collective-permute-start | bytes 2359304 | tf_op jit(solution)/shard_map/ppermute | solution.py:52
  247.2 14.5 %collective-permute-start.28 = (bf16[192,2048]{1,0:T(8,128)(2,1)S(1)}, bf16[192,2048]{1,0:T(8,128)(2,1)S(1)}, u32[]{:S(2)}, u32[]{:S(2)}) collective-permute-start(bf16[192,2048]{1,0:T(8,128)(2,1)S(1)} %collective-permute-done.23), channel_id=1, source_target_pairs={{0,1},{1,0},{2,3},{3,2},{4,5},{5,4},{6,7},{7,6},{8,9},{9,8},{10,11... | collective-permute-start | bytes 2359304 | tf_op jit(solution)/shard_map/ppermute | solution.py:52
  302.1 214.8 %reduce-scatter.7.cloned.1.call-start = ((), (), s32[]{:S(2)}) async-start(), calls=%async_computation.19 | async-start | bytes 5242880 | tf_op jit(solution)/shard_map/reduce_scatter | solution.py:459
  372.9 13.2 %collective-permute-start.32 = (bf16[768,2048]{1,0:T(8,128)(2,1)S(1)}, bf16[768,2048]{1,0:T(8,128)(2,1)S(1)}, u32[]{:S(2)}, u32[]{:S(2)}) collective-permute-start(bf16[768,2048]{1,0:T(8,128)(2,1)S(1)} %add_convert_fusion.1), channel_id=1, source_target_pairs={{0,1},{1,0},{2,3},{3,2},{4,5},{5,4},{6,7},{7,6},{8,9},{9,8},{10,11... | collective-permute-start | bytes 9437192 | tf_op jit(solution)/shard_map/ppermute | solution.py:52
  391.2 20.2 %collective-permute-start.33 = (bf16[192,2048]{1,0:T(8,128)(2,1)}, bf16[192,2048]{1,0:T(8,128)(2,1)S(1)}, u32[]{:S(2)}, u32[]{:S(2)}) collective-permute-start(bf16[192,2048]{1,0:T(8,128)(2,1)} %pad_maximum_fusion.7), channel_id=1, source_target_pairs={{0,2},{1,3},{2,0},{3,1},{4,6},{5,7},{6,4},{7,5},{8,10},{9,11},{10,... | collective-permute-start | bytes 2359304 | tf_op jit(solution)/shard_map/ppermute | solution.py:52
  392.3 20.0 %collective-permute-start.34 = (bf16[192,2048]{1,0:T(8,128)(2,1)}, bf16[192,2048]{1,0:T(8,128)(2,1)}, u32[]{:S(2)}, u32[]{:S(2)}) collective-permute-start(bf16[192,2048]{1,0:T(8,128)(2,1)} %pad_maximum_fusion.8), channel_id=1, source_target_pairs={{0,4},{1,5},{2,6},{3,7},{4,0},{5,1},{6,2},{7,3},{8,12},{9,13},{10,... | collective-permute-start | bytes 2359304 | tf_op jit(solution)/shard_map/ppermute | solution.py:52
  402.4 219.2 %reduce-scatter.9.cloned.1.call-start = ((), (), s32[]{:S(2)}) async-start(), calls=%async_computation.20 | async-start | bytes 5242880 | tf_op jit(solution)/shard_map/reduce_scatter | solution.py:489
  414.2 10.5 %collective-permute-start.35 = (bf16[96,2048]{1,0:T(8,128)(2,1)S(1)}, bf16[96,2048]{1,0:T(8,128)(2,1)S(1)}, u32[]{:S(2)}, u32[]{:S(2)}) collective-permute-start(bf16[96,2048]{1,0:T(8,128)(2,1)S(1)} %get-tuple-element.84), channel_id=1, source_target_pairs={{0,4},{1,5},{2,6},{3,7},{4,0},{5,1},{6,2},{7,3},{8,12},{9,13},{10,... | collective-permute-start | bytes 1179656 | tf_op jit(solution)/shard_map/ppermute | solution.py:52
  415.7 10.1 %collective-permute-start.36 = (bf16[96,2048]{1,0:T(8,128)(2,1)S(1)}, bf16[96,2048]{1,0:T(8,128)(2,1)S(1)}, u32[]{:S(2)}, u32[]{:S(2)}) collective-permute-start(bf16[96,2048]{1,0:T(8,128)(2,1)S(1)} %get-tuple-element.85), channel_id=1, source_target_pairs={{0,2},{1,3},{2,0},{3,1},{4,6},{5,7},{6,4},{7,5},{8,10},{9,11},{10,... | collective-permute-start | bytes 1179656 | tf_op jit(solution)/shard_map/ppermute | solution.py:52
  430.6 17.9 %collective-permute-start.37 = (bf16[192,2048]{1,0:T(8,128)(2,1)}, bf16[192,2048]{1,0:T(8,128)(2,1)S(1)}, u32[]{:S(2)}, u32[]{:S(2)}) collective-permute-start(bf16[192,2048]{1,0:T(8,128)(2,1)} %add_convert_fusion.2), channel_id=1, source_target_pairs={{0,2},{1,3},{2,0},{3,1},{4,6},{5,7},{6,4},{7,5},{8,10},{9,11},{10,... | collective-permute-start | bytes 2359304 | tf_op jit(solution)/shard_map/ppermute | solution.py:52
  431.4 18.6 %collective-permute-start.40 = (bf16[192,2048]{1,0:T(8,128)(2,1)}, bf16[192,2048]{1,0:T(8,128)(2,1)S(1)}, u32[]{:S(2)}, u32[]{:S(2)}) collective-permute-start(bf16[192,2048]{1,0:T(8,128)(2,1)} %add_convert_fusion.2), channel_id=1, source_target_pairs={{0,4},{1,5},{2,6},{3,7},{4,0},{5,1},{6,2},{7,3},{8,12},{9,13},{10,... | collective-permute-start | bytes 2359304 | tf_op jit(solution)/shard_map/ppermute | solution.py:52
  432.6 25.8 %collective-permute-start.48 = (bf16[192,2048]{1,0:T(8,128)(2,1)}, bf16[192,2048]{1,0:T(8,128)(2,1)S(1)}, u32[]{:S(2)}, u32[]{:S(2)}) collective-permute-start(bf16[192,2048]{1,0:T(8,128)(2,1)} %add_convert_fusion.2), channel_id=1, source_target_pairs={{0,1},{1,0},{2,3},{3,2},{4,5},{5,4},{6,7},{7,6},{8,9},{9,8},{10,11... | collective-permute-start | bytes 2359304 | tf_op jit(solution)/shard_map/ppermute | solution.py:52
  448.5 9.3 %collective-permute-start.38 = (bf16[96,2048]{1,0:T(8,128)(2,1)S(1)}, bf16[96,2048]{1,0:T(8,128)(2,1)S(1)}, u32[]{:S(2)}, u32[]{:S(2)}) collective-permute-start(bf16[96,2048]{1,0:T(8,128)(2,1)S(1)} %slice.511), channel_id=1, source_target_pairs={{0,4},{1,5},{2,6},{3,7},{4,0},{5,1},{6,2},{7,3},{8,12},{9,13},{10,... | collective-permute-start | bytes 1179656 | tf_op jit(solution)/shard_map/ppermute | solution.py:52
  450.1 7.9 %collective-permute-start.41 = (bf16[96,2048]{1,0:T(8,128)(2,1)S(1)}, bf16[96,2048]{1,0:T(8,128)(2,1)S(1)}, u32[]{:S(2)}, u32[]{:S(2)}) collective-permute-start(bf16[96,2048]{1,0:T(8,128)(2,1)S(1)} %slice.512), channel_id=1, source_target_pairs={{0,2},{1,3},{2,0},{3,1},{4,6},{5,7},{6,4},{7,5},{8,10},{9,11},{10,... | collective-permute-start | bytes 1179656 | tf_op jit(solution)/shard_map/ppermute | solution.py:52
  450.5 8.0 %collective-permute-start.49 = (bf16[192,2048]{1,0:T(8,128)(2,1)S(1)}, bf16[192,2048]{1,0:T(8,128)(2,1)S(1)}, u32[]{:S(2)}, u32[]{:S(2)}) collective-permute-start(bf16[192,2048]{1,0:T(8,128)(2,1)S(1)} %collective-permute-done.37), channel_id=1, source_target_pairs={{0,1},{1,0},{2,3},{3,2},{4,5},{5,4},{6,7},{7,6},{8,9},{9,8},{10,11... | collective-permute-start | bytes 2359304 | tf_op jit(solution)/shard_map/ppermute | solution.py:52
  450.5 8.1 %collective-permute-start.50 = (bf16[192,2048]{1,0:T(8,128)(2,1)S(1)}, bf16[192,2048]{1,0:T(8,128)(2,1)S(1)}, u32[]{:S(2)}, u32[]{:S(2)}) collective-permute-start(bf16[192,2048]{1,0:T(8,128)(2,1)S(1)} %collective-permute-done.40), channel_id=1, source_target_pairs={{0,1},{1,0},{2,3},{3,2},{4,5},{5,4},{6,7},{7,6},{8,9},{9,8},{10,11... | collective-permute-start | bytes 2359304 | tf_op jit(solution)/shard_map/ppermute | solution.py:52
  506.9 158.0 %reduce-scatter.11.cloned.1.call-start = ((), (), s32[]{:S(2)}) async-start(), calls=%async_computation.21 | async-start | bytes 5242880 | tf_op jit(solution)/shard_map/reduce_scatter | solution.py:490
  523.7 19.7 %collective-permute-start.51 = (bf16[768,2048]{1,0:T(8,128)(2,1)}, bf16[768,2048]{1,0:T(8,128)(2,1)}, u32[]{:S(2)}, u32[]{:S(2)}) collective-permute-start(bf16[768,2048]{1,0:T(8,128)(2,1)} %convolution_convert_fusion.3), channel_id=1, source_target_pairs={{0,1},{1,0},{2,3},{3,2},{4,5},{5,4},{6,7},{7,6},{8,9},{9,8},{10,11... | collective-permute-start | bytes 9437192 | tf_op jit(solution)/shard_map/ppermute | solution.py:52
  527.9 20.8 %collective-permute-start.43 = (bf16[768,2048]{1,0:T(8,128)(2,1)}, bf16[768,2048]{1,0:T(8,128)(2,1)}, u32[]{:S(2)}, u32[]{:S(2)}) collective-permute-start(bf16[768,2048]{1,0:T(8,128)(2,1)} %convolution_convert_fusion.5), channel_id=1, source_target_pairs={{0,1},{1,0},{2,3},{3,2},{4,5},{5,4},{6,7},{7,6},{8,9},{9,8},{10,11... | collective-permute-start | bytes 9437192 | tf_op jit(solution)/shard_map/ppermute | solution.py:52
  546.6 20.5 %collective-permute-start.52 = (bf16[192,2048]{1,0:T(8,128)(2,1)S(1)}, bf16[192,2048]{1,0:T(8,128)(2,1)S(1)}, u32[]{:S(2)}, u32[]{:S(2)}) collective-permute-start(bf16[192,2048]{1,0:T(8,128)(2,1)S(1)} %pad_maximum_fusion.11), channel_id=1, source_target_pairs={{0,2},{1,3},{2,0},{3,1},{4,6},{5,7},{6,4},{7,5},{8,10},{9,11},{10,... | collective-permute-start | bytes 2359304 | tf_op jit(solution)/shard_map/ppermute | solution.py:52
  547.5 20.4 %collective-permute-start.53 = (bf16[192,2048]{1,0:T(8,128)(2,1)S(1)}, bf16[192,2048]{1,0:T(8,128)(2,1)S(1)}, u32[]{:S(2)}, u32[]{:S(2)}) collective-permute-start(bf16[192,2048]{1,0:T(8,128)(2,1)S(1)} %pad_maximum_fusion.12), channel_id=1, source_target_pairs={{0,4},{1,5},{2,6},{3,7},{4,0},{5,1},{6,2},{7,3},{8,12},{9,13},{10,... | collective-permute-start | bytes 2359304 | tf_op jit(solution)/shard_map/ppermute | solution.py:52
  550.8 33.1 %collective-permute-start.44 = (bf16[192,2048]{1,0:T(8,128)(2,1)S(1)}, bf16[192,2048]{1,0:T(8,128)(2,1)S(1)}, u32[]{:S(2)}, u32[]{:S(2)}) collective-permute-start(bf16[192,2048]{1,0:T(8,128)(2,1)S(1)} %pad_maximum_fusion.9), channel_id=1, source_target_pairs={{0,2},{1,3},{2,0},{3,1},{4,6},{5,7},{6,4},{7,5},{8,10},{9,11},{10,... | collective-permute-start | bytes 2359304 | tf_op jit(solution)/shard_map/ppermute | solution.py:52
  551.5 33.3 %collective-permute-start.45 = (bf16[192,2048]{1,0:T(8,128)(2,1)S(1)}, bf16[192,2048]{1,0:T(8,128)(2,1)S(1)}, u32[]{:S(2)}, u32[]{:S(2)}) collective-permute-start(bf16[192,2048]{1,0:T(8,128)(2,1)S(1)} %pad_maximum_fusion.10), channel_id=1, source_target_pairs={{0,4},{1,5},{2,6},{3,7},{4,0},{5,1},{6,2},{7,3},{8,12},{9,13},{10,... | collective-permute-start | bytes 2359304 | tf_op jit(solution)/shard_map/ppermute | solution.py:52
  570.6 28.9 %collective-permute-start.54 = (bf16[96,2048]{1,0:T(8,128)(2,1)}, bf16[96,2048]{1,0:T(8,128)(2,1)}, u32[]{:S(2)}, u32[]{:S(2)}) collective-permute-start(bf16[96,2048]{1,0:T(8,128)(2,1)} %get-tuple-element.110), channel_id=1, source_target_pairs={{0,4},{1,5},{2,6},{3,7},{4,0},{5,1},{6,2},{7,3},{8,12},{9,13},{10,... | collective-permute-start | bytes 1179656 | tf_op jit(solution)/shard_map/ppermute | solution.py:52
  571.8 27.7 %collective-permute-start.55 = (bf16[96,2048]{1,0:T(8,128)(2,1)}, bf16[96,2048]{1,0:T(8,128)(2,1)}, u32[]{:S(2)}, u32[]{:S(2)}) collective-permute-start(bf16[96,2048]{1,0:T(8,128)(2,1)} %get-tuple-element.111), channel_id=1, source_target_pairs={{0,2},{1,3},{2,0},{3,1},{4,6},{5,7},{6,4},{7,5},{8,10},{9,11},{10,... | collective-permute-start | bytes 1179656 | tf_op jit(solution)/shard_map/ppermute | solution.py:52
  587.5 13.1 %collective-permute-start.46 = (bf16[96,2048]{1,0:T(8,128)(2,1)}, bf16[96,2048]{1,0:T(8,128)(2,1)S(1)}, u32[]{:S(2)}, u32[]{:S(2)}) collective-permute-start(bf16[96,2048]{1,0:T(8,128)(2,1)} %get-tuple-element.96), channel_id=1, source_target_pairs={{0,4},{1,5},{2,6},{3,7},{4,0},{5,1},{6,2},{7,3},{8,12},{9,13},{10,... | collective-permute-start | bytes 1179656 | tf_op jit(solution)/shard_map/ppermute | solution.py:52
  588.7 11.9 %collective-permute-start.47 = (bf16[96,2048]{1,0:T(8,128)(2,1)}, bf16[96,2048]{1,0:T(8,128)(2,1)}, u32[]{:S(2)}, u32[]{:S(2)}) collective-permute-start(bf16[96,2048]{1,0:T(8,128)(2,1)} %get-tuple-element.97), channel_id=1, source_target_pairs={{0,2},{1,3},{2,0},{3,1},{4,6},{5,7},{6,4},{7,5},{8,10},{9,11},{10,... | collective-permute-start | bytes 1179656 | tf_op jit(solution)/shard_map/ppermute | solution.py:52
  609.3 16.8 %all-to-all-start.9 = ((f32[32,1,128]{2,1,0:T(1,128)}), f32[32,1,128]{2,1,0:T(1,128)}, u32[]{:S(2)}, u32[]{:S(2)}) async-start(f32[32,1,128]{2,1,0:T(1,128)} %reshape.397), calls=%async_computation.12 | async-start | bytes 32768 | tf_op jit(solution)/shard_map/all_to_all | solution.py:502
  626.1 38.8 %all-to-all-start.8 = ((bf16[8,64,768]{2,1,0:T(8,128)(2,1)}), bf16[8,64,768]{2,1,0:T(8,128)(2,1)}, u32[]{:S(2)}, u32[]{:S(2)}) async-start(bf16[8,64,768]{2,1,0:T(8,128)(2,1)} %bitcast.122), calls=%async_computation.11 | async-start | bytes 1572864 | tf_op jit(solution)/shard_map/all_to_all | solution.py:496
  (71 other events, 752.7 us)
Sparse Core Ops, SparseCore 0:
  9.6 30.7 all-gather.14
  41.9 62.9 all-gather.6
  106.4 79.3 all-gather.8
  187.3 79.5 all-gather.10
  268.3 79.1 all-gather.12
  349.6 75.2 reduce-scatter.4
  427.2 77.2 reduce-scatter.6
  507.0 77.9 reduce-scatter.8
  587.3 77.5 reduce-scatter.10

commit v4 on v3

--- a/solution.py
+++ b/solution.py
@@ -5,6 +5,7 @@
 import jax.numpy as jnp
 from jax import lax
 from jax.experimental import pallas as pl
+from jax.experimental.layout import Layout, with_layout_constraint
 from jax.experimental.pallas import tpu as pltpu
 from jax.sharding import PartitionSpec as P
 
@@ -381,8 +382,10 @@
         out_w.reshape(share, mine, piece, width), "kv", 0, 0, axis_index_groups=pairs
     )
     out_w = out_w.transpose(1, 0, 2, 3).reshape(wide, width)
-    gate_w = lax.all_gather(w_gate, "seq", axis=0, tiled=True)
-    up_w = lax.all_gather(w_up, "seq", axis=0, tiled=True)
+    units = w_gate.shape[1]
+    gate_up_w = jnp.concatenate([w_gate, w_up], axis=1)
+    gate_up_w = lax.all_gather(gate_up_w, "seq", axis=0, tiled=True)
+    gate_w, up_w = gate_up_w[:, :units], gate_up_w[:, units:]
     down_w = lax.all_gather(w_down, "seq", axis=1, tiled=True)
 
     gains = spread_small(spread_small(jnp.stack([gain_attn, gain_ffn]), "kv"), "seq")
@@ -485,16 +488,15 @@
     grad_w_out = grad_w_out.reshape(mine, share, piece, width).transpose(1, 0, 2, 3)
     grad_w_out = lax.all_to_all(grad_w_out, "kv", 0, 0, axis_index_groups=pairs)
     grad_w_out = grad_w_out.reshape(ring * group * piece, width // group)
-    grad_four = jnp.concatenate([dot_left(normed, dqkv).astype(BF16), grad_w_out], axis=1)
-    grad_four = lax.psum_scatter(grad_four, "seq", scatter_dimension=0, tiled=True)
-    grads_up = lax.psum_scatter(
-        dot_left(after(second_all, *normed_parts), dup).astype(BF16),
-        "seq", scatter_dimension=0, tiled=True,
-    )
-    grad_w_out = grad_four[:, 3 * wide :].reshape(piece, width).astype(F32)
-    grad_three = grad_four[:, : 3 * wide]
+    grad_three = lax.psum_scatter(
+        dot_left(normed, dqkv).astype(BF16), "seq", scatter_dimension=0, tiled=True
+    )
+    grads_up = dot_left(after(second_all, *normed_parts), dup).astype(BF16)
+    grads_last = with_layout_constraint(
+        jnp.concatenate([grads_up, grad_w_out], axis=1), Layout(major_to_minor=(0, 1))
+    )
+    grads_last = lax.psum_scatter(grads_last, "seq", scatter_dimension=0, tiled=True)
     grad_three = lax.all_to_all(grad_three.reshape(group, piece, 3 * wide), "kv", 0, 0)
-    grads_up = after(grads_up, grad_three, *ends)
     grad_three = grad_three.reshape(planes, share, piece, 3, mine, HEAD_DIM)
     grad_three = grad_three.transpose(3, 2, 1, 4, 0, 5).reshape(3, piece, width).astype(F32)
 
@@ -502,20 +504,20 @@
     scales = lax.all_to_all(scales.reshape(ring * group, piece, 2), ("seq", "kv"), 0, 0)
     scales = jnp.sum(scales, axis=0)
 
-    return (
+    early = (
         result.reshape(seqs, local, width).astype(BF16),
         grad_input.reshape(seqs, local, width),
         grad_three[0],
         grad_three[1],
         grad_three[2],
-        grad_w_out,
         scales[:, 0],
         scales[:, 1],
         grads_gate.astype(F32),
-        grads_up.astype(F32),
-        grads_down,
-        summary,
-    )
+    )
+    early, grads_last = lax.optimization_barrier((early, grads_last))
+    grad_w_out = grads_last[:, units:].reshape(piece, width).astype(F32)
+    grads_up = grads_last[:, :units].astype(F32)
+    return early[:5] + (grad_w_out,) + early[5:8] + (grads_up, grads_down, summary)
 
 
 def solution(mesh):

time: 690 us -> 675 us (0.978)
  local copies, waits for them, and re-layouts: 95.3 us -> 83.9 us
  starting transfers between devices: 69.8 us -> 62.5 us
  waiting for transfers between devices: 215 us -> 208 us
    reduce_scatter x2, waiting for transfers between devices: 27.4 us -> 12.9 us  [the longest x1 12.9 us: per_device(): lax.psum_scatter(grads_last, 'seq', scatter_dimension=0, tiled=True)]
    all_gather x1, waiting for transfers between devices: 45.3 us -> 33.7 us  [per_device(): down_w = lax.all_gather(w_down, 'seq', axis=1, tiled=True)]
    all_to_all x1, waiting for transfers between devices: 0.01 us -> 7.35 us  [per_device(): lax.all_to_all(grad_three.reshape(group, piece, 3 * wide), 'kv', 0, 0)]
    ppermute x56, waiting for transfers between devices: 117 us -> 124 us  [swap(): return lax.ppermute(values, 'kv', [(i, i ^ mask) for i in range(size)])]
    unnamed x165 -> x151, local copies, waits for them, and re-layouts: 51.1 us -> 45.8 us
  transfers between devices with their start and end apart: 73 -> 72, of which waited for: 32 -> 32; matrix products, arithmetic and copies ran while one was open for 45% -> 46% of each run, Pallas kernels for 5% -> 6%
where the time goes in v4:
time: 675 us; the launch traced here: 664 us
  waiting for transfers between devices  208 us (31%)
  matrix products  149 us (22%)
  local copies, waits for them, and re-layouts  83.9 us (12%)
  other arithmetic  82.2 us (12%)
  starting transfers between devices  62.5 us (9%)
  Pallas kernels  39.8 us (6%)
  blocking collectives  23.3 us (3%)
  between operations  15.5 us (2%)
    ppermute x56, waiting for transfers between devices, swap(): return lax.ppermute(values, 'kv', [(i, i ^ mask) for i in range(size)])  124 us
    dot_general x8, matrix products, dot_right(): lax.dot_general(left, right, (((1,), (1,)), ((), ())), preferred_element_...  55.5 us
    dot_general x8, matrix products, dot_plain(): return jnp.dot(left, right, preferred_element_type=F32)  50.9 us
    unnamed x151, local copies, waits for them, and re-layouts  45.8 us
    dot_general x5, matrix products, dot_left(): lax.dot_general(left, right, (((0,), (0,)), ((), ())), preferred_element_...  42.7 us
    all_gather x1, waiting for transfers between devices, per_device(): down_w = lax.all_gather(w_down, 'seq', axis=1, tiled=True)  33.7 us
    ppermute x56, starting transfers between devices, swap(): return lax.ppermute(values, 'kv', [(i, i ^ mask) for i in range(size)])  32.9 us
    pallas_call x1, Pallas kernels, attend_backward(): pl.pallas_call(functools.partial(backward_kernel, heads, parts, length, 1...  21.5 us
  transfers between devices with their start and end apart: 72, of which 32 were waited for; matrix products, arithmetic and copies ran while one was open for 46% of the time, Pallas kernels for 6%

profile of v4, /device:TPU:0, one launch (start us, length us, event | category | flops | bytes accessed | tf_op | source)
XLA Modules:
  0.0 664.1 jit_solution(13329488577634869280)
XLA Ops:
  13.7 17.8 %all_to_all.60 = bf16[8,64,768]{2,1,0:T(8,128)(2,1)} all-to-all(bf16[8,64,768]{2,1,0:T(8,128)(2,1)S(1)} %reshape.360), channel_id=1, replica_groups=mesh['seq'=4,'kv'=8] {'kv'}, dimensions={0} | all-to-all | bytes 1572864 | tf_op jit(solution)/shard_map/all_to_all | solution.py:378
  31.5 2.7 pad_maximum_fusion.1
  36.1 3.7 all-to-all-start.1
  40.7 2.9 fusion.37
  46.2 7.9 %all-to-all-done.1 = bf16[8,2,64]{2,1,0:T(2,128)(2,1)S(1)} async-done(((bf16[8,2,64]{2,1,0:T(2,128)(2,1)}), bf16[8,2,64]{2,1,0:T(2,128)(2,1)S(1)}, u32[]{:S(2)}, u32[]{:S(2)}) %all-to-all-start.1) | async-done | bytes 2080 | tf_op jit(solution)/shard_map/all_to_all | solution.py:127
  54.7 3.3 all-to-all-start
  59.4 3.4 all-to-all-done
  62.7 4.9 all-to-all-start.2
  79.9 6.0 collective-permute-done.2
  94.5 15.2 %collective-permute-done.9 = bf16[192,2048]{1,0:T(8,128)(2,1)} collective-permute-done((bf16[192,2048]{1,0:T(8,128)(2,1)S(1)}, bf16[192,2048]{1,0:T(8,128)(2,1)}, u32[]{:S(2)}, u32[]{:S(2)}) %collective-permute-start.9) | collective-permute-done | bytes 786464 | tf_op jit(solution)/shard_map/ppermute | solution.py:53
  113.2 4.9 fusion
  118.1 3.6 all-to-all-start.4
  123.5 6.9 %fusion.2 = bf16[1536,2048]{1,0:T(8,128)(2,1)} fusion(bf16[1536,2048]{1,0:T(8,128)(2,1)} %constant_dynamic-update-slice_fusion, f32[2048]{0:T(1024)S(1)} %mul.298, f32[1536]{0:T(1024)S(1)} %add_rsqrt_fusion), kind=kLoop, calls=%fused_computation.5 | loop fusion | flops 12582912 | bytes 12597248 | tf_op jit(solution)/shard_map/convert_element_type | solution.py:424
  130.5 6.2 convolution_convert_fusion.12.v_hbm
  136.8 7.9 %fusion.14.qk_hbm = f32[1536,512]{1,0:T(8,128)} fusion(bf16[1536,2048]{1,0:T(8,128)(2,1)} %fusion.2, bf16[2048,768]{1,0:T(8,128)(2,1)S(1)} %copy-done.43), kind=kOutput, calls=%fused_computation.41 | convolution fusion | flops 3221225472 | bytes 11534336 | tf_op jit(solution)/shard_map/dot_general | solution.py:21
  144.7 18.3 %attend_forward.1 = (bf16[1536,256]{1,0:T(8,128)(2,1)}, bf16[1536,256]{1,0:T(8,128)(2,1)}, bf16[1536,256]{1,0:T(8,128)(2,1)}, f32[1536,1]{1,0:T(8,128)}, bf16[1536,256]{1,0:T(8,128)(2,1)}) custom-call(s32[16]{0:T(128)} %pad_add_fusion.1.source, s32[6]{0:T(128)} %and_select_fusion.1.first, f32[1536,512]{1,0:T(8,128)} %fusion.14.qk_hbm, ...), custom_call_target="tpu_custom_call" | custom-call | flops 1207959552 | bytes 7077888 | tf_op jit(solution)/shard_map/attend_forward/pallas_call | solution.py:220
  163.1 3.7 convolution_convert_fusion.7
  168.4 4.5 collective-permute-done.17
  184.3 10.5 %collective-permute-done.18 = bf16[192,2048]{1,0:T(8,128)(2,1)S(1)} collective-permute-done((bf16[192,2048]{1,0:T(8,128)(2,1)S(1)}, bf16[192,2048]{1,0:T(8,128)(2,1)S(1)}, u32[]{:S(2)}, u32[]{:S(2)}) %collective-permute-start.18) | collective-permute-done | bytes 786464 | tf_op jit(solution)/shard_map/ppermute | solution.py:53
  201.5 6.3 collective-permute-done.20
  220.5 3.3 all-to-all-start.5
  225.6 5.4 all-to-all-done.5
  234.1 3.2 all-to-all-start.6
  238.3 7.4 %all-to-all-done.6 = f32[32,1,1]{2,1,0:T(1,128)} async-done(((f32[32,1,1]{2,1,0:T(1,128)}), f32[32,1,1]{2,1,0:T(1,128)}, u32[]{:S(2)}, u32[]{:S(2)}) %all-to-all-start.6) | async-done | bytes 160 | tf_op jit(solution)/shard_map/all_to_all | solution.py:439
  253.0 6.0 collective-permute-done.24
  266.8 12.2 %fusion.12 = f32[1536,1024]{1,0:T(8,128)} fusion(bf16[1536,2048]{1,0:T(8,128)(2,1)} %constant_dynamic-update-slice_fusion.10, bf16[2048,2048]{1,0:T(8,128)(2,1)} %all-gather.8.cloned.1.call-done), kind=kOutput, calls=%fused_computation.32 | convolution fusion | flops 6442450944 | bytes 16777216 | tf_op jit(solution)/shard_map/dot_general | solution.py:21
  279.0 10.2 %multiply_convert_fusion.2 = (bf16[1536,1024]{1,0:T(8,128)(2,1)S(1)}, f32[1536,1024]{1,0:T(8,128)}) fusion(f32[1536,1024]{1,0:T(8,128)} %fusion.12, bf16[1536,2048]{1,0:T(8,128)(2,1)S(1)} %copy-done.28, bf16[2048,2048]{1,0:T(8,128)(2,1)S(1)} %copy-done.41), kind=kOutput, calls=%fused_computation.10 | convolution fusion | flops 6451888128 | bytes 26214400 | tf_op jit(solution)/shard_map/dot_general | solution.py:21
  290.9 11.3 %convolution_convert_fusion.2 = bf16[2048,1024]{1,0:T(8,128)(2,1)} fusion(bf16[1536,2048]{1,0:T(8,128)(2,1)} %constant_dynamic-update-slice_fusion.20, bf16[1536,1024]{1,0:T(8,128)(2,1)S(1)} %get-tuple-element.269), kind=kOutput, calls=%fused_computation.16 | convolution fusion | flops 6444548096 | bytes 13631488 | tf_op jit(solution)/shard_map/dot_general | solution.py:25
  302.2 33.7 %all-gather.10.cloned.1.call-done = bf16[1024,2048]{1,0:T(8,128)(2,1)} async-done(((bf16[1024,512]{1,0:T(8,128)(2,1)}), bf16[1024,2048]{1,0:T(8,128)(2,1)}) %all-gather.10.cloned.1.call-update) | async-done | bytes 4194320 | tf_op jit(solution)/shard_map/all_gather | solution.py:389
  335.9 16.0 %multiply_convert_fusion = (bf16[1536,1024]{1,0:T(8,128)(2,1)S(1)}, bf16[1536,1024]{1,0:T(8,128)(2,1)S(1)}) fusion(f32[1536,1024]{1,0:T(8,128)} %fusion.12, f32[1536,1024]{1,0:T(8,128)} %get-tuple-element.270, bf16[1536,2048]{1,0:T(8,128)(2,1)} %constant_dynamic-update-slice_fusion.20, bf16[1024,2048]{1,0:T(8,128)(2,1)} %all-gather.10.cloned.1.call-done), kind=kOutput, calls=%fused_computation.8 | convolution fusion | flops 6462898176 | bytes 29360128 | tf_op jit(solution)/shard_map/dot_general | solution.py:29
  352.0 7.0 %fusion.10 = f32[768,2048]{1,0:T(8,128)S(1)} fusion(bf16[2048,2048]{1,0:T(8,128)(2,1)} %all-gather.8.cloned.1.call-done, bf16[1536,1024]{1,0:T(8,128)(2,1)S(1)} %get-tuple-element.218), kind=kOutput, calls=%fused_computation.30 | convolution fusion | flops 3221225472 | bytes 12058624 | tf_op jit(solution)/shard_map/dot_general | solution.py:29
  359.0 7.2 %add_convert_fusion.1 = bf16[768,2048]{1,0:T(8,128)(2,1)} fusion(f32[768,2048]{1,0:T(8,128)S(1)} %fusion.10, bf16[2048,2048]{1,0:T(8,128)(2,1)} %all-gather.8.cloned.1.call-done, bf16[1536,1024]{1,0:T(8,128)(2,1)S(1)} %get-tuple-element.217), kind=kOutput, calls=%fused_computation.7 | convolution fusion | flops 3224371200 | bytes 15204352 | tf_op jit(solution)/shard_map/dot_general | solution.py:29
  366.2 5.0 fusion.8
  371.2 6.5 add_convert_fusion
  377.8 10.5 %convolution_convert_fusion.1 = bf16[2048,1024]{1,0:T(8,128)(2,1)} fusion(bf16[1536,2048]{1,0:T(8,128)(2,1)S(1)} %bitcast.124, bf16[1536,1024]{1,0:T(8,128)(2,1)} %copy-done.47), kind=kOutput, calls=%fused_computation.15 | convolution fusion | flops 6444548096 | bytes 13631488 | tf_op jit(solution)/shard_map/dot_general | solution.py:25
  393.9 17.1 %collective-permute-done.33 = bf16[192,2048]{1,0:T(8,128)(2,1)S(1)} collective-permute-done((bf16[192,2048]{1,0:T(8,128)(2,1)S(1)}, bf16[192,2048]{1,0:T(8,128)(2,1)S(1)}, u32[]{:S(2)}, u32[]{:S(2)}) %collective-permute-start.33) | collective-permute-done | bytes 786464 | tf_op jit(solution)/shard_map/ppermute | solution.py:53
  415.6 8.3 %collective-permute-done.35 = bf16[96,2048]{1,0:T(8,128)(2,1)S(1)} collective-permute-done((bf16[96,2048]{1,0:T(8,128)(2,1)S(1)}, bf16[96,2048]{1,0:T(8,128)(2,1)S(1)}, u32[]{:S(2)}, u32[]{:S(2)}) %collective-permute-start.35) | collective-permute-done | bytes 393248 | tf_op jit(solution)/shard_map/ppermute | solution.py:53
  432.3 14.7 %collective-permute-done.37 = bf16[192,2048]{1,0:T(8,128)(2,1)S(1)} collective-permute-done((bf16[192,2048]{1,0:T(8,128)(2,1)}, bf16[192,2048]{1,0:T(8,128)(2,1)S(1)}, u32[]{:S(2)}, u32[]{:S(2)}) %collective-permute-start.37) | collective-permute-done | bytes 786464 | tf_op jit(solution)/shard_map/ppermute | solution.py:53
  450.1 5.8 collective-permute-done.38
  458.2 2.9 convolution_convert_fusion.11.g_hbm
  461.2 21.5 %attend_backward.1 = bf16[1536,768]{1,0:T(8,128)(2,1)} custom-call(s32[16]{0:T(128)} %pad_add_fusion.1.source, s32[6]{0:T(128)} %and_select_fusion.last, bf16[1536,256]{1,0:T(8,128)(2,1)} %get-tuple-element.108.q_ref, bf16[1536,256]{1,0:T(8,128)(2,1)} %get-tuple-element.109.k_ref, bf16[1536,256]{1,0:T(8,128)(2,1)} %get-tuple-element.110.v_ref, ...), custom_call_target="tpu_custom_call" | custom-call | flops 3019898880 | bytes 5505024 | tf_op jit(solution)/shard_map/attend_backward/pallas_call | solution.py:320
  482.7 9.2 %convolution_convert_fusion.9 = bf16[2048,768]{1,0:T(8,128)(2,1)} fusion(bf16[1536,2048]{1,0:T(8,128)(2,1)} %fusion.2, bf16[1536,768]{1,0:T(8,128)(2,1)} %attend_backward.1), kind=kOutput, calls=%fused_computation.23 | convolution fusion | flops 4833411072 | bytes 11796480 | tf_op jit(solution)/shard_map/dot_general | solution.py:25
  491.9 3.3 fusion.40
  495.2 6.7 %convolution_convert_fusion.4 = bf16[768,2048]{1,0:T(8,128)(2,1)} fusion(bf16[768,768]{1,0:T(8,128)(2,1)} %get-tuple-element.112, bf16[2048,768]{1,0:T(8,128)(2,1)} %all-gather.6.cloned.1.call-done), kind=kOutput, calls=%fused_computation.18 | convolution fusion | flops 2417491968 | bytes 7471104 | tf_op jit(solution)/shard_map/dot_general | solution.py:29
  501.9 4.1 convolution_convert_fusion.3
  507.9 5.5 all_to_all.61
  515.8 10.0 %convolution_convert_fusion = bf16[2048,1024]{1,0:T(8,128)(2,1)S(1)} fusion(bf16[1536,2048]{1,0:T(8,128)(2,1)} %constant_dynamic-update-slice_fusion.10, bf16[1536,1024]{1,0:T(8,128)(2,1)} %copy-done.48), kind=kOutput, calls=%fused_computation.14 | convolution fusion | flops 6444548096 | bytes 13631488 | tf_op jit(solution)/shard_map/dot_general | solution.py:25
  525.8 2.9 pad_maximum_fusion
  531.8 4.8 convolution_convert_fusion.5
  536.7 4.8 convolution_convert_fusion.6
  542.8 2.8 add_convert_fusion.9
  557.0 2.9 copy.84
  559.8 2.8 convert_element_type.728
  562.6 5.6 collective-permute-done.52
  573.2 11.9 %collective-permute-done.44 = bf16[192,2048]{1,0:T(8,128)(2,1)} collective-permute-done((bf16[192,2048]{1,0:T(8,128)(2,1)}, bf16[192,2048]{1,0:T(8,128)(2,1)}, u32[]{:S(2)}, u32[]{:S(2)}) %collective-permute-start.44) | collective-permute-done | bytes 786464 | tf_op jit(solution)/shard_map/ppermute | solution.py:53
  586.3 2.9 add_convert_fusion.14
  590.8 3.8 collective-permute-done.54
  603.0 3.4 all-to-all-start.8
  607.3 3.5 add_bitcast_fusion.1
  613.2 2.6 all-to-all-done.8
  615.8 3.5 all-to-all-start.7
  624.5 7.4 %all-to-all-done.7 = bf16[8,64,768]{2,1,0:T(8,128)(2,1)S(1)} async-done(((bf16[8,64,768]{2,1,0:T(8,128)(2,1)}), bf16[8,64,768]{2,1,0:T(8,128)(2,1)S(1)}, u32[]{:S(2)}, u32[]{:S(2)}) %all-to-all-start.7) | async-done | bytes 786464 | tf_op jit(solution)/shard_map/all_to_all | solution.py:499
  639.5 12.9 %reduce-scatter.11.cloned.1.call-done = bf16[512,1280]{1,0:T(8,128)(2,1)} async-done(((bf16[2048,1280]{1,0:T(8,128)(2,1)}), bf16[512,1280]{1,0:T(8,128)(2,1)}) %reduce-scatter.11.cloned.1.call-update) | async-done | bytes 1310736 | tf_op jit(solution)/shard_map/reduce_scatter | solution.py:498
  652.4 2.8 slice_convert_fusion
  (381 shorter events, 172.5 us)
Async XLA Ops:
  7.2 110.9 %all-gather.12.cloned.1.call-start = ((), (), s32[]{:S(2)}) async-start(), calls=%async_computation.21 | async-start | bytes 1310720 | tf_op jit(solution)/shard_map/all_gather | solution.py:380
  7.9 122.6 %all-gather.6.cloned.1.call-start = ((), (), s32[]{:S(2)}) async-start(), calls=%async_computation.14 | async-start | bytes 3932160 | tf_op jit(solution)/shard_map/all_gather | solution.py:379
  31.5 235.3 %all-gather.8.cloned.1.call-start = ((), (), s32[]{:S(2)}) async-start(), calls=%async_computation.15 | async-start | bytes 10485760 | tf_op jit(solution)/shard_map/all_gather | solution.py:387
  34.3 39.4 %collective-permute-start = (bf16[192,2048]{1,0:T(8,128)(2,1)S(1)}, bf16[192,2048]{1,0:T(8,128)(2,1)}, u32[]{:S(2)}, u32[]{:S(2)}) collective-permute-start(bf16[192,2048]{1,0:T(8,128)(2,1)S(1)} %bitcast.95), channel_id=1, source_target_pairs={{0,2},{1,3},{2,0},{3,1},{4,6},{5,7},{6,4},{7,5},{8,10},{9,11},{10,... | collective-permute-start | bytes 2359304 | tf_op jit(solution)/shard_map/ppermute | solution.py:53
  34.9 41.2 %collective-permute-start.1 = (bf16[192,2048]{1,0:T(8,128)(2,1)S(1)}, bf16[192,2048]{1,0:T(8,128)(2,1)S(1)}, u32[]{:S(2)}, u32[]{:S(2)}) collective-permute-start(bf16[192,2048]{1,0:T(8,128)(2,1)S(1)} %bitcast.96), channel_id=1, source_target_pairs={{0,4},{1,5},{2,6},{3,7},{4,0},{5,1},{6,2},{7,3},{8,12},{9,13},{10,... | collective-permute-start | bytes 2359304 | tf_op jit(solution)/shard_map/ppermute | solution.py:53
  35.5 52.5 %collective-permute-start.4 = (bf16[192,2048]{1,0:T(8,128)(2,1)S(1)}, bf16[192,2048]{1,0:T(8,128)(2,1)}, u32[]{:S(2)}, u32[]{:S(2)}) collective-permute-start(bf16[192,2048]{1,0:T(8,128)(2,1)S(1)} %bitcast.97), channel_id=1, source_target_pairs={{0,1},{1,0},{2,3},{3,2},{4,5},{5,4},{6,7},{7,6},{8,9},{9,8},{10,11... | collective-permute-start | bytes 2359304 | tf_op jit(solution)/shard_map/ppermute | solution.py:53
  36.1 18.0 %all-to-all-start.1 = ((bf16[8,2,64]{2,1,0:T(2,128)(2,1)}), bf16[8,2,64]{2,1,0:T(2,128)(2,1)S(1)}, u32[]{:S(2)}, u32[]{:S(2)}) async-start(bf16[8,2,64]{2,1,0:T(2,128)(2,1)} %broadcast_in_dim.9), calls=%async_computation.1 | async-start | bytes 8192 | tf_op jit(solution)/shard_map/all_to_all | solution.py:127
  54.7 8.0 %all-to-all-start = ((s32[8,1,192]{2,1,0:T(1,128)}), s32[8,1,192]{2,1,0:T(1,128)S(1)}, u32[]{:S(2)}, u32[]{:S(2)}) async-start(s32[8,1,192]{2,1,0:T(1,128)} %broadcast_in_dim.8), calls=%async_computation | async-start | bytes 16384 | tf_op jit(solution)/shard_map/all_to_all | solution.py:127
  62.7 10.7 %all-to-all-start.2 = ((bf16[4,2,512]{2,1,0:T(2,128)(2,1)}), bf16[4,2,512]{2,1,0:T(2,128)(2,1)S(1)}, u32[]{:S(2)}, u32[]{:S(2)}) async-start(bf16[4,2,512]{2,1,0:T(2,128)(2,1)} %reshape.395), calls=%async_computation.2 | async-start | bytes 16384 | tf_op jit(solution)/shard_map/all_to_all | solution.py:127
  74.8 11.1 %collective-permute-start.2 = (bf16[96,2048]{1,0:T(8,128)(2,1)S(1)}, bf16[96,2048]{1,0:T(8,128)(2,1)S(1)}, u32[]{:S(2)}, u32[]{:S(2)}) collective-permute-start(bf16[96,2048]{1,0:T(8,128)(2,1)S(1)} %slice.472), channel_id=1, source_target_pairs={{0,4},{1,5},{2,6},{3,7},{4,0},{5,1},{6,2},{7,3},{8,12},{9,13},{10,... | collective-permute-start | bytes 1179656 | tf_op jit(solution)/shard_map/ppermute | solution.py:53
  76.2 10.5 %collective-permute-start.3 = (bf16[96,2048]{1,0:T(8,128)(2,1)S(1)}, bf16[96,2048]{1,0:T(8,128)(2,1)S(1)}, u32[]{:S(2)}, u32[]{:S(2)}) collective-permute-start(bf16[96,2048]{1,0:T(8,128)(2,1)S(1)} %slice.473), channel_id=1, source_target_pairs={{0,2},{1,3},{2,0},{3,1},{4,6},{5,7},{6,4},{7,5},{8,10},{9,11},{10,... | collective-permute-start | bytes 1179656 | tf_op jit(solution)/shard_map/ppermute | solution.py:53
  76.3 14.7 %collective-permute-start.5 = (bf16[192,2048]{1,0:T(8,128)(2,1)}, bf16[192,2048]{1,0:T(8,128)(2,1)S(1)}, u32[]{:S(2)}, u32[]{:S(2)}) collective-permute-start(bf16[192,2048]{1,0:T(8,128)(2,1)} %collective-permute-done), channel_id=1, source_target_pairs={{0,1},{1,0},{2,3},{3,2},{4,5},{5,4},{6,7},{7,6},{8,9},{9,8},{10,11... | collective-permute-start | bytes 2359304 | tf_op jit(solution)/shard_map/ppermute | solution.py:53
  76.3 15.6 %collective-permute-start.6 = (bf16[192,2048]{1,0:T(8,128)(2,1)S(1)}, bf16[192,2048]{1,0:T(8,128)(2,1)S(1)}, u32[]{:S(2)}, u32[]{:S(2)}) collective-permute-start(bf16[192,2048]{1,0:T(8,128)(2,1)S(1)} %collective-permute-done.1), channel_id=1, source_target_pairs={{0,1},{1,0},{2,3},{3,2},{4,5},{5,4},{6,7},{7,6},{8,9},{9,8},{10,11... | collective-permute-start | bytes 2359304 | tf_op jit(solution)/shard_map/ppermute | solution.py:53
  90.1 19.6 %collective-permute-start.9 = (bf16[192,2048]{1,0:T(8,128)(2,1)S(1)}, bf16[192,2048]{1,0:T(8,128)(2,1)}, u32[]{:S(2)}, u32[]{:S(2)}) collective-permute-start(bf16[192,2048]{1,0:T(8,128)(2,1)S(1)} %bitcast.111), channel_id=1, source_target_pairs={{0,2},{1,3},{2,0},{3,1},{4,6},{5,7},{6,4},{7,5},{8,10},{9,11},{10,... | collective-permute-start | bytes 2359304 | tf_op jit(solution)/shard_map/ppermute | solution.py:53
  90.1 21.7 %collective-permute-start.11 = (bf16[192,2048]{1,0:T(8,128)(2,1)S(1)}, bf16[192,2048]{1,0:T(8,128)(2,1)}, u32[]{:S(2)}, u32[]{:S(2)}) collective-permute-start(bf16[192,2048]{1,0:T(8,128)(2,1)S(1)} %bitcast.112), channel_id=1, source_target_pairs={{0,4},{1,5},{2,6},{3,7},{4,0},{5,1},{6,2},{7,3},{8,12},{9,13},{10,... | collective-permute-start | bytes 2359304 | tf_op jit(solution)/shard_map/ppermute | solution.py:53
  110.7 11.9 %collective-permute-start.13 = (bf16[96,2048]{1,0:T(8,128)(2,1)S(1)}, bf16[96,2048]{1,0:T(8,128)(2,1)}, u32[]{:S(2)}, u32[]{:S(2)}) collective-permute-start(bf16[96,2048]{1,0:T(8,128)(2,1)S(1)} %slice.475), channel_id=1, source_target_pairs={{0,4},{1,5},{2,6},{3,7},{4,0},{5,1},{6,2},{7,3},{8,12},{9,13},{10,... | collective-permute-start | bytes 1179656 | tf_op jit(solution)/shard_map/ppermute | solution.py:53
  112.9 10.5 %collective-permute-start.15 = (bf16[96,2048]{1,0:T(8,128)(2,1)S(1)}, bf16[96,2048]{1,0:T(8,128)(2,1)}, u32[]{:S(2)}, u32[]{:S(2)}) collective-permute-start(bf16[96,2048]{1,0:T(8,128)(2,1)S(1)} %slice.476), channel_id=1, source_target_pairs={{0,2},{1,3},{2,0},{3,1},{4,6},{5,7},{6,4},{7,5},{8,10},{9,11},{10,... | collective-permute-start | bytes 1179656 | tf_op jit(solution)/shard_map/ppermute | solution.py:53
  118.1 12.2 %all-to-all-start.4 = ((bf16[2,2,64,2048]{3,2,1,0:T(8,128)(2,1)}), bf16[2,2,64,2048]{3,2,1,0:T(8,128)(2,1)S(1)}, u32[]{:S(2)}, u32[]{:S(2)}) async-start(bf16[2,2,64,2048]{3,2,1,0:T(8,128)(2,1)} %bitcast.120), calls=%async_computation.4 | async-start | bytes 2097152 | tf_op jit(solution)/shard_map/all_to_all | solution.py:381
  121.7 214.2 %all-gather.10.cloned.1.call-start = ((), (), s32[]{:S(2)}) async-start(), calls=%async_computation.16 | async-start | bytes 5242880 | tf_op jit(solution)/shard_map/all_gather | solution.py:389
  122.0 8.5 %collective-permute-start.10 = (bf16[192,2048]{1,0:T(8,128)(2,1)}, bf16[192,2048]{1,0:T(8,128)(2,1)}, u32[]{:S(2)}, u32[]{:S(2)}) collective-permute-start(bf16[192,2048]{1,0:T(8,128)(2,1)} %collective-permute-done.9), channel_id=1, source_target_pairs={{0,1},{1,0},{2,3},{3,2},{4,5},{5,4},{6,7},{7,6},{8,9},{9,8},{10,11... | collective-permute-start | bytes 2359304 | tf_op jit(solution)/shard_map/ppermute | solution.py:53
  122.5 8.0 %collective-permute-start.12 = (bf16[192,2048]{1,0:T(8,128)(2,1)}, bf16[192,2048]{1,0:T(8,128)(2,1)}, u32[]{:S(2)}, u32[]{:S(2)}) collective-permute-start(bf16[192,2048]{1,0:T(8,128)(2,1)} %collective-permute-done.11), channel_id=1, source_target_pairs={{0,1},{1,0},{2,3},{3,2},{4,5},{5,4},{6,7},{7,6},{8,9},{9,8},{10,11... | collective-permute-start | bytes 2359304 | tf_op jit(solution)/shard_map/ppermute | solution.py:53
  122.6 7.9 %collective-permute-start.14 = (bf16[96,2048]{1,0:T(8,128)(2,1)}, bf16[96,2048]{1,0:T(8,128)(2,1)}, u32[]{:S(2)}, u32[]{:S(2)}) collective-permute-start(bf16[96,2048]{1,0:T(8,128)(2,1)} %collective-permute-done.13), channel_id=1, source_target_pairs={{0,1},{1,0},{2,3},{3,2},{4,5},{5,4},{6,7},{7,6},{8,9},{9,8},{10,11... | collective-permute-start | bytes 1179656 | tf_op jit(solution)/shard_map/ppermute | solution.py:53
  174.9 19.9 %collective-permute-start.18 = (bf16[192,2048]{1,0:T(8,128)(2,1)S(1)}, bf16[192,2048]{1,0:T(8,128)(2,1)S(1)}, u32[]{:S(2)}, u32[]{:S(2)}) collective-permute-start(bf16[192,2048]{1,0:T(8,128)(2,1)S(1)} %pad_maximum_fusion.6), channel_id=1, source_target_pairs={{0,2},{1,3},{2,0},{3,1},{4,6},{5,7},{6,4},{7,5},{8,10},{9,11},{10,... | collective-permute-start | bytes 2359304 | tf_op jit(solution)/shard_map/ppermute | solution.py:53
  176.3 19.5 %collective-permute-start.19 = (bf16[192,2048]{1,0:T(8,128)(2,1)S(1)}, bf16[192,2048]{1,0:T(8,128)(2,1)S(1)}, u32[]{:S(2)}, u32[]{:S(2)}) collective-permute-start(bf16[192,2048]{1,0:T(8,128)(2,1)S(1)} %pad_maximum_fusion.7), channel_id=1, source_target_pairs={{0,4},{1,5},{2,6},{3,7},{4,0},{5,1},{6,2},{7,3},{8,12},{9,13},{10,... | collective-permute-start | bytes 2359304 | tf_op jit(solution)/shard_map/ppermute | solution.py:53
  178.3 22.3 %collective-permute-start.31 = (bf16[192,2048]{1,0:T(8,128)(2,1)S(1)}, bf16[192,2048]{1,0:T(8,128)(2,1)S(1)}, u32[]{:S(2)}, u32[]{:S(2)}) collective-permute-start(bf16[192,2048]{1,0:T(8,128)(2,1)S(1)} %bitcast.114), channel_id=1, source_target_pairs={{0,1},{1,0},{2,3},{3,2},{4,5},{5,4},{6,7},{7,6},{8,9},{9,8},{10,11... | collective-permute-start | bytes 2359304 | tf_op jit(solution)/shard_map/ppermute | solution.py:53
  197.4 10.4 %collective-permute-start.20 = (bf16[96,2048]{1,0:T(8,128)(2,1)S(1)}, bf16[96,2048]{1,0:T(8,128)(2,1)S(1)}, u32[]{:S(2)}, u32[]{:S(2)}) collective-permute-start(bf16[96,2048]{1,0:T(8,128)(2,1)S(1)} %get-tuple-element.79), channel_id=1, source_target_pairs={{0,4},{1,5},{2,6},{3,7},{4,0},{5,1},{6,2},{7,3},{8,12},{9,13},{10,... | collective-permute-start | bytes 1179656 | tf_op jit(solution)/shard_map/ppermute | solution.py:53
  198.4 10.1 %collective-permute-start.21 = (bf16[96,2048]{1,0:T(8,128)(2,1)S(1)}, bf16[96,2048]{1,0:T(8,128)(2,1)S(1)}, u32[]{:S(2)}, u32[]{:S(2)}) collective-permute-start(bf16[96,2048]{1,0:T(8,128)(2,1)S(1)} %get-tuple-element.80), channel_id=1, source_target_pairs={{0,2},{1,3},{2,0},{3,1},{4,6},{5,7},{6,4},{7,5},{8,10},{9,11},{10,... | collective-permute-start | bytes 1179656 | tf_op jit(solution)/shard_map/ppermute | solution.py:53
  212.4 34.6 %collective-permute-start.22 = (bf16[192,2048]{1,0:T(8,128)(2,1)}, bf16[192,2048]{1,0:T(8,128)(2,1)}, u32[]{:S(2)}, u32[]{:S(2)}) collective-permute-start(bf16[192,2048]{1,0:T(8,128)(2,1)} %get-tuple-element.216), channel_id=1, source_target_pairs={{0,2},{1,3},{2,0},{3,1},{4,6},{5,7},{6,4},{7,5},{8,10},{9,11},{10,... | collective-permute-start | bytes 2359304 | tf_op jit(solution)/shard_map/ppermute | solution.py:53
  213.0 35.9 %collective-permute-start.23 = (bf16[192,2048]{1,0:T(8,128)(2,1)}, bf16[192,2048]{1,0:T(8,128)(2,1)S(1)}, u32[]{:S(2)}, u32[]{:S(2)}) collective-permute-start(bf16[192,2048]{1,0:T(8,128)(2,1)} %get-tuple-element.216), channel_id=1, source_target_pairs={{0,4},{1,5},{2,6},{3,7},{4,0},{5,1},{6,2},{7,3},{8,12},{9,13},{10,... | collective-permute-start | bytes 2359304 | tf_op jit(solution)/shard_map/ppermute | solution.py:53
  220.5 10.5 %all-to-all-start.5 = ((f32[8,1,192]{2,1,0:T(1,128)}), f32[8,1,192]{2,1,0:T(1,128)S(1)}, u32[]{:S(2)}, u32[]{:S(2)}) async-start(f32[8,1,192]{2,1,0:T(1,128)} %all_to_all.49), calls=%async_computation.5 | async-start | bytes 16384 | tf_op jit(solution)/shard_map/all_to_all | solution.py:436
  234.1 11.6 %all-to-all-start.6 = ((f32[32,1,1]{2,1,0:T(1,128)}), f32[32,1,1]{2,1,0:T(1,128)}, u32[]{:S(2)}, u32[]{:S(2)}) async-start(f32[32,1,1]{2,1,0:T(1,128)} %broadcast_in_dim.11), calls=%async_computation.6 | async-start | bytes 32768 | tf_op jit(solution)/shard_map/all_to_all | solution.py:439
  237.4 191.7 %reduce-scatter.5.cloned.1.call-start = ((), (), s32[]{:S(2)}) async-start(), calls=%async_computation.17 | async-start | bytes 5242880 | tf_op jit(solution)/shard_map/reduce_scatter | solution.py:446
  238.2 22.9 %collective-permute-start.26 = (bf16[192,2048]{1,0:T(8,128)(2,1)}, bf16[192,2048]{1,0:T(8,128)(2,1)}, u32[]{:S(2)}, u32[]{:S(2)}) collective-permute-start(bf16[192,2048]{1,0:T(8,128)(2,1)} %get-tuple-element.216), channel_id=1, source_target_pairs={{0,1},{1,0},{2,3},{3,2},{4,5},{5,4},{6,7},{7,6},{8,9},{9,8},{10,11... | collective-permute-start | bytes 2359304 | tf_op jit(solution)/shard_map/ppermute | solution.py:53
  248.1 11.0 %collective-permute-start.24 = (bf16[96,2048]{1,0:T(8,128)(2,1)S(1)}, bf16[96,2048]{1,0:T(8,128)(2,1)S(1)}, u32[]{:S(2)}, u32[]{:S(2)}) collective-permute-start(bf16[96,2048]{1,0:T(8,128)(2,1)S(1)} %slice.496), channel_id=1, source_target_pairs={{0,4},{1,5},{2,6},{3,7},{4,0},{5,1},{6,2},{7,3},{8,12},{9,13},{10,... | collective-permute-start | bytes 1179656 | tf_op jit(solution)/shard_map/ppermute | solution.py:53
  248.9 10.9 %collective-permute-start.25 = (bf16[96,2048]{1,0:T(8,128)(2,1)S(1)}, bf16[96,2048]{1,0:T(8,128)(2,1)S(1)}, u32[]{:S(2)}, u32[]{:S(2)}) collective-permute-start(bf16[96,2048]{1,0:T(8,128)(2,1)S(1)} %slice.497), channel_id=1, source_target_pairs={{0,2},{1,3},{2,0},{3,1},{4,6},{5,7},{6,4},{7,5},{8,10},{9,11},{10,... | collective-permute-start | bytes 1179656 | tf_op jit(solution)/shard_map/ppermute | solution.py:53
  249.5 13.8 %collective-permute-start.27 = (bf16[192,2048]{1,0:T(8,128)(2,1)}, bf16[192,2048]{1,0:T(8,128)(2,1)S(1)}, u32[]{:S(2)}, u32[]{:S(2)}) collective-permute-start(bf16[192,2048]{1,0:T(8,128)(2,1)} %collective-permute-done.22), channel_id=1, source_target_pairs={{0,1},{1,0},{2,3},{3,2},{4,5},{5,4},{6,7},{7,6},{8,9},{9,8},{10,11... | collective-permute-start | bytes 2359304 | tf_op jit(solution)/shard_map/ppermute | solution.py:53
  249.5 14.8 %collective-permute-start.28 = (bf16[192,2048]{1,0:T(8,128)(2,1)S(1)}, bf16[192,2048]{1,0:T(8,128)(2,1)S(1)}, u32[]{:S(2)}, u32[]{:S(2)}) collective-permute-start(bf16[192,2048]{1,0:T(8,128)(2,1)S(1)} %collective-permute-done.23), channel_id=1, source_target_pairs={{0,1},{1,0},{2,3},{3,2},{4,5},{5,4},{6,7},{7,6},{8,9},{9,8},{10,11... | collective-permute-start | bytes 2359304 | tf_op jit(solution)/shard_map/ppermute | solution.py:53
  302.1 193.0 %reduce-scatter.7.cloned.1.call-start = ((), (), s32[]{:S(2)}) async-start(), calls=%async_computation.18 | async-start | bytes 5242880 | tf_op jit(solution)/shard_map/reduce_scatter | solution.py:462
  366.2 22.2 %collective-permute-start.32 = (bf16[768,2048]{1,0:T(8,128)(2,1)}, bf16[768,2048]{1,0:T(8,128)(2,1)}, u32[]{:S(2)}, u32[]{:S(2)}) collective-permute-start(bf16[768,2048]{1,0:T(8,128)(2,1)} %add_convert_fusion.1), channel_id=1, source_target_pairs={{0,1},{1,0},{2,3},{3,2},{4,5},{5,4},{6,7},{7,6},{8,9},{9,8},{10,11... | collective-permute-start | bytes 9437192 | tf_op jit(solution)/shard_map/ppermute | solution.py:53
  388.3 227.5 %reduce-scatter.9.cloned.1.call-start = ((), (), s32[]{:S(2)}) async-start(), calls=%async_computation.19 | async-start | bytes 3932160 | tf_op jit(solution)/shard_map/reduce_scatter | solution.py:491
  391.1 19.9 %collective-permute-start.33 = (bf16[192,2048]{1,0:T(8,128)(2,1)S(1)}, bf16[192,2048]{1,0:T(8,128)(2,1)S(1)}, u32[]{:S(2)}, u32[]{:S(2)}) collective-permute-start(bf16[192,2048]{1,0:T(8,128)(2,1)S(1)} %pad_maximum_fusion.8), channel_id=1, source_target_pairs={{0,2},{1,3},{2,0},{3,1},{4,6},{5,7},{6,4},{7,5},{8,10},{9,11},{10,... | collective-permute-start | bytes 2359304 | tf_op jit(solution)/shard_map/ppermute | solution.py:53
  392.5 19.5 %collective-permute-start.34 = (bf16[192,2048]{1,0:T(8,128)(2,1)S(1)}, bf16[192,2048]{1,0:T(8,128)(2,1)S(1)}, u32[]{:S(2)}, u32[]{:S(2)}) collective-permute-start(bf16[192,2048]{1,0:T(8,128)(2,1)S(1)} %pad_maximum_fusion.9), channel_id=1, source_target_pairs={{0,4},{1,5},{2,6},{3,7},{4,0},{5,1},{6,2},{7,3},{8,12},{9,13},{10,... | collective-permute-start | bytes 2359304 | tf_op jit(solution)/shard_map/ppermute | solution.py:53
  413.5 10.4 %collective-permute-start.35 = (bf16[96,2048]{1,0:T(8,128)(2,1)S(1)}, bf16[96,2048]{1,0:T(8,128)(2,1)S(1)}, u32[]{:S(2)}, u32[]{:S(2)}) collective-permute-start(bf16[96,2048]{1,0:T(8,128)(2,1)S(1)} %get-tuple-element.92), channel_id=1, source_target_pairs={{0,4},{1,5},{2,6},{3,7},{4,0},{5,1},{6,2},{7,3},{8,12},{9,13},{10,... | collective-permute-start | bytes 1179656 | tf_op jit(solution)/shard_map/ppermute | solution.py:53
  415.1 10.1 %collective-permute-start.36 = (bf16[96,2048]{1,0:T(8,128)(2,1)S(1)}, bf16[96,2048]{1,0:T(8,128)(2,1)S(1)}, u32[]{:S(2)}, u32[]{:S(2)}) collective-permute-start(bf16[96,2048]{1,0:T(8,128)(2,1)S(1)} %get-tuple-element.93), channel_id=1, source_target_pairs={{0,2},{1,3},{2,0},{3,1},{4,6},{5,7},{6,4},{7,5},{8,10},{9,11},{10,... | collective-permute-start | bytes 1179656 | tf_op jit(solution)/shard_map/ppermute | solution.py:53
  429.1 17.9 %collective-permute-start.37 = (bf16[192,2048]{1,0:T(8,128)(2,1)}, bf16[192,2048]{1,0:T(8,128)(2,1)S(1)}, u32[]{:S(2)}, u32[]{:S(2)}) collective-permute-start(bf16[192,2048]{1,0:T(8,128)(2,1)} %add_convert_fusion.2), channel_id=1, source_target_pairs={{0,2},{1,3},{2,0},{3,1},{4,6},{5,7},{6,4},{7,5},{8,10},{9,11},{10,... | collective-permute-start | bytes 2359304 | tf_op jit(solution)/shard_map/ppermute | solution.py:53
  429.7 18.2 %collective-permute-start.40 = (bf16[192,2048]{1,0:T(8,128)(2,1)}, bf16[192,2048]{1,0:T(8,128)(2,1)S(1)}, u32[]{:S(2)}, u32[]{:S(2)}) collective-permute-start(bf16[192,2048]{1,0:T(8,128)(2,1)} %add_convert_fusion.2), channel_id=1, source_target_pairs={{0,4},{1,5},{2,6},{3,7},{4,0},{5,1},{6,2},{7,3},{8,12},{9,13},{10,... | collective-permute-start | bytes 2359304 | tf_op jit(solution)/shard_map/ppermute | solution.py:53
  431.0 25.5 %collective-permute-start.48 = (bf16[192,2048]{1,0:T(8,128)(2,1)}, bf16[192,2048]{1,0:T(8,128)(2,1)S(1)}, u32[]{:S(2)}, u32[]{:S(2)}) collective-permute-start(bf16[192,2048]{1,0:T(8,128)(2,1)} %add_convert_fusion.2), channel_id=1, source_target_pairs={{0,1},{1,0},{2,3},{3,2},{4,5},{5,4},{6,7},{7,6},{8,9},{9,8},{10,11... | collective-permute-start | bytes 2359304 | tf_op jit(solution)/shard_map/ppermute | solution.py:53
  447.0 8.9 %collective-permute-start.38 = (bf16[96,2048]{1,0:T(8,128)(2,1)S(1)}, bf16[96,2048]{1,0:T(8,128)(2,1)S(1)}, u32[]{:S(2)}, u32[]{:S(2)}) collective-permute-start(bf16[96,2048]{1,0:T(8,128)(2,1)S(1)} %slice.521), channel_id=1, source_target_pairs={{0,4},{1,5},{2,6},{3,7},{4,0},{5,1},{6,2},{7,3},{8,12},{9,13},{10,... | collective-permute-start | bytes 1179656 | tf_op jit(solution)/shard_map/ppermute | solution.py:53
  447.9 8.5 %collective-permute-start.41 = (bf16[96,2048]{1,0:T(8,128)(2,1)S(1)}, bf16[96,2048]{1,0:T(8,128)(2,1)S(1)}, u32[]{:S(2)}, u32[]{:S(2)}) collective-permute-start(bf16[96,2048]{1,0:T(8,128)(2,1)S(1)} %slice.522), channel_id=1, source_target_pairs={{0,2},{1,3},{2,0},{3,1},{4,6},{5,7},{6,4},{7,5},{8,10},{9,11},{10,... | collective-permute-start | bytes 1179656 | tf_op jit(solution)/shard_map/ppermute | solution.py:53
  449.4 7.2 %collective-permute-start.49 = (bf16[192,2048]{1,0:T(8,128)(2,1)S(1)}, bf16[192,2048]{1,0:T(8,128)(2,1)S(1)}, u32[]{:S(2)}, u32[]{:S(2)}) collective-permute-start(bf16[192,2048]{1,0:T(8,128)(2,1)S(1)} %collective-permute-done.37), channel_id=1, source_target_pairs={{0,1},{1,0},{2,3},{3,2},{4,5},{5,4},{6,7},{7,6},{8,9},{9,8},{10,11... | collective-permute-start | bytes 2359304 | tf_op jit(solution)/shard_map/ppermute | solution.py:53
  449.4 7.2 %collective-permute-start.50 = (bf16[192,2048]{1,0:T(8,128)(2,1)S(1)}, bf16[192,2048]{1,0:T(8,128)(2,1)S(1)}, u32[]{:S(2)}, u32[]{:S(2)}) collective-permute-start(bf16[192,2048]{1,0:T(8,128)(2,1)S(1)} %collective-permute-done.40), channel_id=1, source_target_pairs={{0,1},{1,0},{2,3},{3,2},{4,5},{5,4},{6,7},{7,6},{8,9},{9,8},{10,11... | collective-permute-start | bytes 2359304 | tf_op jit(solution)/shard_map/ppermute | solution.py:53
  491.8 160.6 %reduce-scatter.11.cloned.1.call-start = ((), (), s32[]{:S(2)}) async-start(), calls=%async_computation.20 | async-start | bytes 6553600 | tf_op jit(solution)/shard_map/reduce_scatter | solution.py:498
  528.7 14.1 %collective-permute-start.51 = (bf16[768,2048]{1,0:T(8,128)(2,1)}, bf16[768,2048]{1,0:T(8,128)(2,1)}, u32[]{:S(2)}, u32[]{:S(2)}) collective-permute-start(bf16[768,2048]{1,0:T(8,128)(2,1)} %convolution_convert_fusion.3), channel_id=1, source_target_pairs={{0,1},{1,0},{2,3},{3,2},{4,5},{5,4},{6,7},{7,6},{8,9},{9,8},{10,11... | collective-permute-start | bytes 9437192 | tf_op jit(solution)/shard_map/ppermute | solution.py:53
  536.6 12.8 %collective-permute-start.43 = (bf16[768,2048]{1,0:T(8,128)(2,1)}, bf16[768,2048]{1,0:T(8,128)(2,1)}, u32[]{:S(2)}, u32[]{:S(2)}) collective-permute-start(bf16[768,2048]{1,0:T(8,128)(2,1)} %convolution_convert_fusion.5), channel_id=1, source_target_pairs={{0,1},{1,0},{2,3},{3,2},{4,5},{5,4},{6,7},{7,6},{8,9},{9,8},{10,11... | collective-permute-start | bytes 9437192 | tf_op jit(solution)/shard_map/ppermute | solution.py:53
  547.5 20.7 %collective-permute-start.52 = (bf16[192,2048]{1,0:T(8,128)(2,1)}, bf16[192,2048]{1,0:T(8,128)(2,1)}, u32[]{:S(2)}, u32[]{:S(2)}) collective-permute-start(bf16[192,2048]{1,0:T(8,128)(2,1)} %pad_maximum_fusion.12), channel_id=1, source_target_pairs={{0,2},{1,3},{2,0},{3,1},{4,6},{5,7},{6,4},{7,5},{8,10},{9,11},{10,... | collective-permute-start | bytes 2359304 | tf_op jit(solution)/shard_map/ppermute | solution.py:53
  548.7 20.7 %collective-permute-start.53 = (bf16[192,2048]{1,0:T(8,128)(2,1)}, bf16[192,2048]{1,0:T(8,128)(2,1)}, u32[]{:S(2)}, u32[]{:S(2)}) collective-permute-start(bf16[192,2048]{1,0:T(8,128)(2,1)} %pad_maximum_fusion.13), channel_id=1, source_target_pairs={{0,4},{1,5},{2,6},{3,7},{4,0},{5,1},{6,2},{7,3},{8,12},{9,13},{10,... | collective-permute-start | bytes 2359304 | tf_op jit(solution)/shard_map/ppermute | solution.py:53
  553.2 31.9 %collective-permute-start.44 = (bf16[192,2048]{1,0:T(8,128)(2,1)}, bf16[192,2048]{1,0:T(8,128)(2,1)}, u32[]{:S(2)}, u32[]{:S(2)}) collective-permute-start(bf16[192,2048]{1,0:T(8,128)(2,1)} %pad_maximum_fusion.10), channel_id=1, source_target_pairs={{0,2},{1,3},{2,0},{3,1},{4,6},{5,7},{6,4},{7,5},{8,10},{9,11},{10,... | collective-permute-start | bytes 2359304 | tf_op jit(solution)/shard_map/ppermute | solution.py:53
  554.2 32.1 %collective-permute-start.45 = (bf16[192,2048]{1,0:T(8,128)(2,1)}, bf16[192,2048]{1,0:T(8,128)(2,1)}, u32[]{:S(2)}, u32[]{:S(2)}) collective-permute-start(bf16[192,2048]{1,0:T(8,128)(2,1)} %pad_maximum_fusion.11), channel_id=1, source_target_pairs={{0,4},{1,5},{2,6},{3,7},{4,0},{5,1},{6,2},{7,3},{8,12},{9,13},{10,... | collective-permute-start | bytes 2359304 | tf_op jit(solution)/shard_map/ppermute | solution.py:53
  571.4 23.2 %collective-permute-start.54 = (bf16[96,2048]{1,0:T(8,128)(2,1)S(1)}, bf16[96,2048]{1,0:T(8,128)(2,1)S(1)}, u32[]{:S(2)}, u32[]{:S(2)}) collective-permute-start(bf16[96,2048]{1,0:T(8,128)(2,1)S(1)} %get-tuple-element.118), channel_id=1, source_target_pairs={{0,4},{1,5},{2,6},{3,7},{4,0},{5,1},{6,2},{7,3},{8,12},{9,13},{10,... | collective-permute-start | bytes 1179656 | tf_op jit(solution)/shard_map/ppermute | solution.py:53
  572.2 22.4 %collective-permute-start.55 = (bf16[96,2048]{1,0:T(8,128)(2,1)S(1)}, bf16[96,2048]{1,0:T(8,128)(2,1)S(1)}, u32[]{:S(2)}, u32[]{:S(2)}) collective-permute-start(bf16[96,2048]{1,0:T(8,128)(2,1)S(1)} %get-tuple-element.119), channel_id=1, source_target_pairs={{0,2},{1,3},{2,0},{3,1},{4,6},{5,7},{6,4},{7,5},{8,10},{9,11},{10,... | collective-permute-start | bytes 1179656 | tf_op jit(solution)/shard_map/ppermute | solution.py:53
  589.1 17.4 %collective-permute-start.46 = (bf16[96,2048]{1,0:T(8,128)(2,1)}, bf16[96,2048]{1,0:T(8,128)(2,1)S(1)}, u32[]{:S(2)}, u32[]{:S(2)}) collective-permute-start(bf16[96,2048]{1,0:T(8,128)(2,1)} %get-tuple-element.104), channel_id=1, source_target_pairs={{0,4},{1,5},{2,6},{3,7},{4,0},{5,1},{6,2},{7,3},{8,12},{9,13},{10,... | collective-permute-start | bytes 1179656 | tf_op jit(solution)/shard_map/ppermute | solution.py:53
  589.8 16.7 %collective-permute-start.47 = (bf16[96,2048]{1,0:T(8,128)(2,1)}, bf16[96,2048]{1,0:T(8,128)(2,1)}, u32[]{:S(2)}, u32[]{:S(2)}) collective-permute-start(bf16[96,2048]{1,0:T(8,128)(2,1)} %get-tuple-element.105), channel_id=1, source_target_pairs={{0,2},{1,3},{2,0},{3,1},{4,6},{5,7},{6,4},{7,5},{8,10},{9,11},{10,... | collective-permute-start | bytes 1179656 | tf_op jit(solution)/shard_map/ppermute | solution.py:53
  603.0 12.8 %all-to-all-start.8 = ((f32[32,1,128]{2,1,0:T(1,128)}), f32[32,1,128]{2,1,0:T(1,128)}, u32[]{:S(2)}, u32[]{:S(2)}) async-start(f32[32,1,128]{2,1,0:T(1,128)} %reshape.397), calls=%async_computation.11 | async-start | bytes 32768 | tf_op jit(solution)/shard_map/all_to_all | solution.py:504
  615.8 16.1 %all-to-all-start.7 = ((bf16[8,64,768]{2,1,0:T(8,128)(2,1)}), bf16[8,64,768]{2,1,0:T(8,128)(2,1)S(1)}, u32[]{:S(2)}, u32[]{:S(2)}) async-start(bf16[8,64,768]{2,1,0:T(8,128)(2,1)} %bitcast.121), calls=%async_computation.10 | async-start | bytes 1572864 | tf_op jit(solution)/shard_map/all_to_all | solution.py:499
  (63 other events, 688.5 us)
Sparse Core Ops, SparseCore 0:
  9.6 30.6 all-gather.11
  41.9 62.9 all-gather.5
  107.0 148.5 all-gather.7
  257.0 78.8 all-gather.9
  338.1 75.2 reduce-scatter.4
  415.5 77.2 reduce-scatter.6
  495.2 60.8 reduce-scatter.8
  558.4 93.9 reduce-scatter.10

commit v5 on v4

--- a/solution.py
+++ b/solution.py
@@ -487,13 +487,14 @@
 
     grad_w_out = grad_w_out.reshape(mine, share, piece, width).transpose(1, 0, 2, 3)
     grad_w_out = lax.all_to_all(grad_w_out, "kv", 0, 0, axis_index_groups=pairs)
-    grad_w_out = grad_w_out.reshape(ring * group * piece, width // group)
+    grad_w_out = grad_w_out.reshape(ring, -1, units)
     grad_three = lax.psum_scatter(
         dot_left(normed, dqkv).astype(BF16), "seq", scatter_dimension=0, tiled=True
     )
     grads_up = dot_left(after(second_all, *normed_parts), dup).astype(BF16)
     grads_last = with_layout_constraint(
-        jnp.concatenate([grads_up, grad_w_out], axis=1), Layout(major_to_minor=(0, 1))
+        jnp.concatenate([grads_up.reshape(ring, -1, units), grad_w_out], axis=1).reshape(-1, units),
+        Layout(major_to_minor=(0, 1)),
     )
     grads_last = lax.psum_scatter(grads_last, "seq", scatter_dimension=0, tiled=True)
     grad_three = lax.all_to_all(grad_three.reshape(group, piece, 3 * wide), "kv", 0, 0)
@@ -515,8 +516,9 @@
         grads_gate.astype(F32),
     )
     early, grads_last = lax.optimization_barrier((early, grads_last))
-    grad_w_out = grads_last[:, units:].reshape(piece, width).astype(F32)
-    grads_up = grads_last[:, :units].astype(F32)
+    rows = grads_gate.shape[0]
+    grad_w_out = grads_last[rows:].reshape(piece, width).astype(F32)
+    grads_up = grads_last[:rows].astype(F32)
     return early[:5] + (grad_w_out,) + early[5:8] + (grads_up, grads_down, summary)
 
 

time: 675 us -> 675 us (level)
  transfers between devices with their start and end apart: 72 -> 72, of which waited for: 32 -> 33; matrix products, arithmetic and copies ran while one was open for 46% -> 46% of each run, Pallas kernels for 6% -> 5%
where the time goes in v5:
time: 675 us; the launch traced here: 664 us
  waiting for transfers between devices  210 us (31%)
  matrix products  149 us (22%)
  local copies, waits for them, and re-layouts  84.1 us (12%)
  other arithmetic  82.2 us (12%)
  starting transfers between devices  65.2 us (10%)
  Pallas kernels  35.2 us (5%)
  blocking collectives  23.3 us (3%)
  between operations  15.6 us (2%)
    ppermute x56, waiting for transfers between devices, swap(): return lax.ppermute(values, 'kv', [(i, i ^ mask) for i in range(size)])  124 us
    dot_general x8, matrix products, dot_right(): lax.dot_general(left, right, (((1,), (1,)), ((), ())), preferred_element_...  55.5 us
    dot_general x8, matrix products, dot_plain(): return jnp.dot(left, right, preferred_element_type=F32)  50.9 us
    unnamed x151, local copies, waits for them, and re-layouts  46.1 us
    dot_general x5, matrix products, dot_left(): lax.dot_general(left, right, (((0,), (0,)), ((), ())), preferred_element_...  42.7 us
    all_gather x1, waiting for transfers between devices, per_device(): down_w = lax.all_gather(w_down, 'seq', axis=1, tiled=True)  33.7 us
    ppermute x56, starting transfers between devices, swap(): return lax.ppermute(values, 'kv', [(i, i ^ mask) for i in range(size)])  33.6 us
    pallas_call x1, Pallas kernels, attend_backward(): pl.pallas_call(functools.partial(backward_kernel, heads, parts, length, 1...  18.7 us
  transfers between devices with their start and end apart: 72, of which 33 were waited for; matrix products, arithmetic and copies ran while one was open for 46% of the time, Pallas kernels for 5%

profile of v5, /device:TPU:0, one launch (start us, length us, event | category | flops | bytes accessed | tf_op | source)
XLA Modules:
  0.0 664.2 jit_solution(12937319829182108769)
XLA Ops:
  13.7 17.8 %all_to_all.60 = bf16[8,64,768]{2,1,0:T(8,128)(2,1)} all-to-all(bf16[8,64,768]{2,1,0:T(8,128)(2,1)S(1)} %reshape.366), channel_id=1, replica_groups=mesh['seq'=4,'kv'=8] {'kv'}, dimensions={0} | all-to-all | bytes 1572864 | tf_op jit(solution)/shard_map/all_to_all | solution.py:378
  31.5 2.7 pad_maximum_fusion.1
  36.1 3.7 all-to-all-start.1
  40.7 2.9 fusion.37
  46.2 7.9 %all-to-all-done.1 = bf16[8,2,64]{2,1,0:T(2,128)(2,1)S(1)} async-done(((bf16[8,2,64]{2,1,0:T(2,128)(2,1)}), bf16[8,2,64]{2,1,0:T(2,128)(2,1)S(1)}, u32[]{:S(2)}, u32[]{:S(2)}) %all-to-all-start.1) | async-done | bytes 2080 | tf_op jit(solution)/shard_map/all_to_all | solution.py:127
  54.7 3.3 all-to-all-start
  59.4 3.4 all-to-all-done
  62.7 4.9 all-to-all-start.2
  79.9 6.0 collective-permute-done.2
  94.5 15.2 %collective-permute-done.9 = bf16[192,2048]{1,0:T(8,128)(2,1)} collective-permute-done((bf16[192,2048]{1,0:T(8,128)(2,1)S(1)}, bf16[192,2048]{1,0:T(8,128)(2,1)}, u32[]{:S(2)}, u32[]{:S(2)}) %collective-permute-start.9) | collective-permute-done | bytes 786464 | tf_op jit(solution)/shard_map/ppermute | solution.py:53
  113.2 4.9 fusion
  118.1 3.6 all-to-all-start.4
  123.5 6.9 %fusion.2 = bf16[1536,2048]{1,0:T(8,128)(2,1)} fusion(bf16[1536,2048]{1,0:T(8,128)(2,1)} %constant_dynamic-update-slice_fusion, f32[2048]{0:T(1024)S(1)} %mul.298, f32[1536]{0:T(1024)S(1)} %add_rsqrt_fusion), kind=kLoop, calls=%fused_computation.5 | loop fusion | flops 12582912 | bytes 12597248 | tf_op jit(solution)/shard_map/convert_element_type | solution.py:424
  130.5 6.2 convolution_convert_fusion.12.v_hbm
  136.8 7.9 %fusion.14.qk_hbm = f32[1536,512]{1,0:T(8,128)} fusion(bf16[1536,2048]{1,0:T(8,128)(2,1)} %fusion.2, bf16[2048,768]{1,0:T(8,128)(2,1)S(1)} %copy-done.43), kind=kOutput, calls=%fused_computation.41 | convolution fusion | flops 3221225472 | bytes 11534336 | tf_op jit(solution)/shard_map/dot_general | solution.py:21
  144.7 16.5 %attend_forward.1 = (bf16[1536,256]{1,0:T(8,128)(2,1)}, bf16[1536,256]{1,0:T(8,128)(2,1)}, bf16[1536,256]{1,0:T(8,128)(2,1)}, f32[1536,1]{1,0:T(8,128)}, bf16[1536,256]{1,0:T(8,128)(2,1)}) custom-call(s32[16]{0:T(128)} %pad_add_fusion.1.source, s32[6]{0:T(128)} %and_select_fusion.1.first, f32[1536,512]{1,0:T(8,128)} %fusion.14.qk_hbm, ...), custom_call_target="tpu_custom_call" | custom-call | flops 1207959552 | bytes 7077888 | tf_op jit(solution)/shard_map/attend_forward/pallas_call | solution.py:220
  161.3 3.7 convolution_convert_fusion.7
  166.6 4.5 collective-permute-done.17
  182.5 10.5 %collective-permute-done.18 = bf16[192,2048]{1,0:T(8,128)(2,1)S(1)} collective-permute-done((bf16[192,2048]{1,0:T(8,128)(2,1)S(1)}, bf16[192,2048]{1,0:T(8,128)(2,1)S(1)}, u32[]{:S(2)}, u32[]{:S(2)}) %collective-permute-start.18) | collective-permute-done | bytes 786464 | tf_op jit(solution)/shard_map/ppermute | solution.py:53
  199.8 6.2 collective-permute-done.20
  218.7 3.3 all-to-all-start.5
  223.8 5.5 all-to-all-done.5
  232.4 4.3 all-to-all-start.6
  237.7 8.0 %all-to-all-done.6 = f32[32,1,1]{2,1,0:T(1,128)} async-done(((f32[32,1,1]{2,1,0:T(1,128)}), f32[32,1,1]{2,1,0:T(1,128)}, u32[]{:S(2)}, u32[]{:S(2)}) %all-to-all-start.6) | async-done | bytes 160 | tf_op jit(solution)/shard_map/all_to_all | solution.py:439
  253.0 6.0 collective-permute-done.24
  266.8 12.2 %fusion.12 = f32[1536,1024]{1,0:T(8,128)} fusion(bf16[1536,2048]{1,0:T(8,128)(2,1)} %constant_dynamic-update-slice_fusion.10, bf16[2048,2048]{1,0:T(8,128)(2,1)} %all-gather.8.cloned.1.call-done), kind=kOutput, calls=%fused_computation.32 | convolution fusion | flops 6442450944 | bytes 16777216 | tf_op jit(solution)/shard_map/dot_general | solution.py:21
  279.0 10.2 %multiply_convert_fusion.2 = (bf16[1536,1024]{1,0:T(8,128)(2,1)S(1)}, f32[1536,1024]{1,0:T(8,128)}) fusion(f32[1536,1024]{1,0:T(8,128)} %fusion.12, bf16[1536,2048]{1,0:T(8,128)(2,1)S(1)} %copy-done.28, bf16[2048,2048]{1,0:T(8,128)(2,1)S(1)} %copy-done.41), kind=kOutput, calls=%fused_computation.10 | convolution fusion | flops 6451888128 | bytes 26214400 | tf_op jit(solution)/shard_map/dot_general | solution.py:21
  290.9 11.3 %convolution_convert_fusion.2 = bf16[2048,1024]{1,0:T(8,128)(2,1)} fusion(bf16[1536,2048]{1,0:T(8,128)(2,1)} %constant_dynamic-update-slice_fusion.20, bf16[1536,1024]{1,0:T(8,128)(2,1)S(1)} %get-tuple-element.269), kind=kOutput, calls=%fused_computation.16 | convolution fusion | flops 6444548096 | bytes 13631488 | tf_op jit(solution)/shard_map/dot_general | solution.py:25
  302.2 33.7 %all-gather.10.cloned.1.call-done = bf16[1024,2048]{1,0:T(8,128)(2,1)} async-done(((bf16[1024,512]{1,0:T(8,128)(2,1)}), bf16[1024,2048]{1,0:T(8,128)(2,1)}) %all-gather.10.cloned.1.call-update) | async-done | bytes 4194320 | tf_op jit(solution)/shard_map/all_gather | solution.py:389
  335.9 16.0 %multiply_convert_fusion = (bf16[1536,1024]{1,0:T(8,128)(2,1)S(1)}, bf16[1536,1024]{1,0:T(8,128)(2,1)S(1)}) fusion(f32[1536,1024]{1,0:T(8,128)} %fusion.12, f32[1536,1024]{1,0:T(8,128)} %get-tuple-element.270, bf16[1536,2048]{1,0:T(8,128)(2,1)} %constant_dynamic-update-slice_fusion.20, bf16[1024,2048]{1,0:T(8,128)(2,1)} %all-gather.10.cloned.1.call-done), kind=kOutput, calls=%fused_computation.8 | convolution fusion | flops 6462898176 | bytes 29360128 | tf_op jit(solution)/shard_map/dot_general | solution.py:29
  352.0 7.0 %fusion.10 = f32[768,2048]{1,0:T(8,128)S(1)} fusion(bf16[2048,2048]{1,0:T(8,128)(2,1)} %all-gather.8.cloned.1.call-done, bf16[1536,1024]{1,0:T(8,128)(2,1)S(1)} %get-tuple-element.218), kind=kOutput, calls=%fused_computation.30 | convolution fusion | flops 3221225472 | bytes 12058624 | tf_op jit(solution)/shard_map/dot_general | solution.py:29
  359.0 7.2 %add_convert_fusion.1 = bf16[768,2048]{1,0:T(8,128)(2,1)} fusion(f32[768,2048]{1,0:T(8,128)S(1)} %fusion.10, bf16[2048,2048]{1,0:T(8,128)(2,1)} %all-gather.8.cloned.1.call-done, bf16[1536,1024]{1,0:T(8,128)(2,1)S(1)} %get-tuple-element.217), kind=kOutput, calls=%fused_computation.7 | convolution fusion | flops 3224371200 | bytes 15204352 | tf_op jit(solution)/shard_map/dot_general | solution.py:29
  366.2 5.0 fusion.8
  371.2 6.5 add_convert_fusion
  377.8 10.5 %convolution_convert_fusion.1 = bf16[2048,1024]{1,0:T(8,128)(2,1)} fusion(bf16[1536,2048]{1,0:T(8,128)(2,1)S(1)} %bitcast.128, bf16[1536,1024]{1,0:T(8,128)(2,1)} %copy-done.47), kind=kOutput, calls=%fused_computation.15 | convolution fusion | flops 6444548096 | bytes 13631488 | tf_op jit(solution)/shard_map/dot_general | solution.py:25
  388.4 2.6 add_convert_fusion.29
  393.9 17.1 %collective-permute-done.33 = bf16[192,2048]{1,0:T(8,128)(2,1)S(1)} collective-permute-done((bf16[192,2048]{1,0:T(8,128)(2,1)S(1)}, bf16[192,2048]{1,0:T(8,128)(2,1)S(1)}, u32[]{:S(2)}, u32[]{:S(2)}) %collective-permute-start.33) | collective-permute-done | bytes 786464 | tf_op jit(solution)/shard_map/ppermute | solution.py:53
  415.6 8.3 %collective-permute-done.35 = bf16[96,2048]{1,0:T(8,128)(2,1)S(1)} collective-permute-done((bf16[96,2048]{1,0:T(8,128)(2,1)S(1)}, bf16[96,2048]{1,0:T(8,128)(2,1)S(1)}, u32[]{:S(2)}, u32[]{:S(2)}) %collective-permute-start.35) | collective-permute-done | bytes 393248 | tf_op jit(solution)/shard_map/ppermute | solution.py:53
  432.3 14.7 %collective-permute-done.37 = bf16[192,2048]{1,0:T(8,128)(2,1)S(1)} collective-permute-done((bf16[192,2048]{1,0:T(8,128)(2,1)}, bf16[192,2048]{1,0:T(8,128)(2,1)S(1)}, u32[]{:S(2)}, u32[]{:S(2)}) %collective-permute-start.37) | collective-permute-done | bytes 786464 | tf_op jit(solution)/shard_map/ppermute | solution.py:53
  450.1 5.8 collective-permute-done.38
  458.2 2.9 convolution_convert_fusion.11.g_hbm
  461.2 18.7 %attend_backward.1 = bf16[1536,768]{1,0:T(8,128)(2,1)} custom-call(s32[16]{0:T(128)} %pad_add_fusion.1.source, s32[6]{0:T(128)} %and_select_fusion.last, bf16[1536,256]{1,0:T(8,128)(2,1)} %get-tuple-element.108.q_ref, bf16[1536,256]{1,0:T(8,128)(2,1)} %get-tuple-element.109.k_ref, bf16[1536,256]{1,0:T(8,128)(2,1)} %get-tuple-element.110.v_ref, ...), custom_call_target="tpu_custom_call" | custom-call | flops 3019898880 | bytes 5505024 | tf_op jit(solution)/shard_map/attend_backward/pallas_call | solution.py:320
  479.8 9.2 %convolution_convert_fusion.9 = bf16[2048,768]{1,0:T(8,128)(2,1)} fusion(bf16[1536,2048]{1,0:T(8,128)(2,1)} %fusion.2, bf16[1536,768]{1,0:T(8,128)(2,1)} %attend_backward.1), kind=kOutput, calls=%fused_computation.23 | convolution fusion | flops 4833411072 | bytes 11796480 | tf_op jit(solution)/shard_map/dot_general | solution.py:25
  489.1 3.2 fusion.40
  492.9 6.7 %convolution_convert_fusion.4 = bf16[768,2048]{1,0:T(8,128)(2,1)} fusion(bf16[768,768]{1,0:T(8,128)(2,1)} %get-tuple-element.112, bf16[2048,768]{1,0:T(8,128)(2,1)} %all-gather.6.cloned.1.call-done), kind=kOutput, calls=%fused_computation.18 | convolution fusion | flops 2417491968 | bytes 7471104 | tf_op jit(solution)/shard_map/dot_general | solution.py:29
  499.6 4.1 convolution_convert_fusion.3
  505.6 5.5 all_to_all.61
  513.3 10.0 %convolution_convert_fusion = bf16[2048,1024]{1,0:T(8,128)(2,1)S(1)} fusion(bf16[1536,2048]{1,0:T(8,128)(2,1)} %constant_dynamic-update-slice_fusion.10, bf16[1536,1024]{1,0:T(8,128)(2,1)} %copy-done.48), kind=kOutput, calls=%fused_computation.14 | convolution fusion | flops 6444548096 | bytes 13631488 | tf_op jit(solution)/shard_map/dot_general | solution.py:25
  523.3 2.9 pad_maximum_fusion
  529.5 4.8 convolution_convert_fusion.5
  534.4 4.8 convolution_convert_fusion.6
  540.4 2.7 add_convert_fusion.9
  554.5 3.1 copy.78
  557.6 2.8 convert_element_type.728
  560.4 5.4 collective-permute-done.52
  571.4 11.3 %collective-permute-done.44 = bf16[192,2048]{1,0:T(8,128)(2,1)} collective-permute-done((bf16[192,2048]{1,0:T(8,128)(2,1)}, bf16[192,2048]{1,0:T(8,128)(2,1)}, u32[]{:S(2)}, u32[]{:S(2)}) %collective-permute-start.44) | collective-permute-done | bytes 786464 | tf_op jit(solution)/shard_map/ppermute | solution.py:53
  584.1 2.9 add_convert_fusion.14
  589.0 3.4 collective-permute-done.54
  600.8 4.3 all-to-all-start.8
  606.1 3.4 add_bitcast_fusion.1
  612.4 3.6 all-to-all-start.7
  621.2 7.4 %all-to-all-done.7 = bf16[8,64,768]{2,1,0:T(8,128)(2,1)S(1)} async-done(((bf16[8,64,768]{2,1,0:T(8,128)(2,1)}), bf16[8,64,768]{2,1,0:T(8,128)(2,1)S(1)}, u32[]{:S(2)}, u32[]{:S(2)}) %all-to-all-start.7) | async-done | bytes 786464 | tf_op jit(solution)/shard_map/all_to_all | solution.py:500
  636.2 16.2 %reduce-scatter.11.cloned.1.call-done = bf16[640,1024]{1,0:T(8,128)(2,1)} async-done(((bf16[2560,1024]{1,0:T(8,128)(2,1)}), bf16[640,1024]{1,0:T(8,128)(2,1)}) %reduce-scatter.11.cloned.1.call-update) | async-done | bytes 1310736 | tf_op jit(solution)/shard_map/reduce_scatter | solution.py:499
  652.4 2.8 slice_convert_fusion
  (381 shorter events, 172.6 us)
Async XLA Ops:
  7.2 110.9 %all-gather.12.cloned.1.call-start = ((), (), s32[]{:S(2)}) async-start(), calls=%async_computation.21 | async-start | bytes 1310720 | tf_op jit(solution)/shard_map/all_gather | solution.py:380
  7.9 122.6 %all-gather.6.cloned.1.call-start = ((), (), s32[]{:S(2)}) async-start(), calls=%async_computation.14 | async-start | bytes 3932160 | tf_op jit(solution)/shard_map/all_gather | solution.py:379
  31.5 235.3 %all-gather.8.cloned.1.call-start = ((), (), s32[]{:S(2)}) async-start(), calls=%async_computation.15 | async-start | bytes 10485760 | tf_op jit(solution)/shard_map/all_gather | solution.py:387
  34.3 39.4 %collective-permute-start = (bf16[192,2048]{1,0:T(8,128)(2,1)S(1)}, bf16[192,2048]{1,0:T(8,128)(2,1)}, u32[]{:S(2)}, u32[]{:S(2)}) collective-permute-start(bf16[192,2048]{1,0:T(8,128)(2,1)S(1)} %bitcast.97), channel_id=1, source_target_pairs={{0,2},{1,3},{2,0},{3,1},{4,6},{5,7},{6,4},{7,5},{8,10},{9,11},{10,... | collective-permute-start | bytes 2359304 | tf_op jit(solution)/shard_map/ppermute | solution.py:53
  34.9 41.2 %collective-permute-start.1 = (bf16[192,2048]{1,0:T(8,128)(2,1)S(1)}, bf16[192,2048]{1,0:T(8,128)(2,1)S(1)}, u32[]{:S(2)}, u32[]{:S(2)}) collective-permute-start(bf16[192,2048]{1,0:T(8,128)(2,1)S(1)} %bitcast.98), channel_id=1, source_target_pairs={{0,4},{1,5},{2,6},{3,7},{4,0},{5,1},{6,2},{7,3},{8,12},{9,13},{10,... | collective-permute-start | bytes 2359304 | tf_op jit(solution)/shard_map/ppermute | solution.py:53
  35.5 52.5 %collective-permute-start.4 = (bf16[192,2048]{1,0:T(8,128)(2,1)S(1)}, bf16[192,2048]{1,0:T(8,128)(2,1)}, u32[]{:S(2)}, u32[]{:S(2)}) collective-permute-start(bf16[192,2048]{1,0:T(8,128)(2,1)S(1)} %bitcast.99), channel_id=1, source_target_pairs={{0,1},{1,0},{2,3},{3,2},{4,5},{5,4},{6,7},{7,6},{8,9},{9,8},{10,11... | collective-permute-start | bytes 2359304 | tf_op jit(solution)/shard_map/ppermute | solution.py:53
  36.1 18.0 %all-to-all-start.1 = ((bf16[8,2,64]{2,1,0:T(2,128)(2,1)}), bf16[8,2,64]{2,1,0:T(2,128)(2,1)S(1)}, u32[]{:S(2)}, u32[]{:S(2)}) async-start(bf16[8,2,64]{2,1,0:T(2,128)(2,1)} %broadcast_in_dim.9), calls=%async_computation.1 | async-start | bytes 8192 | tf_op jit(solution)/shard_map/all_to_all | solution.py:127
  54.7 8.0 %all-to-all-start = ((s32[8,1,192]{2,1,0:T(1,128)}), s32[8,1,192]{2,1,0:T(1,128)S(1)}, u32[]{:S(2)}, u32[]{:S(2)}) async-start(s32[8,1,192]{2,1,0:T(1,128)} %broadcast_in_dim.8), calls=%async_computation | async-start | bytes 16384 | tf_op jit(solution)/shard_map/all_to_all | solution.py:127
  62.7 10.7 %all-to-all-start.2 = ((bf16[4,2,512]{2,1,0:T(2,128)(2,1)}), bf16[4,2,512]{2,1,0:T(2,128)(2,1)S(1)}, u32[]{:S(2)}, u32[]{:S(2)}) async-start(bf16[4,2,512]{2,1,0:T(2,128)(2,1)} %reshape.403), calls=%async_computation.2 | async-start | bytes 16384 | tf_op jit(solution)/shard_map/all_to_all | solution.py:127
  74.8 11.1 %collective-permute-start.2 = (bf16[96,2048]{1,0:T(8,128)(2,1)S(1)}, bf16[96,2048]{1,0:T(8,128)(2,1)S(1)}, u32[]{:S(2)}, u32[]{:S(2)}) collective-permute-start(bf16[96,2048]{1,0:T(8,128)(2,1)S(1)} %slice.472), channel_id=1, source_target_pairs={{0,4},{1,5},{2,6},{3,7},{4,0},{5,1},{6,2},{7,3},{8,12},{9,13},{10,... | collective-permute-start | bytes 1179656 | tf_op jit(solution)/shard_map/ppermute | solution.py:53
  76.2 10.5 %collective-permute-start.3 = (bf16[96,2048]{1,0:T(8,128)(2,1)S(1)}, bf16[96,2048]{1,0:T(8,128)(2,1)S(1)}, u32[]{:S(2)}, u32[]{:S(2)}) collective-permute-start(bf16[96,2048]{1,0:T(8,128)(2,1)S(1)} %slice.473), channel_id=1, source_target_pairs={{0,2},{1,3},{2,0},{3,1},{4,6},{5,7},{6,4},{7,5},{8,10},{9,11},{10,... | collective-permute-start | bytes 1179656 | tf_op jit(solution)/shard_map/ppermute | solution.py:53
  76.3 14.7 %collective-permute-start.5 = (bf16[192,2048]{1,0:T(8,128)(2,1)}, bf16[192,2048]{1,0:T(8,128)(2,1)S(1)}, u32[]{:S(2)}, u32[]{:S(2)}) collective-permute-start(bf16[192,2048]{1,0:T(8,128)(2,1)} %collective-permute-done), channel_id=1, source_target_pairs={{0,1},{1,0},{2,3},{3,2},{4,5},{5,4},{6,7},{7,6},{8,9},{9,8},{10,11... | collective-permute-start | bytes 2359304 | tf_op jit(solution)/shard_map/ppermute | solution.py:53
  76.3 15.6 %collective-permute-start.6 = (bf16[192,2048]{1,0:T(8,128)(2,1)S(1)}, bf16[192,2048]{1,0:T(8,128)(2,1)S(1)}, u32[]{:S(2)}, u32[]{:S(2)}) collective-permute-start(bf16[192,2048]{1,0:T(8,128)(2,1)S(1)} %collective-permute-done.1), channel_id=1, source_target_pairs={{0,1},{1,0},{2,3},{3,2},{4,5},{5,4},{6,7},{7,6},{8,9},{9,8},{10,11... | collective-permute-start | bytes 2359304 | tf_op jit(solution)/shard_map/ppermute | solution.py:53
  90.1 19.6 %collective-permute-start.9 = (bf16[192,2048]{1,0:T(8,128)(2,1)S(1)}, bf16[192,2048]{1,0:T(8,128)(2,1)}, u32[]{:S(2)}, u32[]{:S(2)}) collective-permute-start(bf16[192,2048]{1,0:T(8,128)(2,1)S(1)} %bitcast.114), channel_id=1, source_target_pairs={{0,2},{1,3},{2,0},{3,1},{4,6},{5,7},{6,4},{7,5},{8,10},{9,11},{10,... | collective-permute-start | bytes 2359304 | tf_op jit(solution)/shard_map/ppermute | solution.py:53
  90.1 21.7 %collective-permute-start.11 = (bf16[192,2048]{1,0:T(8,128)(2,1)S(1)}, bf16[192,2048]{1,0:T(8,128)(2,1)}, u32[]{:S(2)}, u32[]{:S(2)}) collective-permute-start(bf16[192,2048]{1,0:T(8,128)(2,1)S(1)} %bitcast.115), channel_id=1, source_target_pairs={{0,4},{1,5},{2,6},{3,7},{4,0},{5,1},{6,2},{7,3},{8,12},{9,13},{10,... | collective-permute-start | bytes 2359304 | tf_op jit(solution)/shard_map/ppermute | solution.py:53
  110.7 11.9 %collective-permute-start.13 = (bf16[96,2048]{1,0:T(8,128)(2,1)S(1)}, bf16[96,2048]{1,0:T(8,128)(2,1)}, u32[]{:S(2)}, u32[]{:S(2)}) collective-permute-start(bf16[96,2048]{1,0:T(8,128)(2,1)S(1)} %slice.475), channel_id=1, source_target_pairs={{0,4},{1,5},{2,6},{3,7},{4,0},{5,1},{6,2},{7,3},{8,12},{9,13},{10,... | collective-permute-start | bytes 1179656 | tf_op jit(solution)/shard_map/ppermute | solution.py:53
  112.9 10.5 %collective-permute-start.15 = (bf16[96,2048]{1,0:T(8,128)(2,1)S(1)}, bf16[96,2048]{1,0:T(8,128)(2,1)}, u32[]{:S(2)}, u32[]{:S(2)}) collective-permute-start(bf16[96,2048]{1,0:T(8,128)(2,1)S(1)} %slice.476), channel_id=1, source_target_pairs={{0,2},{1,3},{2,0},{3,1},{4,6},{5,7},{6,4},{7,5},{8,10},{9,11},{10,... | collective-permute-start | bytes 1179656 | tf_op jit(solution)/shard_map/ppermute | solution.py:53
  118.1 12.2 %all-to-all-start.4 = ((bf16[2,2,64,2048]{3,2,1,0:T(8,128)(2,1)}), bf16[2,2,64,2048]{3,2,1,0:T(8,128)(2,1)S(1)}, u32[]{:S(2)}, u32[]{:S(2)}) async-start(bf16[2,2,64,2048]{3,2,1,0:T(8,128)(2,1)} %bitcast.124), calls=%async_computation.4 | async-start | bytes 2097152 | tf_op jit(solution)/shard_map/all_to_all | solution.py:381
  121.7 214.2 %all-gather.10.cloned.1.call-start = ((), (), s32[]{:S(2)}) async-start(), calls=%async_computation.16 | async-start | bytes 5242880 | tf_op jit(solution)/shard_map/all_gather | solution.py:389
  122.0 8.5 %collective-permute-start.10 = (bf16[192,2048]{1,0:T(8,128)(2,1)}, bf16[192,2048]{1,0:T(8,128)(2,1)}, u32[]{:S(2)}, u32[]{:S(2)}) collective-permute-start(bf16[192,2048]{1,0:T(8,128)(2,1)} %collective-permute-done.9), channel_id=1, source_target_pairs={{0,1},{1,0},{2,3},{3,2},{4,5},{5,4},{6,7},{7,6},{8,9},{9,8},{10,11... | collective-permute-start | bytes 2359304 | tf_op jit(solution)/shard_map/ppermute | solution.py:53
  122.5 8.0 %collective-permute-start.12 = (bf16[192,2048]{1,0:T(8,128)(2,1)}, bf16[192,2048]{1,0:T(8,128)(2,1)}, u32[]{:S(2)}, u32[]{:S(2)}) collective-permute-start(bf16[192,2048]{1,0:T(8,128)(2,1)} %collective-permute-done.11), channel_id=1, source_target_pairs={{0,1},{1,0},{2,3},{3,2},{4,5},{5,4},{6,7},{7,6},{8,9},{9,8},{10,11... | collective-permute-start | bytes 2359304 | tf_op jit(solution)/shard_map/ppermute | solution.py:53
  122.6 7.9 %collective-permute-start.14 = (bf16[96,2048]{1,0:T(8,128)(2,1)}, bf16[96,2048]{1,0:T(8,128)(2,1)}, u32[]{:S(2)}, u32[]{:S(2)}) collective-permute-start(bf16[96,2048]{1,0:T(8,128)(2,1)} %collective-permute-done.13), channel_id=1, source_target_pairs={{0,1},{1,0},{2,3},{3,2},{4,5},{5,4},{6,7},{7,6},{8,9},{9,8},{10,11... | collective-permute-start | bytes 1179656 | tf_op jit(solution)/shard_map/ppermute | solution.py:53
  173.2 19.9 %collective-permute-start.18 = (bf16[192,2048]{1,0:T(8,128)(2,1)S(1)}, bf16[192,2048]{1,0:T(8,128)(2,1)S(1)}, u32[]{:S(2)}, u32[]{:S(2)}) collective-permute-start(bf16[192,2048]{1,0:T(8,128)(2,1)S(1)} %pad_maximum_fusion.6), channel_id=1, source_target_pairs={{0,2},{1,3},{2,0},{3,1},{4,6},{5,7},{6,4},{7,5},{8,10},{9,11},{10,... | collective-permute-start | bytes 2359304 | tf_op jit(solution)/shard_map/ppermute | solution.py:53
  174.6 19.5 %collective-permute-start.19 = (bf16[192,2048]{1,0:T(8,128)(2,1)S(1)}, bf16[192,2048]{1,0:T(8,128)(2,1)S(1)}, u32[]{:S(2)}, u32[]{:S(2)}) collective-permute-start(bf16[192,2048]{1,0:T(8,128)(2,1)S(1)} %pad_maximum_fusion.7), channel_id=1, source_target_pairs={{0,4},{1,5},{2,6},{3,7},{4,0},{5,1},{6,2},{7,3},{8,12},{9,13},{10,... | collective-permute-start | bytes 2359304 | tf_op jit(solution)/shard_map/ppermute | solution.py:53
  176.5 22.3 %collective-permute-start.31 = (bf16[192,2048]{1,0:T(8,128)(2,1)S(1)}, bf16[192,2048]{1,0:T(8,128)(2,1)S(1)}, u32[]{:S(2)}, u32[]{:S(2)}) collective-permute-start(bf16[192,2048]{1,0:T(8,128)(2,1)S(1)} %bitcast.117), channel_id=1, source_target_pairs={{0,1},{1,0},{2,3},{3,2},{4,5},{5,4},{6,7},{7,6},{8,9},{9,8},{10,11... | collective-permute-start | bytes 2359304 | tf_op jit(solution)/shard_map/ppermute | solution.py:53
  195.6 10.4 %collective-permute-start.20 = (bf16[96,2048]{1,0:T(8,128)(2,1)S(1)}, bf16[96,2048]{1,0:T(8,128)(2,1)S(1)}, u32[]{:S(2)}, u32[]{:S(2)}) collective-permute-start(bf16[96,2048]{1,0:T(8,128)(2,1)S(1)} %get-tuple-element.79), channel_id=1, source_target_pairs={{0,4},{1,5},{2,6},{3,7},{4,0},{5,1},{6,2},{7,3},{8,12},{9,13},{10,... | collective-permute-start | bytes 1179656 | tf_op jit(solution)/shard_map/ppermute | solution.py:53
  196.7 10.1 %collective-permute-start.21 = (bf16[96,2048]{1,0:T(8,128)(2,1)S(1)}, bf16[96,2048]{1,0:T(8,128)(2,1)S(1)}, u32[]{:S(2)}, u32[]{:S(2)}) collective-permute-start(bf16[96,2048]{1,0:T(8,128)(2,1)S(1)} %get-tuple-element.80), channel_id=1, source_target_pairs={{0,2},{1,3},{2,0},{3,1},{4,6},{5,7},{6,4},{7,5},{8,10},{9,11},{10,... | collective-permute-start | bytes 1179656 | tf_op jit(solution)/shard_map/ppermute | solution.py:53
  210.7 36.4 %collective-permute-start.22 = (bf16[192,2048]{1,0:T(8,128)(2,1)}, bf16[192,2048]{1,0:T(8,128)(2,1)}, u32[]{:S(2)}, u32[]{:S(2)}) collective-permute-start(bf16[192,2048]{1,0:T(8,128)(2,1)} %get-tuple-element.216), channel_id=1, source_target_pairs={{0,2},{1,3},{2,0},{3,1},{4,6},{5,7},{6,4},{7,5},{8,10},{9,11},{10,... | collective-permute-start | bytes 2359304 | tf_op jit(solution)/shard_map/ppermute | solution.py:53
  211.2 37.6 %collective-permute-start.23 = (bf16[192,2048]{1,0:T(8,128)(2,1)}, bf16[192,2048]{1,0:T(8,128)(2,1)S(1)}, u32[]{:S(2)}, u32[]{:S(2)}) collective-permute-start(bf16[192,2048]{1,0:T(8,128)(2,1)} %get-tuple-element.216), channel_id=1, source_target_pairs={{0,4},{1,5},{2,6},{3,7},{4,0},{5,1},{6,2},{7,3},{8,12},{9,13},{10,... | collective-permute-start | bytes 2359304 | tf_op jit(solution)/shard_map/ppermute | solution.py:53
  218.7 10.6 %all-to-all-start.5 = ((f32[8,1,192]{2,1,0:T(1,128)}), f32[8,1,192]{2,1,0:T(1,128)S(1)}, u32[]{:S(2)}, u32[]{:S(2)}) async-start(f32[8,1,192]{2,1,0:T(1,128)} %all_to_all.49), calls=%async_computation.5 | async-start | bytes 16384 | tf_op jit(solution)/shard_map/all_to_all | solution.py:436
  232.4 13.3 %all-to-all-start.6 = ((f32[32,1,1]{2,1,0:T(1,128)}), f32[32,1,1]{2,1,0:T(1,128)}, u32[]{:S(2)}, u32[]{:S(2)}) async-start(f32[32,1,1]{2,1,0:T(1,128)} %broadcast_in_dim.11), calls=%async_computation.6 | async-start | bytes 32768 | tf_op jit(solution)/shard_map/all_to_all | solution.py:439
  236.7 192.4 %reduce-scatter.5.cloned.1.call-start = ((), (), s32[]{:S(2)}) async-start(), calls=%async_computation.17 | async-start | bytes 5242880 | tf_op jit(solution)/shard_map/reduce_scatter | solution.py:446
  237.5 23.6 %collective-permute-start.26 = (bf16[192,2048]{1,0:T(8,128)(2,1)}, bf16[192,2048]{1,0:T(8,128)(2,1)}, u32[]{:S(2)}, u32[]{:S(2)}) collective-permute-start(bf16[192,2048]{1,0:T(8,128)(2,1)} %get-tuple-element.216), channel_id=1, source_target_pairs={{0,1},{1,0},{2,3},{3,2},{4,5},{5,4},{6,7},{7,6},{8,9},{9,8},{10,11... | collective-permute-start | bytes 2359304 | tf_op jit(solution)/shard_map/ppermute | solution.py:53
  248.1 11.0 %collective-permute-start.24 = (bf16[96,2048]{1,0:T(8,128)(2,1)S(1)}, bf16[96,2048]{1,0:T(8,128)(2,1)S(1)}, u32[]{:S(2)}, u32[]{:S(2)}) collective-permute-start(bf16[96,2048]{1,0:T(8,128)(2,1)S(1)} %slice.496), channel_id=1, source_target_pairs={{0,4},{1,5},{2,6},{3,7},{4,0},{5,1},{6,2},{7,3},{8,12},{9,13},{10,... | collective-permute-start | bytes 1179656 | tf_op jit(solution)/shard_map/ppermute | solution.py:53
  248.9 10.9 %collective-permute-start.25 = (bf16[96,2048]{1,0:T(8,128)(2,1)S(1)}, bf16[96,2048]{1,0:T(8,128)(2,1)S(1)}, u32[]{:S(2)}, u32[]{:S(2)}) collective-permute-start(bf16[96,2048]{1,0:T(8,128)(2,1)S(1)} %slice.497), channel_id=1, source_target_pairs={{0,2},{1,3},{2,0},{3,1},{4,6},{5,7},{6,4},{7,5},{8,10},{9,11},{10,... | collective-permute-start | bytes 1179656 | tf_op jit(solution)/shard_map/ppermute | solution.py:53
  249.5 13.8 %collective-permute-start.27 = (bf16[192,2048]{1,0:T(8,128)(2,1)}, bf16[192,2048]{1,0:T(8,128)(2,1)S(1)}, u32[]{:S(2)}, u32[]{:S(2)}) collective-permute-start(bf16[192,2048]{1,0:T(8,128)(2,1)} %collective-permute-done.22), channel_id=1, source_target_pairs={{0,1},{1,0},{2,3},{3,2},{4,5},{5,4},{6,7},{7,6},{8,9},{9,8},{10,11... | collective-permute-start | bytes 2359304 | tf_op jit(solution)/shard_map/ppermute | solution.py:53
  249.5 14.8 %collective-permute-start.28 = (bf16[192,2048]{1,0:T(8,128)(2,1)S(1)}, bf16[192,2048]{1,0:T(8,128)(2,1)S(1)}, u32[]{:S(2)}, u32[]{:S(2)}) collective-permute-start(bf16[192,2048]{1,0:T(8,128)(2,1)S(1)} %collective-permute-done.23), channel_id=1, source_target_pairs={{0,1},{1,0},{2,3},{3,2},{4,5},{5,4},{6,7},{7,6},{8,9},{9,8},{10,11... | collective-permute-start | bytes 2359304 | tf_op jit(solution)/shard_map/ppermute | solution.py:53
  302.1 190.7 %reduce-scatter.7.cloned.1.call-start = ((), (), s32[]{:S(2)}) async-start(), calls=%async_computation.18 | async-start | bytes 5242880 | tf_op jit(solution)/shard_map/reduce_scatter | solution.py:462
  366.2 22.2 %collective-permute-start.32 = (bf16[768,2048]{1,0:T(8,128)(2,1)}, bf16[768,2048]{1,0:T(8,128)(2,1)}, u32[]{:S(2)}, u32[]{:S(2)}) collective-permute-start(bf16[768,2048]{1,0:T(8,128)(2,1)} %add_convert_fusion.1), channel_id=1, source_target_pairs={{0,1},{1,0},{2,3},{3,2},{4,5},{5,4},{6,7},{7,6},{8,9},{9,8},{10,11... | collective-permute-start | bytes 9437192 | tf_op jit(solution)/shard_map/ppermute | solution.py:53
  388.3 224.1 %reduce-scatter.9.cloned.1.call-start = ((), (), s32[]{:S(2)}) async-start(), calls=%async_computation.19 | async-start | bytes 3932160 | tf_op jit(solution)/shard_map/reduce_scatter | solution.py:491
  391.1 19.9 %collective-permute-start.33 = (bf16[192,2048]{1,0:T(8,128)(2,1)S(1)}, bf16[192,2048]{1,0:T(8,128)(2,1)S(1)}, u32[]{:S(2)}, u32[]{:S(2)}) collective-permute-start(bf16[192,2048]{1,0:T(8,128)(2,1)S(1)} %pad_maximum_fusion.8), channel_id=1, source_target_pairs={{0,2},{1,3},{2,0},{3,1},{4,6},{5,7},{6,4},{7,5},{8,10},{9,11},{10,... | collective-permute-start | bytes 2359304 | tf_op jit(solution)/shard_map/ppermute | solution.py:53
  392.5 19.5 %collective-permute-start.34 = (bf16[192,2048]{1,0:T(8,128)(2,1)S(1)}, bf16[192,2048]{1,0:T(8,128)(2,1)S(1)}, u32[]{:S(2)}, u32[]{:S(2)}) collective-permute-start(bf16[192,2048]{1,0:T(8,128)(2,1)S(1)} %pad_maximum_fusion.9), channel_id=1, source_target_pairs={{0,4},{1,5},{2,6},{3,7},{4,0},{5,1},{6,2},{7,3},{8,12},{9,13},{10,... | collective-permute-start | bytes 2359304 | tf_op jit(solution)/shard_map/ppermute | solution.py:53
  413.5 10.4 %collective-permute-start.35 = (bf16[96,2048]{1,0:T(8,128)(2,1)S(1)}, bf16[96,2048]{1,0:T(8,128)(2,1)S(1)}, u32[]{:S(2)}, u32[]{:S(2)}) collective-permute-start(bf16[96,2048]{1,0:T(8,128)(2,1)S(1)} %get-tuple-element.92), channel_id=1, source_target_pairs={{0,4},{1,5},{2,6},{3,7},{4,0},{5,1},{6,2},{7,3},{8,12},{9,13},{10,... | collective-permute-start | bytes 1179656 | tf_op jit(solution)/shard_map/ppermute | solution.py:53
  415.1 10.1 %collective-permute-start.36 = (bf16[96,2048]{1,0:T(8,128)(2,1)S(1)}, bf16[96,2048]{1,0:T(8,128)(2,1)S(1)}, u32[]{:S(2)}, u32[]{:S(2)}) collective-permute-start(bf16[96,2048]{1,0:T(8,128)(2,1)S(1)} %get-tuple-element.93), channel_id=1, source_target_pairs={{0,2},{1,3},{2,0},{3,1},{4,6},{5,7},{6,4},{7,5},{8,10},{9,11},{10,... | collective-permute-start | bytes 1179656 | tf_op jit(solution)/shard_map/ppermute | solution.py:53
  429.1 17.9 %collective-permute-start.37 = (bf16[192,2048]{1,0:T(8,128)(2,1)}, bf16[192,2048]{1,0:T(8,128)(2,1)S(1)}, u32[]{:S(2)}, u32[]{:S(2)}) collective-permute-start(bf16[192,2048]{1,0:T(8,128)(2,1)} %add_convert_fusion.2), channel_id=1, source_target_pairs={{0,2},{1,3},{2,0},{3,1},{4,6},{5,7},{6,4},{7,5},{8,10},{9,11},{10,... | collective-permute-start | bytes 2359304 | tf_op jit(solution)/shard_map/ppermute | solution.py:53
  429.7 18.2 %collective-permute-start.40 = (bf16[192,2048]{1,0:T(8,128)(2,1)}, bf16[192,2048]{1,0:T(8,128)(2,1)S(1)}, u32[]{:S(2)}, u32[]{:S(2)}) collective-permute-start(bf16[192,2048]{1,0:T(8,128)(2,1)} %add_convert_fusion.2), channel_id=1, source_target_pairs={{0,4},{1,5},{2,6},{3,7},{4,0},{5,1},{6,2},{7,3},{8,12},{9,13},{10,... | collective-permute-start | bytes 2359304 | tf_op jit(solution)/shard_map/ppermute | solution.py:53
  431.0 25.5 %collective-permute-start.48 = (bf16[192,2048]{1,0:T(8,128)(2,1)}, bf16[192,2048]{1,0:T(8,128)(2,1)S(1)}, u32[]{:S(2)}, u32[]{:S(2)}) collective-permute-start(bf16[192,2048]{1,0:T(8,128)(2,1)} %add_convert_fusion.2), channel_id=1, source_target_pairs={{0,1},{1,0},{2,3},{3,2},{4,5},{5,4},{6,7},{7,6},{8,9},{9,8},{10,11... | collective-permute-start | bytes 2359304 | tf_op jit(solution)/shard_map/ppermute | solution.py:53
  447.0 8.9 %collective-permute-start.38 = (bf16[96,2048]{1,0:T(8,128)(2,1)S(1)}, bf16[96,2048]{1,0:T(8,128)(2,1)S(1)}, u32[]{:S(2)}, u32[]{:S(2)}) collective-permute-start(bf16[96,2048]{1,0:T(8,128)(2,1)S(1)} %slice.521), channel_id=1, source_target_pairs={{0,4},{1,5},{2,6},{3,7},{4,0},{5,1},{6,2},{7,3},{8,12},{9,13},{10,... | collective-permute-start | bytes 1179656 | tf_op jit(solution)/shard_map/ppermute | solution.py:53
  447.9 8.5 %collective-permute-start.41 = (bf16[96,2048]{1,0:T(8,128)(2,1)S(1)}, bf16[96,2048]{1,0:T(8,128)(2,1)S(1)}, u32[]{:S(2)}, u32[]{:S(2)}) collective-permute-start(bf16[96,2048]{1,0:T(8,128)(2,1)S(1)} %slice.522), channel_id=1, source_target_pairs={{0,2},{1,3},{2,0},{3,1},{4,6},{5,7},{6,4},{7,5},{8,10},{9,11},{10,... | collective-permute-start | bytes 1179656 | tf_op jit(solution)/shard_map/ppermute | solution.py:53
  449.5 7.1 %collective-permute-start.49 = (bf16[192,2048]{1,0:T(8,128)(2,1)S(1)}, bf16[192,2048]{1,0:T(8,128)(2,1)S(1)}, u32[]{:S(2)}, u32[]{:S(2)}) collective-permute-start(bf16[192,2048]{1,0:T(8,128)(2,1)S(1)} %collective-permute-done.37), channel_id=1, source_target_pairs={{0,1},{1,0},{2,3},{3,2},{4,5},{5,4},{6,7},{7,6},{8,9},{9,8},{10,11... | collective-permute-start | bytes 2359304 | tf_op jit(solution)/shard_map/ppermute | solution.py:53
  449.5 7.2 %collective-permute-start.50 = (bf16[192,2048]{1,0:T(8,128)(2,1)S(1)}, bf16[192,2048]{1,0:T(8,128)(2,1)S(1)}, u32[]{:S(2)}, u32[]{:S(2)}) collective-permute-start(bf16[192,2048]{1,0:T(8,128)(2,1)S(1)} %collective-permute-done.40), channel_id=1, source_target_pairs={{0,1},{1,0},{2,3},{3,2},{4,5},{5,4},{6,7},{7,6},{8,9},{9,8},{10,11... | collective-permute-start | bytes 2359304 | tf_op jit(solution)/shard_map/ppermute | solution.py:53
  489.1 163.3 %reduce-scatter.11.cloned.1.call-start = ((), (), s32[]{:S(2)}) async-start(), calls=%async_computation.20 | async-start | bytes 6553600 | tf_op jit(solution)/shard_map/reduce_scatter | solution.py:499
  526.3 14.2 %collective-permute-start.51 = (bf16[768,2048]{1,0:T(8,128)(2,1)}, bf16[768,2048]{1,0:T(8,128)(2,1)}, u32[]{:S(2)}, u32[]{:S(2)}) collective-permute-start(bf16[768,2048]{1,0:T(8,128)(2,1)} %convolution_convert_fusion.3), channel_id=1, source_target_pairs={{0,1},{1,0},{2,3},{3,2},{4,5},{5,4},{6,7},{7,6},{8,9},{9,8},{10,11... | collective-permute-start | bytes 9437192 | tf_op jit(solution)/shard_map/ppermute | solution.py:53
  534.3 13.8 %collective-permute-start.43 = (bf16[768,2048]{1,0:T(8,128)(2,1)}, bf16[768,2048]{1,0:T(8,128)(2,1)}, u32[]{:S(2)}, u32[]{:S(2)}) collective-permute-start(bf16[768,2048]{1,0:T(8,128)(2,1)} %convolution_convert_fusion.5), channel_id=1, source_target_pairs={{0,1},{1,0},{2,3},{3,2},{4,5},{5,4},{6,7},{7,6},{8,9},{9,8},{10,11... | collective-permute-start | bytes 9437192 | tf_op jit(solution)/shard_map/ppermute | solution.py:53
  545.1 20.7 %collective-permute-start.52 = (bf16[192,2048]{1,0:T(8,128)(2,1)}, bf16[192,2048]{1,0:T(8,128)(2,1)}, u32[]{:S(2)}, u32[]{:S(2)}) collective-permute-start(bf16[192,2048]{1,0:T(8,128)(2,1)} %pad_maximum_fusion.12), channel_id=1, source_target_pairs={{0,2},{1,3},{2,0},{3,1},{4,6},{5,7},{6,4},{7,5},{8,10},{9,11},{10,... | collective-permute-start | bytes 2359304 | tf_op jit(solution)/shard_map/ppermute | solution.py:53
  546.6 20.7 %collective-permute-start.53 = (bf16[192,2048]{1,0:T(8,128)(2,1)}, bf16[192,2048]{1,0:T(8,128)(2,1)}, u32[]{:S(2)}, u32[]{:S(2)}) collective-permute-start(bf16[192,2048]{1,0:T(8,128)(2,1)} %pad_maximum_fusion.13), channel_id=1, source_target_pairs={{0,4},{1,5},{2,6},{3,7},{4,0},{5,1},{6,2},{7,3},{8,12},{9,13},{10,... | collective-permute-start | bytes 2359304 | tf_op jit(solution)/shard_map/ppermute | solution.py:53
  551.9 30.8 %collective-permute-start.44 = (bf16[192,2048]{1,0:T(8,128)(2,1)}, bf16[192,2048]{1,0:T(8,128)(2,1)}, u32[]{:S(2)}, u32[]{:S(2)}) collective-permute-start(bf16[192,2048]{1,0:T(8,128)(2,1)} %pad_maximum_fusion.10), channel_id=1, source_target_pairs={{0,2},{1,3},{2,0},{3,1},{4,6},{5,7},{6,4},{7,5},{8,10},{9,11},{10,... | collective-permute-start | bytes 2359304 | tf_op jit(solution)/shard_map/ppermute | solution.py:53
  552.4 31.7 %collective-permute-start.45 = (bf16[192,2048]{1,0:T(8,128)(2,1)}, bf16[192,2048]{1,0:T(8,128)(2,1)}, u32[]{:S(2)}, u32[]{:S(2)}) collective-permute-start(bf16[192,2048]{1,0:T(8,128)(2,1)} %pad_maximum_fusion.11), channel_id=1, source_target_pairs={{0,4},{1,5},{2,6},{3,7},{4,0},{5,1},{6,2},{7,3},{8,12},{9,13},{10,... | collective-permute-start | bytes 2359304 | tf_op jit(solution)/shard_map/ppermute | solution.py:53
  569.3 23.2 %collective-permute-start.54 = (bf16[96,2048]{1,0:T(8,128)(2,1)S(1)}, bf16[96,2048]{1,0:T(8,128)(2,1)S(1)}, u32[]{:S(2)}, u32[]{:S(2)}) collective-permute-start(bf16[96,2048]{1,0:T(8,128)(2,1)S(1)} %get-tuple-element.118), channel_id=1, source_target_pairs={{0,4},{1,5},{2,6},{3,7},{4,0},{5,1},{6,2},{7,3},{8,12},{9,13},{10,... | collective-permute-start | bytes 1179656 | tf_op jit(solution)/shard_map/ppermute | solution.py:53
  570.9 21.6 %collective-permute-start.55 = (bf16[96,2048]{1,0:T(8,128)(2,1)S(1)}, bf16[96,2048]{1,0:T(8,128)(2,1)S(1)}, u32[]{:S(2)}, u32[]{:S(2)}) collective-permute-start(bf16[96,2048]{1,0:T(8,128)(2,1)S(1)} %get-tuple-element.119), channel_id=1, source_target_pairs={{0,2},{1,3},{2,0},{3,1},{4,6},{5,7},{6,4},{7,5},{8,10},{9,11},{10,... | collective-permute-start | bytes 1179656 | tf_op jit(solution)/shard_map/ppermute | solution.py:53
  587.0 18.2 %collective-permute-start.46 = (bf16[96,2048]{1,0:T(8,128)(2,1)}, bf16[96,2048]{1,0:T(8,128)(2,1)S(1)}, u32[]{:S(2)}, u32[]{:S(2)}) collective-permute-start(bf16[96,2048]{1,0:T(8,128)(2,1)} %get-tuple-element.104), channel_id=1, source_target_pairs={{0,4},{1,5},{2,6},{3,7},{4,0},{5,1},{6,2},{7,3},{8,12},{9,13},{10,... | collective-permute-start | bytes 1179656 | tf_op jit(solution)/shard_map/ppermute | solution.py:53
  588.5 16.8 %collective-permute-start.47 = (bf16[96,2048]{1,0:T(8,128)(2,1)}, bf16[96,2048]{1,0:T(8,128)(2,1)}, u32[]{:S(2)}, u32[]{:S(2)}) collective-permute-start(bf16[96,2048]{1,0:T(8,128)(2,1)} %get-tuple-element.105), channel_id=1, source_target_pairs={{0,2},{1,3},{2,0},{3,1},{4,6},{5,7},{6,4},{7,5},{8,10},{9,11},{10,... | collective-permute-start | bytes 1179656 | tf_op jit(solution)/shard_map/ppermute | solution.py:53
  600.8 11.6 %all-to-all-start.8 = ((f32[32,1,128]{2,1,0:T(1,128)}), f32[32,1,128]{2,1,0:T(1,128)}, u32[]{:S(2)}, u32[]{:S(2)}) async-start(f32[32,1,128]{2,1,0:T(1,128)} %reshape.405), calls=%async_computation.11 | async-start | bytes 32768 | tf_op jit(solution)/shard_map/all_to_all | solution.py:505
  612.4 16.1 %all-to-all-start.7 = ((bf16[8,64,768]{2,1,0:T(8,128)(2,1)}), bf16[8,64,768]{2,1,0:T(8,128)(2,1)S(1)}, u32[]{:S(2)}, u32[]{:S(2)}) async-start(bf16[8,64,768]{2,1,0:T(8,128)(2,1)} %bitcast.125), calls=%async_computation.10 | async-start | bytes 1572864 | tf_op jit(solution)/shard_map/all_to_all | solution.py:500
  (63 other events, 687.7 us)
Sparse Core Ops, SparseCore 0:
  9.6 30.6 all-gather.11
  41.9 62.9 all-gather.5
  107.0 148.5 all-gather.7
  257.0 78.8 all-gather.9
  338.1 75.2 reduce-scatter.4
  415.5 77.2 reduce-scatter.6
  495.2 60.8 reduce-scatter.8
  558.4 93.9 reduce-scatter.10
